TPU v7x, 256 devices: a whole 4x4x8 slice. The times are simulated.
256 devices in a mesh: tm: 64 (over y, z, core), region: 4 (over x).
Axes of the slice: x: 4, y: 4, z: 8, core: 2. Of those that a mesh axis runs over, the one named last changes fastest.
Arguments:
- covariates: bfloat16 [8, 8192, 256], P('region', 'tm'), may hold values from -4 to 4
- observed: float32 [8, 8192, 256], P('region', 'tm'), may hold values from -40 to 40
- input_weight: bfloat16 [256, 256], replicated, may hold values from -0.375 to 0.375
- filter_weight: bfloat16 [3, 512, 512], replicated, may hold values from -0.25 to 0.25
- mixing_weight: bfloat16 [3, 256, 256], replicated, may hold values from -0.375 to 0.375
- output_weight: bfloat16 [256, 4096], replicated, may hold values from -0.375 to 0.375
Outputs:
- covariate_grad: bfloat16 [8, 8192, 256], P('region', 'tm')
- input_grad: bfloat16 [256, 256], P('tm')
- filter_grad: bfloat16 [3, 512, 512], P(None, 'tm')
- mixing_grad: bfloat16 [3, 256, 256], P(None, 'tm')
- output_grad: bfloat16 [256, 4096], P('tm')
All inputs are finite; a program needn't handle non-finite values.
Results may differ from a plain program's by a relative error of at most 0.022.
Values may be sent and summed in bfloat16 or wider, within the bound.
No kernel may reach another device: no remote copies, remote signals or barrier semaphores. Data moves between devices by JAX's collectives and lax.ppermute only.
A program may use at most 64 MiB of HBM per device.

v0:
```python
import jax
import jax.numpy as jnp
from jax import lax
from jax.sharding import PartitionSpec as P

epsilon = 1e-05


def passed_along(block, axis, distance):
    devices = range(lax.axis_size(axis))
    route = [(i - distance, i) for i in devices if i - distance in devices]
    return lax.ppermute(block, axis, route)


def energy(predicted, observed, scenarios):
    node_count = observed.shape[-1]
    scenario_vals = predicted.reshape(predicted.shape[:-1] + (scenarios, node_count))
    gram_matrix = jnp.einsum(
        "...sn,...rn->...sr", scenario_vals, scenario_vals, precision=lax.Precision.HIGHEST
    )
    against = jnp.einsum(
        "...sn,...n->...s", scenario_vals, observed, precision=lax.Precision.HIGHEST
    )
    own_sq = jnp.diagonal(gram_matrix, axis1=-2, axis2=-1)
    target = jnp.sum(observed * observed, axis=-1)
    to_target = jnp.sqrt((own_sq - 2.0 * against + target[..., None]) / node_count + epsilon)
    off_diag = 1.0 - jnp.eye(scenarios, dtype=jnp.float32)
    pair_sq = (own_sq[..., :, None] + own_sq[..., None, :] - 2.0 * gram_matrix) / node_count
    between = jnp.sqrt(pair_sq * off_diag + epsilon) * off_diag
    return jnp.mean(to_target, axis=-1) - jnp.sum(between, axis=(-2, -1)) / (
        2.0 * scenarios * (scenarios - 1)
    )


def layer_forward(hidden, delayed, w_filter, w_mixing):
    channels = hidden.shape[-1]
    joined = jnp.concatenate([delayed, hidden], axis=-1)
    preact = jnp.dot(joined, w_filter, preferred_element_type=jnp.float32)
    gated = (jnp.tanh(preact[..., :channels]) * jax.nn.sigmoid(preact[..., channels:])).astype(
        jnp.bfloat16
    )
    result = (
        hidden.astype(jnp.float32) + jnp.dot(gated, w_mixing, preferred_element_type=jnp.float32)
    ).astype(jnp.bfloat16)
    return (result, (joined, preact, gated))


def layer_backward(grad_out, stored_layer, w_filter, w_mixing):
    joined, preact, gated = stored_layer
    channels = gated.shape[-1]
    upstream = grad_out.astype(jnp.float32)
    grad_mixing = jnp.einsum("btc,btd->cd", gated, upstream, preferred_element_type=jnp.float32)
    gated_cot = jnp.dot(upstream, w_mixing.T, preferred_element_type=jnp.float32).astype(
        jnp.bfloat16
    )
    grad_gated = lax.optimization_barrier(gated_cot).astype(jnp.float32)
    filter_act = jnp.tanh(preact[..., :channels])
    gate_act = jax.nn.sigmoid(preact[..., channels:])
    grad_preact = jnp.concatenate(
        [
            grad_gated * gate_act * (1.0 - filter_act * filter_act),
            grad_gated * filter_act * gate_act * (1.0 - gate_act),
        ],
        axis=-1,
    )
    grad_filter = jnp.einsum("btk,btj->kj", joined, grad_preact, preferred_element_type=jnp.float32)
    grad_joined = jnp.dot(grad_preact, w_filter.T, preferred_element_type=jnp.float32).astype(
        jnp.bfloat16
    )
    return (
        grad_joined[..., :channels],
        grad_joined[..., channels:],
        grad_out,
        grad_filter,
        grad_mixing,
    )


def per_device(covariates, observed, input_weight, filter_weight, mixing_weight, output_weight):
    batch_seqs, row_count, node_count = covariates.shape
    layer_total = filter_weight.shape[0]
    channels = mixing_weight.shape[1]
    scenarios = output_weight.shape[1] // node_count
    length = row_count * lax.axis_size("tm")
    local_sq = jnp.sum(observed * observed, axis=(1, 2))
    total_sq = lax.psum(local_sq, "tm")
    inv_scale = 1.0 / jnp.sqrt(total_sq / (length * node_count) + epsilon)
    hidden = jnp.dot(covariates, input_weight, preferred_element_type=jnp.float32).astype(
        jnp.bfloat16
    )
    stored = []
    for layer_no in range(layer_total):
        dilation = 2**layer_no
        incoming = passed_along(hidden[:, row_count - dilation :, :], "tm", 1)
        delayed = jnp.concatenate([incoming, hidden[:, : row_count - dilation, :]], axis=1)
        hidden, stored_layer = layer_forward(
            hidden, delayed, filter_weight[layer_no], mixing_weight[layer_no]
        )
        stored.append(stored_layer)
    predicted = jnp.dot(hidden, output_weight, preferred_element_type=jnp.float32)

    def scoring(values):
        return jnp.sum(energy(values, observed, scenarios) * inv_scale[:, None])

    _, pull_back = jax.vjp(scoring, predicted)
    (grad_pred,) = pull_back(jnp.ones((), jnp.float32))
    grad_output = jnp.einsum("btc,btj->cj", hidden, grad_pred, preferred_element_type=jnp.float32)
    grad_last = jnp.dot(grad_pred, output_weight.T, preferred_element_type=jnp.float32).astype(
        jnp.bfloat16
    )
    grad_hidden = grad_last
    filter_parts = [None] * layer_total
    mixing_parts = [None] * layer_total
    for layer_no in reversed(range(layer_total)):
        dilation = 2**layer_no
        grad_past, grad_now, grad_resid, grad_filter, grad_mixing = layer_backward(
            grad_hidden, stored[layer_no], filter_weight[layer_no], mixing_weight[layer_no]
        )
        extent = grad_past.shape[1]
        inside = jnp.concatenate(
            [grad_past[:, dilation:, :], jnp.zeros((batch_seqs, dilation, channels), jnp.bfloat16)],
            axis=1,
        )
        grad_hidden = grad_resid + grad_now + inside
        returned = passed_along(grad_past[:, :dilation, :], "tm", -1)
        grad_hidden = grad_hidden + jnp.concatenate(
            [jnp.zeros((batch_seqs, extent - dilation, channels), jnp.bfloat16), returned], axis=1
        )
        filter_parts[layer_no] = grad_filter
        mixing_parts[layer_no] = grad_mixing
    grad_input = jnp.einsum(
        "btn,btc->nc", covariates, grad_hidden, preferred_element_type=jnp.float32
    )
    covariate_grad = jnp.dot(
        grad_hidden, input_weight.T, preferred_element_type=jnp.float32
    ).astype(jnp.bfloat16)
    grad_filters = jnp.stack(filter_parts)
    grad_mixings = jnp.stack(mixing_parts)
    shares = (
        lax.psum_scatter(grad_input, "tm", scatter_dimension=0, tiled=True),
        lax.psum_scatter(grad_filters, "tm", scatter_dimension=1, tiled=True),
        lax.psum_scatter(grad_mixings, "tm", scatter_dimension=1, tiled=True),
        lax.psum_scatter(grad_output, "tm", scatter_dimension=0, tiled=True),
    )
    shares = (
        lax.psum(shares[0].astype(jnp.bfloat16), "region").astype(jnp.float32),
        lax.psum(shares[1].astype(jnp.bfloat16), "region").astype(jnp.float32),
        lax.psum(shares[2].astype(jnp.bfloat16), "region").astype(jnp.float32),
        lax.psum(shares[3].astype(jnp.bfloat16), "region").astype(jnp.float32),
    )
    shares = tuple((piece.astype(jnp.bfloat16) for piece in shares))
    return (covariate_grad, shares[0], shares[1], shares[2], shares[3])


def solution(mesh):
    placed = (P("region", "tm", None), P("region", "tm", None), P(), P(), P(), P())
    return jax.shard_map(
        per_device,
        mesh=mesh,
        in_specs=placed,
        out_specs=(
            P("region", "tm", None),
            P("tm", None),
            P(None, "tm", None),
            P(None, "tm", None),
            P("tm", None),
        ),
        check_vma=False,
    )
```

profile of v0, /device:TPU:8, one launch (start us, length us, event | category | flops | bytes accessed | tf_op | source)
XLA Modules:
  0.0 587.4 jit_solution(2315299154174542685)
XLA Ops:
  8.5 1.9 collective-permute-start
  10.5 1.7 multiply_reduce_fusion.1
  12.2 109.8 %psum.35 = f32[2]{0:T(128)S(1)} all-reduce(f32[2]{0:T(128)S(1)} %get-tuple-element.28), channel_id=1, replica_groups=mesh['tm'=64,'region'=4] {'tm'}, use_global_device_ids=true, to_apply=%region_2.3 | all-reduce | flops 2 | bytes 16 | tf_op jit(solution)/shard_map/psum | solution.py:86
  125.9 1.9 collective-permute-start.1
  128.4 4.6 collective-permute-done.1
  134.2 1.9 collective-permute-start.2
  136.6 4.6 collective-permute-done.2
  143.9 1.7 copy.97
  145.7 1.9 copy-done.1
  147.6 6.3 %fusion.6 = f32[2,128,16,16]{3,2,1,0:T(8,128)} fusion(f32[2,128,16,256]{3,2,1,0:T(8,128)S(1)} %bitcast.162), kind=kOutput, calls=%fused_computation.9 | convolution fusion | flops 201326592 | bytes 4456448 | tf_op jit(solution)/shard_map/jvp(...sn,...rn->...sr)/dot_general | solution.py:18
  153.9 3.2 copy.60
  157.2 2.3 copy.63
  159.5 1.7 gather_fusion
  161.8 6.5 %fusion.4 = f32[2,128,1,16]{3,2,1,0:T(1,128)} fusion(f32[2,128,256,1]{2,1,0,3:T(8,128)S(1)} %bitcast.167, f32[2,128,16,256]{3,2,1,0:T(8,128)} %bitcast.163), kind=kOutput, calls=%fused_computation.7 | convolution fusion | flops 12582912 | bytes 4472832 | tf_op jit(solution)/shard_map/jvp(...sn,...n->...s)/dot_general | solution.py:21
  168.2 1.6 copy.82
  170.8 1.4 negate_multiply_fusion.1
  172.4 1.6 scatter_fusion
  174.1 2.1 copy.71
  176.3 6.9 %fusion = f32[2,128,16,256]{3,2,1,0:T(8,128)S(1)} fusion(f32[2,128,16,16]{3,2,1,0:T(8,128)} %copy.71, f32[2,128,16,256]{3,2,1,0:T(8,128)} %bitcast.164), kind=kOutput, calls=%fused_computation.3 | convolution fusion | flops 201326592 | bytes 8650752 | tf_op jit(solution)/shard_map/transpose(jvp(...sn,...rn->...sr))/dot_general | solution.py:18
  183.2 5.7 add_add_fusion
  188.9 4.2 reshape.36
  193.1 2.5 fusion.17
  196.4 1.9 collective-permute-start.3
  200.5 5.7 collective-permute-start.4
  208.6 2.0 pad_maximum_fusion
  212.5 4.3 convolution_bitcast_fusion
  218.8 5.7 collective-permute-start.5
  226.1 264.1 %all-reduce.15 = (bf16[256,256]{0,1:T(8,128)(2,1)S(1)}, bf16[3,256,256]{2,1,0:T(8,128)(2,1)}, bf16[256,4096]{1,0:T(8,128)(2,1)}) all-reduce(f32[256,256]{0,1:T(8,128)S(1)} %convolution_bitcast_fusion.7, f32[3,256,256]{2,1,0:T(8,128)S(1)} %pad_maximum_fusion.1, ...), channel_id=2, replica_groups=mesh['tm'=64,'region'=4] {'tm'}, use_global_device_ids=true, to_apply=%region_6.7.clone | all-reduce | flops 1310720 | bytes 7864320
  492.3 1.5 dynamic-slice_convert_fusion.1
  493.7 1.4 convert_element_type.120
  496.1 79.0 %all-reduce.14.cloned.1.call-done = (bf16[4,256]{0,1:T(8,128)(2,1)}, bf16[3,8,512]{2,1,0:T(8,128)(2,1)}, bf16[3,4,256]{2,1,0:T(4,128)(2,1)}, bf16[4,4096]{1,0:T(4,128)(2,1)}) async-done(((bf16[4,256]{0,1:T(8,128)(2,1)}, bf16[3,8,512]{2,1,0:T(8,128)(2,1)}, bf16[3,4,256]{2,1,0:T(4,128)(2,1)}, bf16[4,4096]{1,0:T(4,128)(2,1)}), (bf16[4,256]{0,1:T(8,128)(2,1)}, bf16[3,8,512]{2,1,0:T(8,128)(2,1)}, ...) | async-done | bytes 65552 | tf_op jit(solution)/shard_map/psum | solution.py:146
  575.0 1.5 copy.80
  (130 shorter events, 28.7 us)
Async XLA Ops:
  7.2 136.0 %copy-start = (bf16[256,4096]{1,0:T(8,128)(2,1)S(1)}, bf16[256,4096]{1,0:T(8,128)(2,1)}, u32[]{:S(2)}) copy-start(bf16[256,4096]{1,0:T(8,128)(2,1)} %param.11) | copy-start | bytes 6291460
  7.2 486.6 %reduce-scatter.4.cloned.1.call-start = ((), (), s32[]{:S(2)}) async-start(), calls=%async_computation.1 | async-start | bytes 3194880 | tf_op jit(solution)/shard_map/reduce_scatter | solution.py:141
  8.5 114.7 %collective-permute-start = (bf16[2,1,256]{2,1,0:T(2,128)(2,1)S(1)}, bf16[2,1,256]{2,1,0:T(2,128)(2,1)S(1)}, u32[]{:S(2)}, u32[]{:S(2)}) collective-permute-start(bf16[2,1,256]{2,1,0:T(2,128)(2,1)S(1)} %slice.133), channel_id=1, source_target_pairs={{0,4},{4,8},{8,12},{12,16},{16,20},{20,24},{24,28},{28,32},{32,36}... | collective-permute-start | bytes 3080 | tf_op jit(solution)/shard_map/ppermute | solution.py:12
  122.0 11.5 %copy-start.30 = (bf16[3,512,512]{2,1,0:T(8,128)(2,1)S(1)}, bf16[3,512,512]{2,1,0:T(8,128)(2,1)}, u32[]{:S(2)}) copy-start(bf16[3,512,512]{2,1,0:T(8,128)(2,1)} %param.9) | copy-start | bytes 4718596
  123.2 10.7 %copy-start.9 = (bf16[3,256,256]{2,1,0:T(8,128)(2,1)S(1)}, bf16[3,256,256]{2,1,0:T(8,128)(2,1)}, u32[]{:S(2)}) copy-start(bf16[3,256,256]{2,1,0:T(8,128)(2,1)} %param.10) | copy-start | bytes 1179652
  124.7 8.2 %copy-start.13 = (bf16[2,128,256]{2,1,0:T(8,128)(2,1)}, bf16[2,128,256]{2,1,0:T(8,128)(2,1)S(1)}, u32[]{:S(2)}) copy-start(bf16[2,128,256]{2,1,0:T(8,128)(2,1)S(1)} %multiply_convert_fusion.2) | copy-start | bytes 393220
  125.9 7.0 %collective-permute-start.1 = (bf16[2,2,256]{2,1,0:T(2,128)(2,1)S(1)}, bf16[2,2,256]{2,1,0:T(2,128)(2,1)S(1)}, u32[]{:S(2)}, u32[]{:S(2)}) collective-permute-start(bf16[2,2,256]{2,1,0:T(2,128)(2,1)S(1)} %slice.137), channel_id=1, source_target_pairs={{0,4},{4,8},{8,12},{12,16},{16,20},{20,24},{24,28},{28,32},{32,36}... | collective-permute-start | bytes 6152 | tf_op jit(solution)/shard_map/ppermute | solution.py:12
  133.8 7.8 %copy-start.5 = (f32[2,128,512]{2,1,0:T(8,128)}, f32[2,128,512]{2,1,0:T(8,128)S(1)}, u32[]{:S(2)}) copy-start(f32[2,128,512]{2,1,0:T(8,128)S(1)} %fusion.24) | copy-start | bytes 1572868
  134.0 7.3 %copy-start.15 = (bf16[2,128,256]{2,1,0:T(8,128)(2,1)}, bf16[2,128,256]{2,1,0:T(8,128)(2,1)S(1)}, u32[]{:S(2)}) copy-start(bf16[2,128,256]{2,1,0:T(8,128)(2,1)S(1)} %multiply_convert_fusion.1) | copy-start | bytes 393220
  134.2 7.0 %collective-permute-start.2 = (bf16[2,4,256]{2,1,0:T(4,128)(2,1)S(1)}, bf16[2,4,256]{2,1,0:T(4,128)(2,1)S(1)}, u32[]{:S(2)}, u32[]{:S(2)}) collective-permute-start(bf16[2,4,256]{2,1,0:T(4,128)(2,1)S(1)} %slice.141), channel_id=1, source_target_pairs={{0,4},{4,8},{8,12},{12,16},{16,20},{20,24},{24,28},{28,32},{32,36}... | collective-permute-start | bytes 12296 | tf_op jit(solution)/shard_map/ppermute | solution.py:12
  145.7 2.0 copy-start.1
  153.9 7.8 %copy-start.4 = (f32[2,128,256]{2,1,0:T(8,128)S(1)}, f32[2,128,256]{2,1,0:T(8,128)}, u32[]{:S(2)}) copy-start(f32[2,128,256]{2,1,0:T(8,128)} %param.7) | copy-start | bytes 786436
  174.1 2.1 copy-start.23
  176.3 6.9 %copy-start.2 = (f32[32,8,16,256]{3,2,1,0:T(8,128)S(1)}, f32[32,8,16,256]{3,2,1,0:T(8,128)}, u32[]{:S(2)}) copy-start(f32[32,8,16,256]{3,2,1,0:T(8,128)} %copy-done.1) | copy-start | bytes 12582916
  176.3 6.9 %copy-start.3 = (f32[2,128,16,16]{3,2,1,0:T(8,128)S(1)}, f32[2,128,16,16]{3,2,1,0:T(8,128)}, u32[]{:S(2)}) copy-start(f32[2,128,16,16]{3,2,1,0:T(8,128)} %copy.71) | copy-start | bytes 786436
  193.1 2.5 copy-start.10
  193.1 2.7 copy-start.8
  193.1 2.9 copy-start.31
  195.6 2.7 copy-start.25
  196.0 3.9 copy-start.6
  196.4 3.2 collective-permute-start.3
  198.7 7.5 %copy-start.29 = (bf16[2,2,256]{2,1,0:T(2,128)(2,1)S(1)}, bf16[2,2,256]{2,1,0:T(2,128)(2,1)}, u32[]{:S(2)}) copy-start(bf16[2,2,256]{2,1,0:T(2,128)(2,1)} %copy-done.28) | copy-start | bytes 6148
  200.4 7.5 %copy-start.27 = (bf16[2,1,256]{2,1,0:T(2,128)(2,1)S(1)}, bf16[2,1,256]{2,1,0:T(2,128)(2,1)}, u32[]{:S(2)}) copy-start(bf16[2,1,256]{2,1,0:T(2,128)(2,1)} %copy-done.26) | copy-start | bytes 3076
  200.5 7.0 %collective-permute-start.4 = (bf16[2,2,256]{2,1,0:T(2,128)(2,1)S(1)}, bf16[2,2,256]{2,1,0:T(2,128)(2,1)S(1)}, u32[]{:S(2)}, u32[]{:S(2)}) collective-permute-start(bf16[2,2,256]{2,1,0:T(2,128)(2,1)S(1)} %slice.150), channel_id=1, source_target_pairs={{4,0},{8,4},{12,8},{16,12},{20,16},{24,20},{28,24},{32,28},{36,32}... | collective-permute-start | bytes 6152 | tf_op jit(solution)/shard_map/ppermute | solution.py:12
  210.6 364.5 %all-reduce.14.cloned.1.call-start = ((), (), s32[]{:S(2)}) async-start(), calls=%async_computation.2 | async-start | bytes 258048 | tf_op jit(solution)/shard_map/psum | solution.py:146
  212.5 4.4 copy-start.18
  212.5 4.6 copy-start.16
  212.5 4.8 copy-start.21
  216.9 7.6 %copy-start.14 = (bf16[2,128,256]{2,1,0:T(8,128)(2,1)S(1)}, bf16[2,128,256]{2,1,0:T(8,128)(2,1)}, u32[]{:S(2)}) copy-start(bf16[2,128,256]{2,1,0:T(8,128)(2,1)} %copy-done.13) | copy-start | bytes 393220
  217.3 8.5 %copy-start.22 = (bf16[2,128,256]{2,1,0:T(8,128)(2,1)S(1)}, bf16[2,128,256]{2,1,0:T(8,128)(2,1)}, u32[]{:S(2)}) copy-start(bf16[2,128,256]{2,1,0:T(8,128)(2,1)} %param.6) | copy-start | bytes 393220
  218.8 7.0 %collective-permute-start.5 = (bf16[2,1,256]{2,1,0:T(2,128)(2,1)S(1)}, bf16[2,1,256]{2,1,0:T(2,128)(2,1)S(1)}, u32[]{:S(2)}, u32[]{:S(2)}) collective-permute-start(bf16[2,1,256]{2,1,0:T(2,128)(2,1)S(1)} %slice.153), channel_id=1, source_target_pairs={{4,0},{8,4},{12,8},{16,12},{20,16},{24,20},{28,24},{32,28},{36,32}... | collective-permute-start | bytes 3080 | tf_op jit(solution)/shard_map/ppermute | solution.py:12
  226.1 269.1 %copy-start.19 = (bf16[256,256]{1,0:T(8,128)(2,1)S(1)}, bf16[256,256]{1,0:T(8,128)(2,1)}, u32[]{:S(2)}) copy-start(bf16[256,256]{1,0:T(8,128)(2,1)} %param.8) | copy-start | bytes 393220
  (9 other events, 8.0 us)
Sparse Core Ops, SparseCore 0:
  210.7 148.8 reduce-scatter.3
  495.3 79.7 all-reduce.13
where the time goes:
time: 589 us; the launch traced here: 587 us
  blocking collectives  374 us (63%)
  waiting for transfers between devices  91 us (15%)
  matrix products  43.1 us (7%)
  local copies, waits for them, and re-layouts  32.3 us (5%)
  starting transfers between devices  19.2 us (3%)
  between operations  15.4 us (3%)
  other arithmetic  12.4 us (2%)
    unnamed x1, blocking collectives  264 us
    psum x1, blocking collectives, per_device(): total_sq = lax.psum(local_sq, 'tm')  110 us
    psum x1, waiting for transfers between devices, per_device(): lax.psum(shares[0].astype(jnp.bfloat16), 'region').astype(jnp.float32)  79 us
    ppermute x6, starting transfers between devices, passed_along(): return lax.ppermute(block, axis, route)  19.1 us
    dot_general x3, matrix products, energy(): jnp.einsum('...sn,...rn->...sr', scenario_vals, scenario_vals, precision=...  18.9 us
    unnamed x72, local copies, waits for them, and re-layouts  12.7 us
    ppermute x6, waiting for transfers between devices, passed_along(): return lax.ppermute(block, axis, route)  11.9 us
  transfers between devices with their start and end apart: 8, of which 6 were waited for; matrix products, arithmetic and copies ran while one was open for 3% of the time, Pallas kernels for 0%

commit v1 on v0

v1 whole, which is shorter than its diff:
```python
import functools

import jax
import jax.numpy as jnp
from jax import lax
from jax.experimental import pallas as pl
from jax.experimental.pallas import tpu as pltpu
from jax.sharding import Mesh
from jax.sharding import PartitionSpec as P

epsilon = 1e-05

NODES = 256
SCENARIOS = 16
LAYERS = 3
HALO = 8
ROWS = 128
BLOCK = ROWS + 2 * HALO
SEQ = 2
ALL_ROWS = SEQ * BLOCK
HEAD = ROWS + HALO
ALL_HEAD = SEQ * HEAD
TM = ("y", "z", "core")
F32 = jnp.float32
BF16 = jnp.bfloat16
VMEM = pltpu.VMEM
PARAMS = pltpu.CompilerParams(vmem_limit_bytes=48 * 1024 * 1024)


def mm(a, b):
    return jnp.dot(a, b, preferred_element_type=F32)


def mm_nt(a, b):
    return lax.dot_general(a, b, (((1,), (1,)), ((), ())), preferred_element_type=F32)


def vmem_specs(count):
    return [pl.BlockSpec(memory_space=VMEM)] * count


def shape(dims, dtype):
    return jax.ShapeDtypeStruct(dims, dtype)


def start_kernel(cov, obs, to_next, to_prev, squares):
    for b in range(SEQ):
        to_next[b] = cov[b, ROWS - HALO :, :]
        to_prev[b, :, :NODES] = cov[b, :HALO, :].astype(F32)
        to_prev[b, :, NODES:] = obs[b, :HALO, :]
        sq = obs[b] * obs[b]
        by_lane = jnp.sum(sq, axis=0, keepdims=True)
        total = jnp.sum(by_lane, axis=1, keepdims=True)
        squares[:, b, :] = jnp.broadcast_to(total, (squares.shape[0], 128))


def own_rows(x):
    return jnp.concatenate([x[HALO : HALO + ROWS], x[BLOCK + HALO : BLOCK + HALO + ROWS]], axis=0)


def permutation(core, group):
    i = lax.broadcasted_iota(jnp.int32, (NODES, NODES), 0)
    c = lax.broadcasted_iota(jnp.int32, (NODES, NODES), 1)
    half = i // 128
    inner = i % 128
    side = jnp.where(half == 0, 1 - core, core)
    wanted = (inner // group) * (2 * group) + side * group + inner % group
    return jnp.where(c == wanted, 1.0, 0.0).astype(BF16)


def energy_rows(y, o):
    inv_nodes = 1.0 / NODES

    def distance(a, b):
        d0 = a[0] - b[0]
        d1 = a[1] - b[1]
        return jnp.sum(d0 * d0 + d1 * d1, axis=1, keepdims=True)

    alpha = [
        lax.rsqrt(distance(y[s], o) * inv_nodes + epsilon) * (1.0 / (SCENARIOS * NODES))
        for s in range(SCENARIOS)
    ]
    factor = 1.0 / (SCENARIOS * (SCENARIOS - 1) * NODES)
    beta = {}
    for s in range(SCENARIOS):
        for r in range(s + 1, SCENARIOS):
            beta[s, r] = lax.rsqrt(distance(y[s], y[r]) * inv_nodes + epsilon) * factor
    result = []
    for s in range(SCENARIOS):
        gamma = alpha[s]
        acc = [-(alpha[s] * o[0]), -(alpha[s] * o[1])]
        for r in range(SCENARIOS):
            if r == s:
                continue
            weight = beta[min(s, r), max(s, r)]
            gamma = gamma - weight
            acc = [acc[0] + weight * y[r][0], acc[1] + weight * y[r][1]]
        result.append(jnp.concatenate([acc[0] + gamma * y[s][0], acc[1] + gamma * y[s][1]], axis=1))
    return result


def forward_kernel(
    place, from_prev, cov, from_next, obs, w_in, w_f, w_m, w_out,
    tanh_out, gate_out, dpred, cov_t, gated_t, last_t, taps_t,
    pred, target,
):
    core = place[0]
    perm4 = permutation(core, 4)
    perm8 = permutation(core, 8)

    def turned(perm, x):
        return mm_nt(perm, own_rows(x).astype(BF16)).astype(BF16)

    pieces = []
    for b in range(SEQ):
        pieces += [
            from_prev[b].astype(F32),
            cov[b].astype(F32),
            from_next[b, :, :NODES],
        ]
    x = jnp.concatenate(pieces, axis=0)
    cov_t[...] = turned(perm4, x)
    hidden = mm(x.astype(BF16), w_in[...]).astype(BF16)
    for layer in range(LAYERS):
        wide = hidden.astype(F32)
        delayed_wide = pltpu.roll(wide, 2**layer, 0)
        delayed = delayed_wide.astype(BF16)
        taps_t[layer, 0] = turned(perm8, delayed_wide)
        taps_t[layer, 1] = turned(perm8, wide)
        preact = mm(delayed, w_f[layer, :NODES, :]) + mm(hidden, w_f[layer, NODES:, :])
        filter_act = jnp.tanh(preact[:, :NODES])
        gate_act = jax.nn.sigmoid(preact[:, NODES:])
        tanh_out[layer] = filter_act
        gate_out[layer] = gate_act
        gated = (filter_act * gate_act).astype(BF16)
        gated_t[layer] = turned(perm4, gated.astype(F32))
        hidden = (wide + mm(gated, w_m[layer])).astype(BF16)
    wide = hidden.astype(F32)
    last_t[...] = turned(perm4, wide)
    head = jnp.concatenate([wide[HALO:BLOCK], wide[BLOCK + HALO :]], axis=0).astype(BF16)
    pred[...] = mm(head, w_out[...])
    for b in range(SEQ):
        target[b * HEAD : b * HEAD + ROWS, :] = obs[b]
        target[b * HEAD + ROWS : (b + 1) * HEAD, :] = from_next[b, :, NODES:]

    def step(i, carry):
        halves = []
        for part in range(2):
            at = pl.ds(pl.multiple_of(i * 16 + part * 8, 8), 8)
            y = [
                (pred[at, s * NODES : s * NODES + 128], pred[at, s * NODES + 128 : (s + 1) * NODES])
                for s in range(SCENARIOS)
            ]
            o = (target[at, :128], target[at, 128:])
            halves.append(energy_rows(y, o))
        at = pl.ds(pl.multiple_of(i * 16, 16), 16)
        for s in range(SCENARIOS):
            both = jnp.concatenate([halves[0][s], halves[1][s]], axis=0)
            dpred[at, s * NODES : (s + 1) * NODES] = both.astype(BF16)
        return carry

    lax.fori_loop(0, ALL_HEAD // 16, step, 0)


def backward_kernel(
    place, sums, tanh_in, gate_in, dpred, cov_t, gated_t, last_t, taps_t, w_in, w_f, w_m, w_out,
    cov_grad, send, keep,
):
    at_end = place[1]
    steps = ROWS * place[2]
    total = jnp.sum(sums[...], axis=0)
    inv = lax.rsqrt(total / (steps * NODES).astype(F32) + epsilon)
    inv = jnp.concatenate([inv, inv], axis=1)
    places = ((send, 0), (keep, 1))

    head_grad = mm_nt(dpred[...], w_out[...])
    pieces = []
    for b in range(SEQ):
        scaled = head_grad[b * HEAD : (b + 1) * HEAD] * inv[b : b + 1, :]
        row = lax.broadcasted_iota(jnp.int32, (HEAD, NODES), 0)
        scaled = jnp.where((row >= ROWS) & (at_end == 1), 0.0, scaled)
        pieces += [jnp.zeros((HALO, NODES), F32), scaled]
    grad = jnp.concatenate(pieces, axis=0).astype(BF16)

    for x in range(4):
        columns = slice(x * 1024, (x + 1) * 1024)
        out_grad = None
        for b in range(SEQ):
            part = mm(
                last_t[:, b * ROWS : (b + 1) * ROWS],
                dpred[b * HEAD : b * HEAD + ROWS, columns],
            ) * inv[b : b + 1, :1]
            out_grad = part if out_grad is None else out_grad + part
        for ref, half in places:
            for y in range(4):
                top = half * 128 + y * 32
                ref[x, y, :, :1024] = out_grad[top : top + 32].astype(BF16)

    def store_small(x, value):
        for ref, half in places:
            for y in range(4):
                top = half * 128 + y * 32
                ref[x, y, :, 1024:1280] = value[top : top + 32].astype(BF16)

    for layer in reversed(range(LAYERS)):
        grad_wide = grad.astype(F32)
        store_small(layer, mm(gated_t[layer], own_rows(grad_wide).astype(BF16)))
        gated_cot = mm_nt(grad, w_m[layer]).astype(BF16).astype(F32)
        filter_act = tanh_in[layer]
        gate_act = gate_in[layer]
        grad_preact = jnp.concatenate(
            [
                gated_cot * gate_act * (1.0 - filter_act * filter_act),
                gated_cot * filter_act * gate_act * (1.0 - gate_act),
            ],
            axis=1,
        )
        own_preact = own_rows(grad_preact).astype(BF16)
        grad_preact = grad_preact.astype(BF16)
        for tap in range(2):
            tap_grad = mm(taps_t[layer, tap], own_preact)
            for ref, half in places:
                for y_low in range(2):
                    top = half * 128 + y_low * 64
                    for x in range(4):
                        columns = slice(x * 128, (x + 1) * 128)
                        for low in range(2):
                            base = 1280 + low * 384 + layer * 128
                            ref[x, tap * 2 + y_low, :, base : base + 128] = tap_grad[
                                top + low * 32 : top + low * 32 + 32, columns
                            ].astype(BF16)
        grad_joined = mm_nt(grad_preact, w_f[layer]).astype(BF16)
        past = grad_joined[:, :NODES].astype(F32)
        now = grad_joined[:, NODES:].astype(F32)
        earlier = pltpu.roll(past, ALL_ROWS - 2**layer, 0)
        grad = ((grad_wide + now).astype(BF16).astype(F32) + earlier).astype(BF16)
    own = own_rows(grad.astype(F32)).astype(BF16)
    store_small(3, mm(cov_t[...], own))
    result = mm_nt(own, w_in[...]).astype(BF16)
    for b in range(SEQ):
        cov_grad[b] = result[b * ROWS : (b + 1) * ROWS]


def add_kernel(a, b, out):
    out[...] = (a[...].astype(F32) + b[...].astype(F32)).astype(BF16)


def plane_kernel(pieces, out):
    total = pieces[0].astype(F32)
    for i in range(1, pieces.shape[0]):
        total = total + pieces[i].astype(F32)
    for z in range(8):
        r = slice(z * 4, z * 4 + 4)
        first = jnp.concatenate([total[r, :512], total[r, 1024:1152]], axis=1)
        second = jnp.concatenate([total[r, 512:1024], total[r, 1152:1280]], axis=1)
        low = z % 4
        base = 1280 + (z // 4) * 384
        taps = total[low * 8 : low * 8 + 8, base : base + 384]
        both = jnp.concatenate([first, second], axis=0)
        out[z] = jnp.concatenate([both, taps], axis=1).astype(BF16)


def line_kernel(pieces, out):
    total = pieces[0].astype(F32)
    for i in range(1, pieces.shape[0]):
        total = total + pieces[i].astype(F32)
    out[...] = total.astype(BF16)


def finish_kernel(g, input_grad, filter_grad, mixing_grad, output_grad):
    for x in range(4):
        v = g[x].astype(F32)
        output_grad[:, x * 1024 : x * 1024 + 512] = v[:4, :512].astype(BF16)
        output_grad[:, x * 1024 + 512 : (x + 1) * 1024] = v[4:, :512].astype(BF16)
        small = jnp.concatenate([v[:4, 512:640], v[4:, 512:640]], axis=1).astype(BF16)
        if x < LAYERS:
            mixing_grad[x] = small
        else:
            input_grad[...] = small
        for layer in range(LAYERS):
            base = 640 + layer * 128
            filter_grad[layer, :, x * 128 : (x + 1) * 128] = v[:, base : base + 128].astype(BF16)


def call(kernel, out_shape, count, scratch=(), scalars=False):
    specs = vmem_specs(count)
    if scalars:
        specs = [pl.BlockSpec(memory_space=pltpu.SMEM)] + specs
    outs = jax.tree.map(lambda _: pl.BlockSpec(memory_space=VMEM), out_shape)
    return pl.pallas_call(
        kernel,
        out_shape=out_shape,
        in_specs=specs,
        out_specs=outs,
        scratch_shapes=scratch,
        compiler_params=PARAMS,
    )


def per_device(cov, obs, w_in, w_f, w_m, w_out):
    count = lax.axis_size(TM)
    me = lax.axis_index(TM)
    place = jnp.stack(
        [
            lax.axis_index("core"),
            jnp.where(me == count - 1, 1, 0),
            jnp.int32(count),
        ]
    ).astype(jnp.int32)
    to_next, to_prev, squares = call(
        start_kernel,
        (
            shape((SEQ, HALO, NODES), BF16),
            shape((SEQ, HALO, 2 * NODES), F32),
            shape((count, SEQ, 128), F32),
        ),
        2,
    )(cov, obs)
    from_prev = lax.ppermute(to_next, TM, [(i, i + 1) for i in range(count - 1)])
    from_next = lax.ppermute(to_prev, TM, [(i + 1, i) for i in range(count - 1)])
    sums = lax.all_to_all(squares, TM, 0, 0, tiled=True)

    saved = call(
        forward_kernel,
        (
            shape((LAYERS, ALL_ROWS, NODES), F32),
            shape((LAYERS, ALL_ROWS, NODES), F32),
            shape((ALL_HEAD, SCENARIOS * NODES), BF16),
            shape((NODES, SEQ * ROWS), BF16),
            shape((LAYERS, NODES, SEQ * ROWS), BF16),
            shape((NODES, SEQ * ROWS), BF16),
            shape((LAYERS, 2, NODES, SEQ * ROWS), BF16),
        ),
        8,
        scratch=[
            pltpu.VMEM((ALL_HEAD, SCENARIOS * NODES), F32),
            pltpu.VMEM((ALL_HEAD, NODES), F32),
        ],
        scalars=True,
    )(place, from_prev, cov, from_next, obs, w_in, w_f, w_m, w_out)

    piece = shape((4, 4, 32, 2048), BF16)
    cov_grad, send, keep = call(
        backward_kernel,
        (shape((SEQ, ROWS, NODES), BF16), piece, piece),
        12,
        scalars=True,
    )(place, sums, *saved, w_in, w_f, w_m, w_out)

    got = lax.ppermute(send, "core", [(0, 1), (1, 0)])
    chip = call(add_kernel, piece, 2)(keep, got)
    plane = lax.all_to_all(chip.reshape(16, 32, 2048), ("x", "y"), 0, 0, tiled=True)
    by_z = call(plane_kernel, shape((8, 8, 1024), BF16), 1)(plane)
    line = lax.all_to_all(by_z, "z", 0, 0, tiled=True)
    mine = call(line_kernel, shape((8, 1024), BF16), 1)(line)
    whole = lax.all_gather(mine, "x")
    input_grad, filter_grad, mixing_grad, output_grad = call(
        finish_kernel,
        (
            shape((4, NODES), BF16),
            shape((LAYERS, 8, 2 * NODES), BF16),
            shape((LAYERS, 4, NODES), BF16),
            shape((4, SCENARIOS * NODES), BF16),
        ),
        1,
    )(whole)
    return (cov_grad, input_grad, filter_grad, mixing_grad, output_grad)


def solution(mesh):
    inner = Mesh(mesh.devices.reshape(4, 8, 2, 4), ("y", "z", "core", "x"))
    data = P("x", TM, None)
    return jax.shard_map(
        per_device,
        mesh=inner,
        in_specs=(data, data, P(), P(), P(), P()),
        out_specs=(data, P(TM, None), P(None, TM, None), P(None, TM, None), P(TM, None)),
        check_vma=False,
    )
```

time: 589 us -> 135 us (0.23)
  blocking collectives: 374 us -> 61.5 us
  waiting for transfers between devices: 91 us -> 5.86 us
  matrix products: 43.1 us -> 0 us
  Pallas kernels: 0 us -> 29.6 us
  local copies, waits for them, and re-layouts: 32.3 us -> 17.2 us
  between operations: 15.4 us -> 0.72 us
  other arithmetic: 12.4 us -> 0.08 us
    unnamed x1 -> x0, blocking collectives: 264 us -> none
    psum x1 -> x0, blocking collectives: 110 us -> none  [per_device(): total_sq = lax.psum(local_sq, 'tm')]
    psum x1 -> x0, waiting for transfers between devices: 79 us -> none  [per_device(): lax.psum(shares[0].astype(jnp.bfloat16), 'region').astype(jnp.float32)]
    all_to_all x0 -> x2, blocking collectives: none -> 49.7 us  [the longest x1 34.4 us: per_device(): lax.all_to_all(chip.reshape(16, 32, 2048), ('x', 'y'), 0, 0, tiled=True)]
    dot_general x28 -> x0, matrix products: 43.1 us -> none  [the longest x3 18.9 us: energy(): jnp.einsum('...sn,...rn->...sr', scenario_vals, scenario_vals, precision=...]
    pallas_call x0 -> x7, Pallas kernels: none -> 29.6 us  [the longest x1 17.6 us: per_device(): call(forward_kernel, (shape((LAYERS, ALL_ROWS, NODES), F32), shape((LAYER...]
    all_to_all x0 -> x1, starting transfers between devices: none -> 12.1 us  [per_device(): sums = lax.all_to_all(squares, TM, 0, 0, tiled=True)]
    all_gather x0 -> x1, blocking collectives: none -> 11.9 us  [per_device(): whole = lax.all_gather(mine, 'x')]
  transfers between devices with their start and end apart: 8 -> 4, of which waited for: 6 -> 2; matrix products, arithmetic and copies ran while one was open for 3% -> 0% of each run, Pallas kernels for 0% -> 13%
where the time goes in v1:
time: 135 us
  blocking collectives  61.5 us (46%)
  Pallas kernels  29.6 us (22%)
  starting transfers between devices  19.8 us (15%)
  local copies, waits for them, and re-layouts  17.2 us (13%)
  waiting for transfers between devices  5.86 us (4%)
    all_to_all x1, blocking collectives, per_device(): lax.all_to_all(chip.reshape(16, 32, 2048), ('x', 'y'), 0, 0, tiled=True)  34.4 us
    pallas_call x1, Pallas kernels, per_device(): call(forward_kernel, (shape((LAYERS, ALL_ROWS, NODES), F32), shape((LAYER...  17.6 us
    unnamed x40, local copies, waits for them, and re-layouts  17.2 us
    all_to_all x1, blocking collectives, per_device(): line = lax.all_to_all(by_z, 'z', 0, 0, tiled=True)  15.2 us
    all_to_all x1, starting transfers between devices, per_device(): sums = lax.all_to_all(squares, TM, 0, 0, tiled=True)  12.1 us
    all_gather x1, blocking collectives, per_device(): whole = lax.all_gather(mine, 'x')  11.9 us
    pallas_call x1, Pallas kernels, per_device(): call(backward_kernel, (shape((SEQ, ROWS, NODES), BF16), piece, piece), 12...  8.15 us
    ppermute x1, starting transfers between devices, per_device(): lax.ppermute(to_prev, TM, [(i + 1, i) for i in range(count - 1)])  5.61 us
  transfers between devices with their start and end apart: 4, of which 2 were waited for; matrix products, arithmetic and copies ran while one was open for 0% of the time, Pallas kernels for 13%

profile of v1, /device:TPU:8, one launch (start us, length us, event | category | flops | bytes accessed | tf_op | source)
XLA Modules:
  0.0 134.7 jit_solution(6618216597074248177)
XLA Ops:
  0.6 0.9 copy-done.5
  1.6 0.9 copy-done.13
  2.5 0.8 shard_map.101
  3.3 12.1 %all-to-all-start = ((f32[64,2,128]{2,1,0:T(2,128)}), f32[64,2,128]{2,1,0:T(2,128)S(1)}, u32[]{:S(2)}, u32[]{:S(2)}) async-start(f32[64,2,128]{2,1,0:T(2,128)} %get-tuple-element.22), calls=%async_computation | async-start | bytes 131072 | tf_op jit(solution)/shard_map/all_to_all | solution.py:321
  15.4 2.1 %collective-permute-start = (bf16[2,8,256]{2,1,0:T(8,128)(2,1)S(1)}, bf16[2,8,256]{2,1,0:T(8,128)(2,1)S(1)}, u32[]{:S(2)}, u32[]{:S(2)}) collective-permute-start(bf16[2,8,256]{2,1,0:T(8,128)(2,1)S(1)} %get-tuple-element.23), channel_id=1, source_target_pairs={{0,4},{4,8},{8,12},{12,16},{16,20},{20,24},{24,28},{28,32},{32,36}... | collective-permute-start | bytes 24584 | tf_op jit(solution)/shard_map/ppermute | solution.py:319
  17.4 5.6 %collective-permute-start.1 = (f32[2,8,512]{2,1,0:T(8,128)S(1)}, f32[2,8,512]{2,1,0:T(8,128)S(1)}, u32[]{:S(2)}, u32[]{:S(2)}) collective-permute-start(f32[2,8,512]{2,1,0:T(8,128)S(1)} %get-tuple-element.24), channel_id=1, source_target_pairs={{4,0},{8,4},{12,8},{16,12},{20,16},{24,20},{28,24},{32,28},{36,32}... | collective-permute-start | bytes 98312 | tf_op jit(solution)/shard_map/ppermute | solution.py:320
  23.1 0.1 pad_add_fusion.place
  23.2 1.5 %collective-permute-done.1.from_next = f32[2,8,512]{2,1,0:T(8,128)S(1)} collective-permute-done((f32[2,8,512]{2,1,0:T(8,128)S(1)}, f32[2,8,512]{2,1,0:T(8,128)S(1)}, u32[]{:S(2)}, u32[]{:S(2)}) %collective-permute-start.1) | collective-permute-done | bytes 32800 | tf_op jit(solution)/shard_map/ppermute | solution.py:320
  24.6 1.4 %copy-done = bf16[3,512,512]{2,1,0:T(8,128)(2,1)S(1)} copy-done((bf16[3,512,512]{2,1,0:T(8,128)(2,1)S(1)}, bf16[3,512,512]{2,1,0:T(8,128)(2,1)}, u32[]{:S(2)}) %copy-start) | copy-done | bytes 1572888
  26.0 1.0 copy-done.3
  27.0 0.9 copy-done.6
  28.0 0.9 copy-done.11
  28.9 0.9 copy-done.14
  29.8 17.6 %shard_map.102 = (f32[3,288,256]{2,1,0:T(8,128)S(1)}, f32[3,288,256]{2,1,0:T(8,128)S(1)}, bf16[272,4096]{1,0:T(8,128)(2,1)}, bf16[256,256]{1,0:T(8,128)(2,1)S(1)...) custom-call(s32[3]{0:T(128)S(1)} %pad_add_fusion.place, ...), custom_call_target="tpu_custom_call" | custom-call | tf_op jit(solution)/shard_map/pallas_call | solution.py:323
  47.4 0.9 copy-done.7
  48.4 0.9 copy-done.9
  49.3 0.7 copy-done.15
  49.9 0.6 copy-done.17
  50.6 1.2 copy-done.8
  51.8 1.1 copy-done.10
  52.9 0.9 copy-done.16
  53.8 0.9 copy-done.18
  54.7 8.1 %shard_map.103 = (bf16[2,128,256]{2,1,0:T(8,128)(2,1)}, bf16[4,4,32,2048]{3,2,1,0:T(8,128)(2,1)}, bf16[4,4,32,2048]{3,2,1,0:T(8,128)(2,1)}) custom-call(s32[3]{0:T(128)S(1)} %pad_add_fusion.place, f32[64,2,128]{2,1,0:T(2,128)S(1)} %all-to-all-done.sums, f32[3,288,256]{2,1,0:T(8,128)S(1)} %get-tuple-element.25.tanh_in, f32[3,288,256]{2,1,0:T(8,128)S(1)} %copy-done.8, ...), custom_call_target="tpu_custom_call" | custom-call | tf_op jit(solution)/shard_map/pallas_call | solution.py:343
  62.8 4.4 %collective-permute-done.2.b = bf16[4,4,32,2048]{3,2,1,0:T(8,128)(2,1)S(1)} collective-permute-done((bf16[4,4,32,2048]{3,2,1,0:T(8,128)(2,1)}, bf16[4,4,32,2048]{3,2,1,0:T(8,128)(2,1)S(1)}, u32[]{:S(2)}, u32[]{:S(2)}) %collective-permute-start.2) | collective-permute-done | bytes 2097184 | tf_op jit(solution)/shard_map/ppermute | solution.py:350
  67.2 1.3 copy-done.19
  68.6 1.6 %copy-done.2 = bf16[4,4,32,2048]{3,2,1,0:T(8,128)(2,1)S(1)} copy-done((bf16[4,4,32,2048]{3,2,1,0:T(8,128)(2,1)S(1)}, bf16[4,4,32,2048]{3,2,1,0:T(8,128)(2,1)}, u32[]{:S(2)}) %copy-start.2) | copy-done | bytes 2097176
  70.1 2.1 %shard_map.104 = bf16[4,4,32,2048]{3,2,1,0:T(8,128)(2,1)S(1)} custom-call(bf16[4,4,32,2048]{3,2,1,0:T(8,128)(2,1)S(1)} %copy-done.2, bf16[4,4,32,2048]{3,2,1,0:T(8,128)(2,1)} %copy-done.19), custom_call_target="tpu_custom_call" | custom-call | tf_op jit(solution)/shard_map/pallas_call | solution.py:351
  72.2 34.4 %all_to_all.15.pieces = bf16[16,32,2048]{2,1,0:T(8,128)(2,1)S(1)} all-to-all(bf16[16,32,2048]{2,1,0:T(8,128)(2,1)S(1)} %bitcast.4), channel_id=1, replica_groups=mesh['y'=4,'z'=8,'core'=2,'x'=4] {'x','y'}, dimensions={0} | all-to-all | bytes 4194304 | tf_op jit(solution)/shard_map/all_to_all | solution.py:352
  106.7 0.3 shard_map.105
  106.9 15.2 %all_to_all.16.pieces = bf16[8,8,1024]{2,1,0:T(8,128)(2,1)S(1)} all-to-all(bf16[8,8,1024]{2,1,0:T(8,128)(2,1)S(1)} %shard_map.105), channel_id=1, replica_groups=mesh['y'=4,'z'=8,'core'=2,'x'=4] {'z'}, dimensions={0} | all-to-all | bytes 262144 | tf_op jit(solution)/shard_map/all_to_all | solution.py:354
  122.2 11.9 %all-gather = bf16[32,1024]{1,0:T(8,128)(2,1)S(1)} all-gather(bf16[8,1024]{1,0:T(8,128)(2,1)S(1)} %shard_map.106), channel_id=2, replica_groups=mesh['y'=4,'z'=8,'core'=2,'x'=4] {'x'}, dimensions={0}, use_global_device_ids=true | all-gather | bytes 81920 | tf_op jit(solution)/shard_map/all_gather | solution.py:356
  134.1 0.6 shard_map.107
  (27 shorter events, 0.1 us)
Async XLA Ops:
  0.6 1.0 copy-start.5
  1.6 0.9 copy-start.13
  3.3 47.3 %all-to-all-start = ((f32[64,2,128]{2,1,0:T(2,128)}), f32[64,2,128]{2,1,0:T(2,128)S(1)}, u32[]{:S(2)}, u32[]{:S(2)}) async-start(f32[64,2,128]{2,1,0:T(2,128)} %get-tuple-element.22), calls=%async_computation | async-start | bytes 131072 | tf_op jit(solution)/shard_map/all_to_all | solution.py:321
  15.4 7.8 %collective-permute-start = (bf16[2,8,256]{2,1,0:T(8,128)(2,1)S(1)}, bf16[2,8,256]{2,1,0:T(8,128)(2,1)S(1)}, u32[]{:S(2)}, u32[]{:S(2)}) collective-permute-start(bf16[2,8,256]{2,1,0:T(8,128)(2,1)S(1)} %get-tuple-element.23), channel_id=1, source_target_pairs={{0,4},{4,8},{8,12},{12,16},{16,20},{20,24},{24,28},{28,32},{32,36}... | collective-permute-start | bytes 24584 | tf_op jit(solution)/shard_map/ppermute | solution.py:319
  17.4 7.2 %collective-permute-start.1 = (f32[2,8,512]{2,1,0:T(8,128)S(1)}, f32[2,8,512]{2,1,0:T(8,128)S(1)}, u32[]{:S(2)}, u32[]{:S(2)}) collective-permute-start(f32[2,8,512]{2,1,0:T(8,128)S(1)} %get-tuple-element.24), channel_id=1, source_target_pairs={{4,0},{8,4},{12,8},{16,12},{20,16},{24,20},{28,24},{32,28},{36,32}... | collective-permute-start | bytes 98312 | tf_op jit(solution)/shard_map/ppermute | solution.py:320
  24.6 1.4 %copy-start = (bf16[3,512,512]{2,1,0:T(8,128)(2,1)S(1)}, bf16[3,512,512]{2,1,0:T(8,128)(2,1)}, u32[]{:S(2)}) copy-start(bf16[3,512,512]{2,1,0:T(8,128)(2,1)} %w_f.3) | copy-start | bytes 4718596
  26.0 1.0 copy-start.3
  27.0 0.9 copy-start.6
  28.0 0.9 copy-start.11
  28.9 0.9 copy-start.14
  29.8 20.8 %copy-start.1 = (bf16[3,512,512]{2,1,0:T(8,128)(2,1)S(1)}, bf16[3,512,512]{2,1,0:T(8,128)(2,1)}, u32[]{:S(2)}) copy-start(bf16[3,512,512]{2,1,0:T(8,128)(2,1)} %w_f.3) | copy-start | bytes 4718596
  29.8 20.8 %copy-start.4 = (bf16[3,256,256]{2,1,0:T(8,128)(2,1)S(1)}, bf16[3,256,256]{2,1,0:T(8,128)(2,1)}, u32[]{:S(2)}) copy-start(bf16[3,256,256]{2,1,0:T(8,128)(2,1)} %w_m.3) | copy-start | bytes 1179652
  29.8 20.8 %copy-start.12 = (bf16[256,256]{1,0:T(8,128)(2,1)S(1)}, bf16[256,256]{1,0:T(8,128)(2,1)}, u32[]{:S(2)}) copy-start(bf16[256,256]{1,0:T(8,128)(2,1)} %w_in.3) | copy-start | bytes 393220
  47.4 0.9 copy-start.7
  48.4 0.9 copy-start.9
  49.3 0.7 copy-start.15
  49.9 0.6 copy-start.17
  50.6 1.2 copy-start.8
  51.7 1.1 copy-start.10
  52.9 0.9 copy-start.16
  53.8 0.9 copy-start.18
  62.8 4.4 %collective-permute-start.2 = (bf16[4,4,32,2048]{3,2,1,0:T(8,128)(2,1)}, bf16[4,4,32,2048]{3,2,1,0:T(8,128)(2,1)S(1)}, u32[]{:S(2)}, u32[]{:S(2)}) collective-permute-start(bf16[4,4,32,2048]{3,2,1,0:T(8,128)(2,1)} %get-tuple-element.34), channel_id=1, source_target_pairs={{0,4},{4,0},{1,5},{5,1},{2,6},{6,2},{3,7},{7,3},{8,12},{12,8},{9,1... | collective-permute-start | bytes 6291464 | tf_op jit(solution)/shard_map/ppermute | solution.py:350
  67.2 1.3 copy-start.19
  68.6 1.6 %copy-start.2 = (bf16[4,4,32,2048]{3,2,1,0:T(8,128)(2,1)S(1)}, bf16[4,4,32,2048]{3,2,1,0:T(8,128)(2,1)}, u32[]{:S(2)}) copy-start(bf16[4,4,32,2048]{3,2,1,0:T(8,128)(2,1)} %get-tuple-element.33.a) | copy-start | bytes 6291460

commit v2 on v1

--- a/solution.py
+++ b/solution.py
@@ -1,5 +1,3 @@
-import functools
-
 import jax
 import jax.numpy as jnp
 from jax import lax
@@ -24,7 +22,6 @@
 F32 = jnp.float32
 BF16 = jnp.bfloat16
 VMEM = pltpu.VMEM
-PARAMS = pltpu.CompilerParams(vmem_limit_bytes=48 * 1024 * 1024)
 
 
 def mm(a, b):
@@ -35,19 +32,19 @@
     return lax.dot_general(a, b, (((1,), (1,)), ((), ())), preferred_element_type=F32)
 
 
-def vmem_specs(count):
-    return [pl.BlockSpec(memory_space=VMEM)] * count
-
-
 def shape(dims, dtype):
     return jax.ShapeDtypeStruct(dims, dtype)
 
 
-def start_kernel(cov, obs, to_next, to_prev, squares):
-    for b in range(SEQ):
-        to_next[b] = cov[b, ROWS - HALO :, :]
-        to_prev[b, :, :NODES] = cov[b, :HALO, :].astype(F32)
-        to_prev[b, :, NODES:] = obs[b, :HALO, :]
+def edge_kernel(cov_tail, cov_head, obs_head, to_next, to_prev):
+    for b in range(SEQ):
+        to_next[b] = cov_tail[b].astype(F32)[HALO:].astype(BF16)
+        to_prev[b, :, :NODES] = cov_head[b].astype(F32)[:HALO]
+        to_prev[b, :, NODES:] = obs_head[b]
+
+
+def square_kernel(obs, before, after, squares):
+    for b in range(SEQ):
         sq = obs[b] * obs[b]
         by_lane = jnp.sum(sq, axis=0, keepdims=True)
         total = jnp.sum(by_lane, axis=1, keepdims=True)
@@ -100,10 +97,19 @@
 
 
 def forward_kernel(
-    place, from_prev, cov, from_next, obs, w_in, w_f, w_m, w_out,
-    tanh_out, gate_out, dpred, cov_t, gated_t, last_t, taps_t,
-    pred, target,
+    place, from_prev, from_next, cov_hbm, obs_hbm, w_in_hbm, w_f_hbm, w_m_hbm, w_out_hbm,
+    tanh_hbm, gate_hbm, dpred_hbm, cov_t_hbm, gated_t_hbm, last_t_hbm, taps_t_hbm,
+    pred, target, cov, obs, w_in, w_f, w_m, w_out,
+    tanh_out, gate_out, dpred, cov_t, gated_t, last_t, taps_t, sems, out_sems,
 ):
+    cov_copy = pltpu.make_async_copy(cov_hbm, cov, sems.at[0])
+    w_in_copy = pltpu.make_async_copy(w_in_hbm, w_in, sems.at[1])
+    w_f_copy = pltpu.make_async_copy(w_f_hbm, w_f, sems.at[2])
+    w_m_copy = pltpu.make_async_copy(w_m_hbm, w_m, sems.at[3])
+    obs_copy = pltpu.make_async_copy(obs_hbm, obs, sems.at[4])
+    w_out_copy = pltpu.make_async_copy(w_out_hbm, w_out, sems.at[5])
+    for copy in (cov_copy, w_in_copy, w_f_copy, w_m_copy, obs_copy, w_out_copy):
+        copy.start()
     core = place[0]
     perm4 = permutation(core, 4)
     perm8 = permutation(core, 8)
@@ -111,6 +117,7 @@
     def turned(perm, x):
         return mm_nt(perm, own_rows(x).astype(BF16)).astype(BF16)
 
+    cov_copy.wait()
     pieces = []
     for b in range(SEQ):
         pieces += [
@@ -120,7 +127,10 @@
         ]
     x = jnp.concatenate(pieces, axis=0)
     cov_t[...] = turned(perm4, x)
+    w_in_copy.wait()
     hidden = mm(x.astype(BF16), w_in[...]).astype(BF16)
+    w_f_copy.wait()
+    w_m_copy.wait()
     for layer in range(LAYERS):
         wide = hidden.astype(F32)
         delayed_wide = pltpu.roll(wide, 2**layer, 0)
@@ -138,10 +148,23 @@
     wide = hidden.astype(F32)
     last_t[...] = turned(perm4, wide)
     head = jnp.concatenate([wide[HALO:BLOCK], wide[BLOCK + HALO :]], axis=0).astype(BF16)
+    w_out_copy.wait()
     pred[...] = mm(head, w_out[...])
+    obs_copy.wait()
     for b in range(SEQ):
         target[b * HEAD : b * HEAD + ROWS, :] = obs[b]
         target[b * HEAD + ROWS : (b + 1) * HEAD, :] = from_next[b, :, NODES:]
+
+    stores = [
+        pltpu.make_async_copy(tanh_out, tanh_hbm, out_sems.at[0]),
+        pltpu.make_async_copy(gate_out, gate_hbm, out_sems.at[1]),
+        pltpu.make_async_copy(cov_t, cov_t_hbm, out_sems.at[2]),
+        pltpu.make_async_copy(gated_t, gated_t_hbm, out_sems.at[3]),
+        pltpu.make_async_copy(last_t, last_t_hbm, out_sems.at[4]),
+        pltpu.make_async_copy(taps_t, taps_t_hbm, out_sems.at[5]),
+    ]
+    for copy in stores:
+        copy.start()
 
     def step(i, carry):
         halves = []
@@ -159,42 +182,77 @@
             dpred[at, s * NODES : (s + 1) * NODES] = both.astype(BF16)
         return carry
 
-    lax.fori_loop(0, ALL_HEAD // 16, step, 0)
+    first, last = 0, 0
+    for part, last in enumerate((12, ALL_HEAD // 16)):
+        lax.fori_loop(first, last, step, 0)
+        rows = pl.ds(first * 16, (last - first) * 16)
+        copy = pltpu.make_async_copy(dpred.at[rows], dpred_hbm.at[rows], out_sems.at[6 + part])
+        copy.start()
+        stores.append(copy)
+        first = last
+    for copy in stores:
+        copy.wait()
 
 
 def backward_kernel(
-    place, sums, tanh_in, gate_in, dpred, cov_t, gated_t, last_t, taps_t, w_in, w_f, w_m, w_out,
+    place, sums, tanh_hbm, gate_hbm, dpred_hbm, cov_t_hbm, gated_t_hbm, last_t_hbm, taps_t_hbm,
+    w_in_hbm, w_f_hbm, w_m_hbm, w_out_hbm,
     cov_grad, send, keep,
+    tanh_in, gate_in, dpred, cov_t, gated_t, last_t, taps_t, w_in, w_f, w_m, w_out, sems,
 ):
+    copies = [pltpu.make_async_copy(last_t_hbm, last_t, sems.at[0])]
+    for x in range(4):
+        columns = pl.ds(x * 1024, 1024)
+        copies.append(
+            pltpu.make_async_copy(dpred_hbm.at[:, columns], dpred.at[:, columns], sems.at[1 + x])
+        )
+    copies.append(pltpu.make_async_copy(w_out_hbm, w_out, sems.at[5]))
+    later = (
+        (w_m_hbm, w_m),
+        (gated_t_hbm, gated_t),
+        (tanh_hbm, tanh_in),
+        (gate_hbm, gate_in),
+        (w_f_hbm, w_f),
+        (taps_t_hbm, taps_t),
+        (cov_t_hbm, cov_t),
+        (w_in_hbm, w_in),
+    )
+    for k, (source, target) in enumerate(later):
+        copies.append(pltpu.make_async_copy(source, target, sems.at[6 + k]))
+    for copy in copies:
+        copy.start()
+    copies[0].wait()
     at_end = place[1]
     steps = ROWS * place[2]
     total = jnp.sum(sums[...], axis=0)
     inv = lax.rsqrt(total / (steps * NODES).astype(F32) + epsilon)
     inv = jnp.concatenate([inv, inv], axis=1)
-    places = ((send, 0), (keep, 1))
-
-    head_grad = mm_nt(dpred[...], w_out[...])
-    pieces = []
-    for b in range(SEQ):
-        scaled = head_grad[b * HEAD : (b + 1) * HEAD] * inv[b : b + 1, :]
-        row = lax.broadcasted_iota(jnp.int32, (HEAD, NODES), 0)
-        scaled = jnp.where((row >= ROWS) & (at_end == 1), 0.0, scaled)
-        pieces += [jnp.zeros((HALO, NODES), F32), scaled]
-    grad = jnp.concatenate(pieces, axis=0).astype(BF16)
-
     for x in range(4):
         columns = slice(x * 1024, (x + 1) * 1024)
         out_grad = None
+        copies[1 + x].wait()
         for b in range(SEQ):
             part = mm(
                 last_t[:, b * ROWS : (b + 1) * ROWS],
                 dpred[b * HEAD : b * HEAD + ROWS, columns],
             ) * inv[b : b + 1, :1]
             out_grad = part if out_grad is None else out_grad + part
-        for ref, half in places:
+        for ref, half in ((send, 0), (keep, 1)):
             for y in range(4):
                 top = half * 128 + y * 32
                 ref[x, y, :, :1024] = out_grad[top : top + 32].astype(BF16)
+    copies[5].wait()
+    head_grad = mm_nt(dpred[...], w_out[...])
+    pieces = []
+    for b in range(SEQ):
+        scaled = head_grad[b * HEAD : (b + 1) * HEAD] * inv[b : b + 1, :]
+        row = lax.broadcasted_iota(jnp.int32, (HEAD, NODES), 0)
+        scaled = jnp.where((row >= ROWS) & (at_end == 1), 0.0, scaled)
+        pieces += [jnp.zeros((HALO, NODES), F32), scaled]
+    grad = jnp.concatenate(pieces, axis=0).astype(BF16)
+    for copy in copies[6:]:
+        copy.wait()
+    places = ((send, 0), (keep, 1))
 
     def store_small(x, value):
         for ref, half in places:
@@ -241,8 +299,8 @@
         cov_grad[b] = result[b * ROWS : (b + 1) * ROWS]
 
 
-def add_kernel(a, b, out):
-    out[...] = (a[...].astype(F32) + b[...].astype(F32)).astype(BF16)
+def add_kernel(keep, got, out):
+    out[...] = keep[...] + got[...]
 
 
 def plane_kernel(pieces, out):
@@ -282,18 +340,22 @@
             filter_grad[layer, :, x * 128 : (x + 1) * 128] = v[:, base : base + 128].astype(BF16)
 
 
-def call(kernel, out_shape, count, scratch=(), scalars=False):
-    specs = vmem_specs(count)
-    if scalars:
-        specs = [pl.BlockSpec(memory_space=pltpu.SMEM)] + specs
-    outs = jax.tree.map(lambda _: pl.BlockSpec(memory_space=VMEM), out_shape)
+BACKWARD_LIMIT = 58
+HBM = pl.BlockSpec(memory_space=pltpu.HBM)
+ANY = pl.BlockSpec(memory_space=pl.ANY)
+SCALARS = pl.BlockSpec(memory_space=pltpu.SMEM)
+WHOLE = pl.BlockSpec(memory_space=VMEM)
+
+
+def call(kernel, out_shape, in_specs, scratch=(), limit=16, name=None, out_spec=WHOLE):
     return pl.pallas_call(
         kernel,
         out_shape=out_shape,
-        in_specs=specs,
-        out_specs=outs,
+        in_specs=in_specs,
+        out_specs=jax.tree.map(lambda _: out_spec, out_shape),
         scratch_shapes=scratch,
-        compiler_params=PARAMS,
+        compiler_params=pltpu.CompilerParams(vmem_limit_bytes=limit * 1024 * 1024),
+        name=name,
     )
 
 
@@ -307,52 +369,80 @@
             jnp.int32(count),
         ]
     ).astype(jnp.int32)
-    to_next, to_prev, squares = call(
-        start_kernel,
-        (
-            shape((SEQ, HALO, NODES), BF16),
-            shape((SEQ, HALO, 2 * NODES), F32),
-            shape((count, SEQ, 128), F32),
-        ),
-        2,
-    )(cov, obs)
+    to_next, to_prev = pl.pallas_call(
+        edge_kernel,
+        grid=(1,),
+        in_specs=[
+            pl.BlockSpec((SEQ, 16, NODES), lambda i: (0, ROWS // 16 - 1, 0)),
+            pl.BlockSpec((SEQ, 16, NODES), lambda i: (0, 0, 0)),
+            pl.BlockSpec((SEQ, HALO, NODES), lambda i: (0, 0, 0)),
+        ],
+        out_specs=(WHOLE, WHOLE),
+        out_shape=(shape((SEQ, HALO, NODES), BF16), shape((SEQ, HALO, 2 * NODES), F32)),
+        name="edges",
+    )(cov, cov, obs)
     from_prev = lax.ppermute(to_next, TM, [(i, i + 1) for i in range(count - 1)])
     from_next = lax.ppermute(to_prev, TM, [(i + 1, i) for i in range(count - 1)])
+    squares = pl.pallas_call(
+        square_kernel,
+        grid=(1,),
+        in_specs=[pl.BlockSpec((SEQ, ROWS, NODES), lambda i: (0, 0, 0)), ANY, ANY],
+        out_specs=WHOLE,
+        out_shape=shape((count, SEQ, 128), F32),
+        name="squares",
+    )(obs, from_prev, from_next)
     sums = lax.all_to_all(squares, TM, 0, 0, tiled=True)
 
+    saved_shapes = (
+        shape((LAYERS, ALL_ROWS, NODES), F32),
+        shape((LAYERS, ALL_ROWS, NODES), F32),
+        shape((ALL_HEAD, SCENARIOS * NODES), BF16),
+        shape((NODES, SEQ * ROWS), BF16),
+        shape((LAYERS, NODES, SEQ * ROWS), BF16),
+        shape((NODES, SEQ * ROWS), BF16),
+        shape((LAYERS, 2, NODES, SEQ * ROWS), BF16),
+    )
     saved = call(
         forward_kernel,
-        (
-            shape((LAYERS, ALL_ROWS, NODES), F32),
-            shape((LAYERS, ALL_ROWS, NODES), F32),
-            shape((ALL_HEAD, SCENARIOS * NODES), BF16),
-            shape((NODES, SEQ * ROWS), BF16),
-            shape((LAYERS, NODES, SEQ * ROWS), BF16),
-            shape((NODES, SEQ * ROWS), BF16),
-            shape((LAYERS, 2, NODES, SEQ * ROWS), BF16),
-        ),
-        8,
+        saved_shapes,
+        [SCALARS, WHOLE, WHOLE] + [HBM] * 6,
         scratch=[
-            pltpu.VMEM((ALL_HEAD, SCENARIOS * NODES), F32),
-            pltpu.VMEM((ALL_HEAD, NODES), F32),
+            VMEM((ALL_HEAD, SCENARIOS * NODES), F32),
+            VMEM((ALL_HEAD, NODES), F32),
+            VMEM(cov.shape, BF16),
+            VMEM(obs.shape, F32),
+            VMEM(w_in.shape, BF16),
+            VMEM(w_f.shape, BF16),
+            VMEM(w_m.shape, BF16),
+            VMEM(w_out.shape, BF16),
+            *(VMEM(saved.shape, saved.dtype) for saved in saved_shapes),
+            pltpu.SemaphoreType.DMA((6,)),
+            pltpu.SemaphoreType.DMA((8,)),
         ],
-        scalars=True,
-    )(place, from_prev, cov, from_next, obs, w_in, w_f, w_m, w_out)
+        limit=60,
+        name="forward",
+        out_spec=HBM,
+    )(place, from_prev, from_next, cov, obs, w_in, w_f, w_m, w_out)
 
     piece = shape((4, 4, 32, 2048), BF16)
     cov_grad, send, keep = call(
         backward_kernel,
         (shape((SEQ, ROWS, NODES), BF16), piece, piece),
-        12,
-        scalars=True,
+        [SCALARS, WHOLE] + [HBM] * 11,
+        scratch=[
+            *(VMEM(saved.shape, saved.dtype) for saved in saved_shapes),
+            *(VMEM(w.shape, BF16) for w in (w_in, w_f, w_m, w_out)),
+            pltpu.SemaphoreType.DMA((14,)),
+        ],
+        limit=BACKWARD_LIMIT,
+        name="backward",
     )(place, sums, *saved, w_in, w_f, w_m, w_out)
-
     got = lax.ppermute(send, "core", [(0, 1), (1, 0)])
-    chip = call(add_kernel, piece, 2)(keep, got)
+    chip = call(add_kernel, piece, [WHOLE] * 2, limit=4, name="pair")(keep, got)
     plane = lax.all_to_all(chip.reshape(16, 32, 2048), ("x", "y"), 0, 0, tiled=True)
-    by_z = call(plane_kernel, shape((8, 8, 1024), BF16), 1)(plane)
+    by_z = call(plane_kernel, shape((8, 8, 1024), BF16), [WHOLE], limit=4, name="plane")(plane)
     line = lax.all_to_all(by_z, "z", 0, 0, tiled=True)
-    mine = call(line_kernel, shape((8, 1024), BF16), 1)(line)
+    mine = call(line_kernel, shape((8, 1024), BF16), [WHOLE], limit=4, name="line")(line)
     whole = lax.all_gather(mine, "x")
     input_grad, filter_grad, mixing_grad, output_grad = call(
         finish_kernel,
@@ -362,7 +452,9 @@
             shape((LAYERS, 4, NODES), BF16),
             shape((4, SCENARIOS * NODES), BF16),
         ),
-        1,
+        [WHOLE],
+        limit=4,
+        name="finish",
     )(whole)
     return (cov_grad, input_grad, filter_grad, mixing_grad, output_grad)
 

time: 135 us -> 124 us (0.919)
  local copies, waits for them, and re-layouts: 17.2 us -> 3.42 us
  starting transfers between devices: 19.8 us -> 15.3 us
  waiting for transfers between devices: 5.86 us -> 9.59 us
  Pallas kernels: 29.6 us -> 32 us
    unnamed x40 -> x8, local copies, waits for them, and re-layouts: 17.2 us -> 3.42 us
    all_to_all x1, starting transfers between devices: 12.1 us -> 6.04 us  [per_device(): sums = lax.all_to_all(squares, TM, 0, 0, tiled=True)]
    ppermute x1, waiting for transfers between devices: 0.01 us -> 5.36 us  [per_device(): lax.ppermute(to_next, TM, [(i, i + 1) for i in range(count - 1)])]
    pallas_call x6 -> x7, Pallas kernels: 28.9 us -> 31.3 us  [the longest x1 17.9 us: per_device(): call(forward_kernel, saved_shapes, [SCALARS, WHOLE, WHOLE] + [HBM] * 6, s...]
    ppermute x1, waiting for transfers between devices: 1.48 us -> 0.01 us  [per_device(): lax.ppermute(to_prev, TM, [(i + 1, i) for i in range(count - 1)])]
    ppermute x1, starting transfers between devices: 5.61 us -> 7.08 us  [per_device(): lax.ppermute(to_prev, TM, [(i + 1, i) for i in range(count - 1)])]
  transfers between devices with their start and end apart: 4 -> 4, of which waited for: 2 -> 2; matrix products, arithmetic and copies ran while one was open for 0% -> 1% of each run, Pallas kernels for 13% -> 15%
where the time goes in v2:
time: 124 us
  blocking collectives  61.9 us (50%)
  Pallas kernels  32 us (26%)
  starting transfers between devices  15.3 us (12%)
  waiting for transfers between devices  9.59 us (8%)
  local copies, waits for them, and re-layouts  3.42 us (3%)
    all_to_all x1, blocking collectives, per_device(): lax.all_to_all(chip.reshape(16, 32, 2048), ('x', 'y'), 0, 0, tiled=True)  34.5 us
    pallas_call x1, Pallas kernels, per_device(): call(forward_kernel, saved_shapes, [SCALARS, WHOLE, WHOLE] + [HBM] * 6, s...  17.9 us
    all_to_all x1, blocking collectives, per_device(): line = lax.all_to_all(by_z, 'z', 0, 0, tiled=True)  15.6 us
    all_gather x1, blocking collectives, per_device(): whole = lax.all_gather(mine, 'x')  11.9 us
    pallas_call x1, Pallas kernels, per_device(): call(backward_kernel, (shape((SEQ, ROWS, NODES), BF16), piece, piece), [S...  9.8 us
    ppermute x1, starting transfers between devices, per_device(): lax.ppermute(to_prev, TM, [(i + 1, i) for i in range(count - 1)])  7.08 us
    all_to_all x1, starting transfers between devices, per_device(): sums = lax.all_to_all(squares, TM, 0, 0, tiled=True)  6.04 us
    ppermute x1, waiting for transfers between devices, per_device(): lax.ppermute(to_next, TM, [(i, i + 1) for i in range(count - 1)])  5.36 us
  transfers between devices with their start and end apart: 4, of which 2 were waited for; matrix products, arithmetic and copies ran while one was open for 1% of the time, Pallas kernels for 15%

profile of v2, /device:TPU:8, one launch (start us, length us, event | category | flops | bytes accessed | tf_op | source)
XLA Modules:
  0.0 123.5 jit_solution(2145992977443429814)
XLA Ops:
  0.6 1.4 %edges.1 = (bf16[2,8,256]{2,1,0:T(8,128)(2,1)}, f32[2,8,512]{2,1,0:T(8,128)}) custom-call(bf16[2,128,256]{2,1,0:T(8,128)(2,1)} %cov_hbm.1, bf16[2,128,256]{2,1,0:T(8,128)(2,1)} %cov_hbm.1, f32[2,128,256]{2,1,0:T(8,128)} %obs_hbm.1), custom_call_target="tpu_custom_call" | custom-call | tf_op jit(solution)/shard_map/edges/pallas_call | solution.py:372
  2.0 7.1 %collective-permute-start.1 = (f32[2,8,512]{2,1,0:T(8,128)}, f32[2,8,512]{2,1,0:T(8,128)S(1)}, u32[]{:S(2)}, u32[]{:S(2)}) collective-permute-start(f32[2,8,512]{2,1,0:T(8,128)} %get-tuple-element.22), channel_id=1, source_target_pairs={{4,0},{8,4},{12,8},{16,12},{20,16},{24,20},{28,24},{32,28},{36,32}... | collective-permute-start | bytes 98312 | tf_op jit(solution)/shard_map/ppermute | solution.py:385
  9.1 1.9 %collective-permute-start = (bf16[2,8,256]{2,1,0:T(8,128)(2,1)}, bf16[2,8,256]{2,1,0:T(8,128)(2,1)S(1)}, u32[]{:S(2)}, u32[]{:S(2)}) collective-permute-start(bf16[2,8,256]{2,1,0:T(8,128)(2,1)} %get-tuple-element.21), channel_id=1, source_target_pairs={{0,4},{4,8},{8,12},{12,16},{16,20},{20,24},{24,28},{28,32},{32,36}... | collective-permute-start | bytes 24584 | tf_op jit(solution)/shard_map/ppermute | solution.py:384
  11.0 5.4 %collective-permute-done.before.from_prev = bf16[2,8,256]{2,1,0:T(8,128)(2,1)S(1)} collective-permute-done((bf16[2,8,256]{2,1,0:T(8,128)(2,1)}, bf16[2,8,256]{2,1,0:T(8,128)(2,1)S(1)}, u32[]{:S(2)}, u32[]{:S(2)}) %collective-permute-start) | collective-permute-done | bytes 8224 | tf_op jit(solution)/shard_map/ppermute | solution.py:384
  16.4 0.0 copy-start.3
  16.4 0.0 collective-permute-done.1.after.from_next
  16.4 0.6 copy-done.3
  17.0 0.0 copy-start.2
  17.0 0.6 copy-done.2
  17.6 1.7 %squares.1 = f32[64,2,128]{2,1,0:T(2,128)} custom-call(f32[2,128,256]{2,1,0:T(8,128)} %obs_hbm.1, bf16[2,8,256]{2,1,0:T(8,128)(2,1)} %copy-done.3, f32[2,8,512]{2,1,0:T(8,128)} %copy-done.2), custom_call_target="tpu_custom_call" | custom-call | tf_op jit(solution)/shard_map/squares/pallas_call | solution.py:386
  19.3 6.0 %all-to-all-start = ((f32[64,2,128]{2,1,0:T(2,128)}), f32[64,2,128]{2,1,0:T(2,128)S(1)}, u32[]{:S(2)}, u32[]{:S(2)}) async-start(f32[64,2,128]{2,1,0:T(2,128)} %squares.1), calls=%async_computation | async-start | bytes 131072 | tf_op jit(solution)/shard_map/all_to_all | solution.py:394
  25.4 0.7 pad_add_fusion.place
  26.0 17.9 %forward.1 = (f32[3,288,256]{2,1,0:T(8,128)}, f32[3,288,256]{2,1,0:T(8,128)}, bf16[272,4096]{1,0:T(8,128)(2,1)}, bf16[256,256]{1,0:T(8,128)(2,1)}, bf16[3,256,25...) custom-call(s32[3]{0:T(128)} %pad_add_fusion.place, bf16[2,8,256]{2,1,0:T(8,128)(2,1)} %copy-done.3, ...), custom_call_target="tpu_custom_call" | custom-call | tf_op jit(solution)/shard_map/forward/pallas_call | solution.py:405
  44.0 0.0 all-to-all-done.sums
  44.0 0.0 copy-start.1
  44.0 0.6 copy-done.1
  44.6 9.8 %backward.1 = (bf16[2,128,256]{2,1,0:T(8,128)(2,1)}, bf16[4,4,32,2048]{3,2,1,0:T(8,128)(2,1)}, bf16[4,4,32,2048]{3,2,1,0:T(8,128)(2,1)}) custom-call(s32[3]{0:T(128)} %pad_add_fusion.place, f32[64,2,128]{2,1,0:T(2,128)} %copy-done.1, f32[3,288,256]{2,1,0:T(8,128)} %get-tuple-element.23.tanh_hbm, f32[3,288,256]{2,1,0:T(8,128)} %get-tuple-element.24.gate_hbm, ...), custom_call_target="tpu_custom_call" | custom-call | tf_op jit(solution)/shard_map/backward/pallas_call | solution.py:428
  54.4 0.2 collective-permute-start.2
  54.6 4.2 %collective-permute-done.2.got = bf16[4,4,32,2048]{3,2,1,0:T(8,128)(2,1)S(1)} collective-permute-done((bf16[4,4,32,2048]{3,2,1,0:T(8,128)(2,1)}, bf16[4,4,32,2048]{3,2,1,0:T(8,128)(2,1)S(1)}, u32[]{:S(2)}, u32[]{:S(2)}) %collective-permute-start.2) | collective-permute-done | bytes 2097184 | tf_op jit(solution)/shard_map/ppermute | solution.py:440
  58.9 0.0 copy-start
  58.9 1.6 %copy-done = bf16[4,4,32,2048]{3,2,1,0:T(8,128)(2,1)S(1)} copy-done((bf16[4,4,32,2048]{3,2,1,0:T(8,128)(2,1)S(1)}, bf16[4,4,32,2048]{3,2,1,0:T(8,128)(2,1)}, u32[]{:S(2)}) %copy-start) | copy-done | bytes 2097176
  60.5 0.2 pair.1
  60.7 34.5 %all_to_all.15.pieces = bf16[16,32,2048]{2,1,0:T(8,128)(2,1)S(1)} all-to-all(bf16[16,32,2048]{2,1,0:T(8,128)(2,1)S(1)} %bitcast.4), channel_id=1, replica_groups=mesh['y'=4,'z'=8,'core'=2,'x'=4] {'x','y'}, dimensions={0} | all-to-all | bytes 4194304 | tf_op jit(solution)/shard_map/all_to_all | solution.py:442
  95.1 0.3 plane.1
  95.4 15.6 %all_to_all.16.pieces = bf16[8,8,1024]{2,1,0:T(8,128)(2,1)S(1)} all-to-all(bf16[8,8,1024]{2,1,0:T(8,128)(2,1)S(1)} %plane.1), channel_id=1, replica_groups=mesh['y'=4,'z'=8,'core'=2,'x'=4] {'z'}, dimensions={0} | all-to-all | bytes 262144 | tf_op jit(solution)/shard_map/all_to_all | solution.py:444
  111.0 11.9 %all-gather = bf16[32,1024]{1,0:T(8,128)(2,1)S(1)} all-gather(bf16[8,1024]{1,0:T(8,128)(2,1)S(1)} %line.1), channel_id=2, replica_groups=mesh['y'=4,'z'=8,'core'=2,'x'=4] {'x'}, dimensions={0}, use_global_device_ids=true | all-gather | bytes 81920 | tf_op jit(solution)/shard_map/all_gather | solution.py:446
  122.9 0.6 finish.1
  (1 shorter events, 0.0 us)
Async XLA Ops:
  2.0 14.4 %collective-permute-start.1 = (f32[2,8,512]{2,1,0:T(8,128)}, f32[2,8,512]{2,1,0:T(8,128)S(1)}, u32[]{:S(2)}, u32[]{:S(2)}) collective-permute-start(f32[2,8,512]{2,1,0:T(8,128)} %get-tuple-element.22), channel_id=1, source_target_pairs={{4,0},{8,4},{12,8},{16,12},{20,16},{24,20},{28,24},{32,28},{36,32}... | collective-permute-start | bytes 98312 | tf_op jit(solution)/shard_map/ppermute | solution.py:385
  9.1 7.3 %collective-permute-start = (bf16[2,8,256]{2,1,0:T(8,128)(2,1)}, bf16[2,8,256]{2,1,0:T(8,128)(2,1)S(1)}, u32[]{:S(2)}, u32[]{:S(2)}) collective-permute-start(bf16[2,8,256]{2,1,0:T(8,128)(2,1)} %get-tuple-element.21), channel_id=1, source_target_pairs={{0,4},{4,8},{8,12},{12,16},{16,20},{20,24},{24,28},{28,32},{32,36}... | collective-permute-start | bytes 24584 | tf_op jit(solution)/shard_map/ppermute | solution.py:384
  16.4 0.6 copy-start.3
  17.0 0.6 copy-start.2
  19.3 24.7 %all-to-all-start = ((f32[64,2,128]{2,1,0:T(2,128)}), f32[64,2,128]{2,1,0:T(2,128)S(1)}, u32[]{:S(2)}, u32[]{:S(2)}) async-start(f32[64,2,128]{2,1,0:T(2,128)} %squares.1), calls=%async_computation | async-start | bytes 131072 | tf_op jit(solution)/shard_map/all_to_all | solution.py:394
  44.0 0.6 copy-start.1
  54.4 4.5 %collective-permute-start.2 = (bf16[4,4,32,2048]{3,2,1,0:T(8,128)(2,1)}, bf16[4,4,32,2048]{3,2,1,0:T(8,128)(2,1)S(1)}, u32[]{:S(2)}, u32[]{:S(2)}) collective-permute-start(bf16[4,4,32,2048]{3,2,1,0:T(8,128)(2,1)} %get-tuple-element.32), channel_id=1, source_target_pairs={{0,4},{4,0},{1,5},{5,1},{2,6},{6,2},{3,7},{7,3},{8,12},{12,8},{9,1... | collective-permute-start | bytes 6291464 | tf_op jit(solution)/shard_map/ppermute | solution.py:440
  58.9 1.6 %copy-start = (bf16[4,4,32,2048]{3,2,1,0:T(8,128)(2,1)S(1)}, bf16[4,4,32,2048]{3,2,1,0:T(8,128)(2,1)}, u32[]{:S(2)}) copy-start(bf16[4,4,32,2048]{3,2,1,0:T(8,128)(2,1)} %get-tuple-element.31.keep) | copy-start | bytes 6291460

commit v3 on v2

--- a/solution.py
+++ b/solution.py
@@ -36,15 +36,20 @@
     return jax.ShapeDtypeStruct(dims, dtype)
 
 
-def edge_kernel(cov_tail, cov_head, obs_head, to_next, to_prev):
+def start_kernel(cov_hbm, obs_hbm, to_next, to_prev, squares, tail, head, obs, sems):
+    copies = [
+        pltpu.make_async_copy(obs_hbm, obs, sems.at[0]),
+        pltpu.make_async_copy(cov_hbm.at[:, pl.ds(ROWS - 16, 16), :], tail, sems.at[1]),
+        pltpu.make_async_copy(cov_hbm.at[:, pl.ds(0, 16), :], head, sems.at[2]),
+    ]
+    for copy in copies:
+        copy.start()
+    for copy in copies:
+        copy.wait()
     for b in range(SEQ):
-        to_next[b] = cov_tail[b].astype(F32)[HALO:].astype(BF16)
-        to_prev[b, :, :NODES] = cov_head[b].astype(F32)[:HALO]
-        to_prev[b, :, NODES:] = obs_head[b]
-
-
-def square_kernel(obs, before, after, squares):
-    for b in range(SEQ):
+        to_next[b] = tail[b].astype(F32)[16 - HALO :].astype(BF16)
+        to_prev[b, :, :NODES] = head[b].astype(F32)[:HALO]
+        to_prev[b, :, NODES:] = obs[b, :HALO, :]
         sq = obs[b] * obs[b]
         by_lane = jnp.sum(sq, axis=0, keepdims=True)
         total = jnp.sum(by_lane, axis=1, keepdims=True)
@@ -65,35 +70,27 @@
     return jnp.where(c == wanted, 1.0, 0.0).astype(BF16)
 
 
+def inverse_root(total, factor):
+    return lax.rsqrt(total * (1.0 / (NODES * factor * factor)) + epsilon / (factor * factor))
+
+
 def energy_rows(y, o):
-    inv_nodes = 1.0 / NODES
-
-    def distance(a, b):
+    to_target = 1.0 / (SCENARIOS * NODES)
+    between = 1.0 / (SCENARIOS * (SCENARIOS - 1) * NODES)
+
+    def pull(a, b, factor):
         d0 = a[0] - b[0]
         d1 = a[1] - b[1]
-        return jnp.sum(d0 * d0 + d1 * d1, axis=1, keepdims=True)
-
-    alpha = [
-        lax.rsqrt(distance(y[s], o) * inv_nodes + epsilon) * (1.0 / (SCENARIOS * NODES))
-        for s in range(SCENARIOS)
-    ]
-    factor = 1.0 / (SCENARIOS * (SCENARIOS - 1) * NODES)
-    beta = {}
+        weight = inverse_root(jnp.sum(d0 * d0 + d1 * d1, axis=1, keepdims=True), factor)
+        return weight * d0, weight * d1
+
+    result = [pull(y[s], o, to_target) for s in range(SCENARIOS)]
     for s in range(SCENARIOS):
         for r in range(s + 1, SCENARIOS):
-            beta[s, r] = lax.rsqrt(distance(y[s], y[r]) * inv_nodes + epsilon) * factor
-    result = []
-    for s in range(SCENARIOS):
-        gamma = alpha[s]
-        acc = [-(alpha[s] * o[0]), -(alpha[s] * o[1])]
-        for r in range(SCENARIOS):
-            if r == s:
-                continue
-            weight = beta[min(s, r), max(s, r)]
-            gamma = gamma - weight
-            acc = [acc[0] + weight * y[r][0], acc[1] + weight * y[r][1]]
-        result.append(jnp.concatenate([acc[0] + gamma * y[s][0], acc[1] + gamma * y[s][1]], axis=1))
-    return result
+            p0, p1 = pull(y[s], y[r], between)
+            result[s] = (result[s][0] - p0, result[s][1] - p1)
+            result[r] = (result[r][0] + p0, result[r][1] + p1)
+    return [jnp.concatenate(pair, axis=1) for pair in result]
 
 
 def forward_kernel(
@@ -340,7 +337,7 @@
             filter_grad[layer, :, x * 128 : (x + 1) * 128] = v[:, base : base + 128].astype(BF16)
 
 
-BACKWARD_LIMIT = 58
+BACKWARD_LIMIT = 40
 HBM = pl.BlockSpec(memory_space=pltpu.HBM)
 ANY = pl.BlockSpec(memory_space=pl.ANY)
 SCALARS = pl.BlockSpec(memory_space=pltpu.SMEM)
@@ -369,38 +366,38 @@
             jnp.int32(count),
         ]
     ).astype(jnp.int32)
-    to_next, to_prev = pl.pallas_call(
-        edge_kernel,
-        grid=(1,),
-        in_specs=[
-            pl.BlockSpec((SEQ, 16, NODES), lambda i: (0, ROWS // 16 - 1, 0)),
-            pl.BlockSpec((SEQ, 16, NODES), lambda i: (0, 0, 0)),
-            pl.BlockSpec((SEQ, HALO, NODES), lambda i: (0, 0, 0)),
+    cov, obs, w_in, w_f, w_m, w_out = (
+        pltpu.with_memory_space_constraint(a, pltpu.HBM) for a in (cov, obs, w_in, w_f, w_m, w_out)
+    )
+    to_next, to_prev, squares = call(
+        start_kernel,
+        (
+            shape((SEQ, HALO, NODES), BF16),
+            shape((SEQ, HALO, 2 * NODES), F32),
+            shape((count, SEQ, 128), F32),
+        ),
+        [HBM, HBM],
+        scratch=[
+            VMEM((SEQ, 16, NODES), BF16),
+            VMEM((SEQ, 16, NODES), BF16),
+            VMEM(obs.shape, F32),
+            pltpu.SemaphoreType.DMA((3,)),
         ],
-        out_specs=(WHOLE, WHOLE),
-        out_shape=(shape((SEQ, HALO, NODES), BF16), shape((SEQ, HALO, 2 * NODES), F32)),
-        name="edges",
-    )(cov, cov, obs)
+        limit=4,
+        name="start",
+    )(cov, obs)
+    sums = lax.all_to_all(squares, TM, 0, 0, tiled=True)
     from_prev = lax.ppermute(to_next, TM, [(i, i + 1) for i in range(count - 1)])
     from_next = lax.ppermute(to_prev, TM, [(i + 1, i) for i in range(count - 1)])
-    squares = pl.pallas_call(
-        square_kernel,
-        grid=(1,),
-        in_specs=[pl.BlockSpec((SEQ, ROWS, NODES), lambda i: (0, 0, 0)), ANY, ANY],
-        out_specs=WHOLE,
-        out_shape=shape((count, SEQ, 128), F32),
-        name="squares",
-    )(obs, from_prev, from_next)
-    sums = lax.all_to_all(squares, TM, 0, 0, tiled=True)
 
     saved_shapes = (
-        shape((LAYERS, ALL_ROWS, NODES), F32),
-        shape((LAYERS, ALL_ROWS, NODES), F32),
-        shape((ALL_HEAD, SCENARIOS * NODES), BF16),
-        shape((NODES, SEQ * ROWS), BF16),
-        shape((LAYERS, NODES, SEQ * ROWS), BF16),
-        shape((NODES, SEQ * ROWS), BF16),
-        shape((LAYERS, 2, NODES, SEQ * ROWS), BF16),
+        pltpu.HBM((LAYERS, ALL_ROWS, NODES), F32),
+        pltpu.HBM((LAYERS, ALL_ROWS, NODES), F32),
+        pltpu.HBM((ALL_HEAD, SCENARIOS * NODES), BF16),
+        pltpu.HBM((NODES, SEQ * ROWS), BF16),
+        pltpu.HBM((LAYERS, NODES, SEQ * ROWS), BF16),
+        pltpu.HBM((NODES, SEQ * ROWS), BF16),
+        pltpu.HBM((LAYERS, 2, NODES, SEQ * ROWS), BF16),
     )
     saved = call(
         forward_kernel,
@@ -419,11 +416,12 @@
             pltpu.SemaphoreType.DMA((6,)),
             pltpu.SemaphoreType.DMA((8,)),
         ],
-        limit=60,
+        limit=40,
         name="forward",
         out_spec=HBM,
     )(place, from_prev, from_next, cov, obs, w_in, w_f, w_m, w_out)
 
+    saved = [pltpu.with_memory_space_constraint(a, pltpu.HBM) for a in saved]
     piece = shape((4, 4, 32, 2048), BF16)
     cov_grad, send, keep = call(
         backward_kernel,

time: 124 us -> 114 us (0.919)
  Pallas kernels: 32 us -> 25.4 us
  starting transfers between devices: 15.3 us -> 19.9 us
  waiting for transfers between devices: 9.59 us -> 5.64 us
  local copies, waits for them, and re-layouts: 3.42 us -> 0 us
    all_to_all x1, starting transfers between devices: 6.04 us -> 12.1 us  [per_device(): sums = lax.all_to_all(squares, TM, 0, 0, tiled=True)]
    ppermute x1, waiting for transfers between devices: 5.36 us -> 0.01 us  [per_device(): lax.ppermute(to_next, TM, [(i, i + 1) for i in range(count - 1)])]
    pallas_call x1, Pallas kernels: 17.9 us -> 14.3 us  [per_device(): call(forward_kernel, saved_shapes, [SCALARS, WHOLE, WHOLE] + [HBM] * 6, s...]
    unnamed x8 -> x0, local copies, waits for them, and re-layouts: 3.42 us -> none
    pallas_call x1, Pallas kernels: 9.8 us -> 8.17 us  [per_device(): call(backward_kernel, (shape((SEQ, ROWS, NODES), BF16), piece, piece), [S...]
    ppermute x1, waiting for transfers between devices: 0.01 us -> 1.48 us  [per_device(): lax.ppermute(to_prev, TM, [(i + 1, i) for i in range(count - 1)])]
    ppermute x1, starting transfers between devices: 7.08 us -> 5.61 us  [per_device(): lax.ppermute(to_prev, TM, [(i + 1, i) for i in range(count - 1)])]
    pallas_call x2 -> x1, Pallas kernels: 3.09 us -> 1.75 us  [per_device(): call(start_kernel, (shape((SEQ, HALO, NODES), BF16), shape((SEQ, HALO, 2...]
  transfers between devices with their start and end apart: 4 -> 4, of which waited for: 2 -> 2; matrix products, arithmetic and copies ran while one was open for 1% -> 0% of each run, Pallas kernels for 15% -> 13%
where the time goes in v3:
time: 114 us; the launch traced here: 113 us
  blocking collectives  61.5 us (54%)
  Pallas kernels  25.4 us (22%)
  starting transfers between devices  19.9 us (17%)
  waiting for transfers between devices  5.64 us (5%)
    all_to_all x1, blocking collectives, per_device(): lax.all_to_all(chip.reshape(16, 32, 2048), ('x', 'y'), 0, 0, tiled=True)  34.4 us
    all_to_all x1, blocking collectives, per_device(): line = lax.all_to_all(by_z, 'z', 0, 0, tiled=True)  15.2 us
    pallas_call x1, Pallas kernels, per_device(): call(forward_kernel, saved_shapes, [SCALARS, WHOLE, WHOLE] + [HBM] * 6, s...  14.3 us
    all_to_all x1, starting transfers between devices, per_device(): sums = lax.all_to_all(squares, TM, 0, 0, tiled=True)  12.1 us
    all_gather x1, blocking collectives, per_device(): whole = lax.all_gather(mine, 'x')  11.9 us
    pallas_call x1, Pallas kernels, per_device(): call(backward_kernel, (shape((SEQ, ROWS, NODES), BF16), piece, piece), [S...  8.17 us
    ppermute x1, starting transfers between devices, per_device(): lax.ppermute(to_prev, TM, [(i + 1, i) for i in range(count - 1)])  5.61 us
    ppermute x1, waiting for transfers between devices, per_device(): got = lax.ppermute(send, 'core', [(0, 1), (1, 0)])  4.15 us
  transfers between devices with their start and end apart: 4, of which 2 were waited for; matrix products, arithmetic and copies ran while one was open for 0% of the time, Pallas kernels for 13%

profile of v3, /device:TPU:8, one launch (start us, length us, event | category | flops | bytes accessed | tf_op | source)
XLA Modules:
  0.0 113.2 jit_solution(502354021677835536)
XLA Ops:
  0.6 1.7 %start.1 = (bf16[2,8,256]{2,1,0:T(8,128)(2,1)S(1)}, f32[2,8,512]{2,1,0:T(8,128)S(1)}, f32[64,2,128]{2,1,0:T(2,128)}) custom-call(bf16[2,128,256]{2,1,0:T(8,128)(2,1)} %cov_hbm.3, f32[2,128,256]{2,1,0:T(8,128)} %obs_hbm.3), custom_call_target="tpu_custom_call" | custom-call | tf_op jit(solution)/shard_map/start/pallas_call | solution.py:372
  2.4 12.1 %all-to-all-start = ((f32[64,2,128]{2,1,0:T(2,128)}), f32[64,2,128]{2,1,0:T(2,128)S(1)}, u32[]{:S(2)}, u32[]{:S(2)}) async-start(f32[64,2,128]{2,1,0:T(2,128)} %get-tuple-element.22), calls=%async_computation | async-start | bytes 131072 | tf_op jit(solution)/shard_map/all_to_all | solution.py:389
  14.5 2.1 %collective-permute-start = (bf16[2,8,256]{2,1,0:T(8,128)(2,1)S(1)}, bf16[2,8,256]{2,1,0:T(8,128)(2,1)S(1)}, u32[]{:S(2)}, u32[]{:S(2)}) collective-permute-start(bf16[2,8,256]{2,1,0:T(8,128)(2,1)S(1)} %get-tuple-element.23), channel_id=1, source_target_pairs={{0,4},{4,8},{8,12},{12,16},{16,20},{20,24},{24,28},{28,32},{32,36}... | collective-permute-start | bytes 24584 | tf_op jit(solution)/shard_map/ppermute | solution.py:390
  16.6 5.6 %collective-permute-start.1 = (f32[2,8,512]{2,1,0:T(8,128)S(1)}, f32[2,8,512]{2,1,0:T(8,128)S(1)}, u32[]{:S(2)}, u32[]{:S(2)}) collective-permute-start(f32[2,8,512]{2,1,0:T(8,128)S(1)} %get-tuple-element.24), channel_id=1, source_target_pairs={{4,0},{8,4},{12,8},{16,12},{20,16},{24,20},{28,24},{32,28},{36,32}... | collective-permute-start | bytes 98312 | tf_op jit(solution)/shard_map/ppermute | solution.py:391
  22.2 0.1 pad_add_fusion.place
  22.3 0.0 collective-permute-done.from_prev
  22.3 1.5 %collective-permute-done.1.from_next = f32[2,8,512]{2,1,0:T(8,128)S(1)} collective-permute-done((f32[2,8,512]{2,1,0:T(8,128)S(1)}, f32[2,8,512]{2,1,0:T(8,128)S(1)}, u32[]{:S(2)}, u32[]{:S(2)}) %collective-permute-start.1) | collective-permute-done | bytes 32800 | tf_op jit(solution)/shard_map/ppermute | solution.py:391
  23.8 14.3 %forward.1 = (f32[3,288,256]{2,1,0:T(8,128)}, f32[3,288,256]{2,1,0:T(8,128)}, bf16[272,4096]{1,0:T(8,128)(2,1)}, bf16[256,256]{1,0:T(8,128)(2,1)}, bf16[3,256,25...) custom-call(s32[3]{0:T(128)S(1)} %pad_add_fusion.place, ...), custom_call_target="tpu_custom_call" | custom-call | tf_op jit(solution)/shard_map/forward/pallas_call | solution.py:402
  38.1 0.0 all-to-all-done.sums
  38.1 8.2 %backward.1 = (bf16[2,128,256]{2,1,0:T(8,128)(2,1)}, bf16[4,4,32,2048]{3,2,1,0:T(8,128)(2,1)S(1)}, bf16[4,4,32,2048]{3,2,1,0:T(8,128)(2,1)S(1)}) custom-call(s32[3]{0:T(128)S(1)} %pad_add_fusion.place, f32[64,2,128]{2,1,0:T(2,128)S(1)} %all-to-all-done.sums, f32[3,288,256]{2,1,0:T(8,128)} %get-tuple-element.25.tanh_hbm, ...), custom_call_target="tpu_custom_call" | custom-call | tf_op jit(solution)/shard_map/backward/pallas_call | solution.py:426
  46.3 0.1 collective-permute-start.2
  46.4 4.1 %collective-permute-done.2.got = bf16[4,4,32,2048]{3,2,1,0:T(8,128)(2,1)S(1)} collective-permute-done((bf16[4,4,32,2048]{3,2,1,0:T(8,128)(2,1)S(1)}, bf16[4,4,32,2048]{3,2,1,0:T(8,128)(2,1)S(1)}, u32[]{:S(2)}, u32[]{:S(2)}) %collective-permute-start.2) | collective-permute-done | bytes 2097184 | tf_op jit(solution)/shard_map/ppermute | solution.py:438
  50.6 0.2 pair.1
  50.8 34.4 %all_to_all.15.pieces = bf16[16,32,2048]{2,1,0:T(8,128)(2,1)S(1)} all-to-all(bf16[16,32,2048]{2,1,0:T(8,128)(2,1)S(1)} %bitcast.4), channel_id=1, replica_groups=mesh['y'=4,'z'=8,'core'=2,'x'=4] {'x','y'}, dimensions={0} | all-to-all | bytes 4194304 | tf_op jit(solution)/shard_map/all_to_all | solution.py:440
  85.2 0.3 plane.1
  85.5 15.2 %all_to_all.16.pieces = bf16[8,8,1024]{2,1,0:T(8,128)(2,1)S(1)} all-to-all(bf16[8,8,1024]{2,1,0:T(8,128)(2,1)S(1)} %plane.1), channel_id=1, replica_groups=mesh['y'=4,'z'=8,'core'=2,'x'=4] {'z'}, dimensions={0} | all-to-all | bytes 262144 | tf_op jit(solution)/shard_map/all_to_all | solution.py:442
  100.7 11.9 %all-gather = bf16[32,1024]{1,0:T(8,128)(2,1)S(1)} all-gather(bf16[8,1024]{1,0:T(8,128)(2,1)S(1)} %line.1), channel_id=2, replica_groups=mesh['y'=4,'z'=8,'core'=2,'x'=4] {'x'}, dimensions={0}, use_global_device_ids=true | all-gather | bytes 81920 | tf_op jit(solution)/shard_map/all_gather | solution.py:444
  112.6 0.6 finish.1
  (1 shorter events, 0.0 us)
Async XLA Ops:
  2.4 35.7 %all-to-all-start = ((f32[64,2,128]{2,1,0:T(2,128)}), f32[64,2,128]{2,1,0:T(2,128)S(1)}, u32[]{:S(2)}, u32[]{:S(2)}) async-start(f32[64,2,128]{2,1,0:T(2,128)} %get-tuple-element.22), calls=%async_computation | async-start | bytes 131072 | tf_op jit(solution)/shard_map/all_to_all | solution.py:389
  14.5 7.8 %collective-permute-start = (bf16[2,8,256]{2,1,0:T(8,128)(2,1)S(1)}, bf16[2,8,256]{2,1,0:T(8,128)(2,1)S(1)}, u32[]{:S(2)}, u32[]{:S(2)}) collective-permute-start(bf16[2,8,256]{2,1,0:T(8,128)(2,1)S(1)} %get-tuple-element.23), channel_id=1, source_target_pairs={{0,4},{4,8},{8,12},{12,16},{16,20},{20,24},{24,28},{28,32},{32,36}... | collective-permute-start | bytes 24584 | tf_op jit(solution)/shard_map/ppermute | solution.py:390
  16.6 7.2 %collective-permute-start.1 = (f32[2,8,512]{2,1,0:T(8,128)S(1)}, f32[2,8,512]{2,1,0:T(8,128)S(1)}, u32[]{:S(2)}, u32[]{:S(2)}) collective-permute-start(f32[2,8,512]{2,1,0:T(8,128)S(1)} %get-tuple-element.24), channel_id=1, source_target_pairs={{4,0},{8,4},{12,8},{16,12},{20,16},{24,20},{28,24},{32,28},{36,32}... | collective-permute-start | bytes 98312 | tf_op jit(solution)/shard_map/ppermute | solution.py:391
  46.3 4.2 %collective-permute-start.2 = (bf16[4,4,32,2048]{3,2,1,0:T(8,128)(2,1)S(1)}, bf16[4,4,32,2048]{3,2,1,0:T(8,128)(2,1)S(1)}, u32[]{:S(2)}, u32[]{:S(2)}) collective-permute-start(bf16[4,4,32,2048]{3,2,1,0:T(8,128)(2,1)S(1)} %get-tuple-element.34), channel_id=1, source_target_pairs={{0,4},{4,0},{1,5},{5,1},{2,6},{6,2},{3,7},{7,3},{8,12},{12,8},{9,1... | collective-permute-start | bytes 6291464 | tf_op jit(solution)/shard_map/ppermute | solution.py:438

commit v4 on v3

--- a/solution.py
+++ b/solution.py
@@ -16,8 +16,8 @@
 BLOCK = ROWS + 2 * HALO
 SEQ = 2
 ALL_ROWS = SEQ * BLOCK
-HEAD = ROWS + HALO
-ALL_HEAD = SEQ * HEAD
+OWN = SEQ * ROWS
+ALL_HEAD = OWN + SEQ * HALO
 TM = ("y", "z", "core")
 F32 = jnp.float32
 BF16 = jnp.bfloat16
@@ -60,6 +60,10 @@
     return jnp.concatenate([x[HALO : HALO + ROWS], x[BLOCK + HALO : BLOCK + HALO + ROWS]], axis=0)
 
 
+def after_rows(x):
+    return jnp.concatenate([x[BLOCK - HALO : BLOCK], x[2 * BLOCK - HALO :]], axis=0)
+
+
 def permutation(core, group):
     i = lax.broadcasted_iota(jnp.int32, (NODES, NODES), 0)
     c = lax.broadcasted_iota(jnp.int32, (NODES, NODES), 1)
@@ -70,34 +74,33 @@
     return jnp.where(c == wanted, 1.0, 0.0).astype(BF16)
 
 
-def inverse_root(total, factor):
-    return lax.rsqrt(total * (1.0 / (NODES * factor * factor)) + epsilon / (factor * factor))
-
-
-def energy_rows(y, o):
-    to_target = 1.0 / (SCENARIOS * NODES)
-    between = 1.0 / (SCENARIOS * (SCENARIOS - 1) * NODES)
-
-    def pull(a, b, factor):
+def energy_rows(y, o, scale):
+    def pull(a, b):
         d0 = a[0] - b[0]
         d1 = a[1] - b[1]
-        weight = inverse_root(jnp.sum(d0 * d0 + d1 * d1, axis=1, keepdims=True), factor)
-        return weight * d0, weight * d1
-
-    result = [pull(y[s], o, to_target) for s in range(SCENARIOS)]
+        total = jnp.sum(d0 * d0 + d1 * d1, axis=1, keepdims=True)
+        return d0, d1, lax.rsqrt(total + NODES * epsilon)
+
+    result = []
+    for s in range(SCENARIOS):
+        d0, d1, weight = pull(y[s], o)
+        weight = weight * (SCENARIOS - 1)
+        result.append((weight * d0, weight * d1))
     for s in range(SCENARIOS):
         for r in range(s + 1, SCENARIOS):
-            p0, p1 = pull(y[s], y[r], between)
+            d0, d1, weight = pull(y[s], y[r])
+            p0 = weight * d0
+            p1 = weight * d1
             result[s] = (result[s][0] - p0, result[s][1] - p1)
             result[r] = (result[r][0] + p0, result[r][1] + p1)
-    return [jnp.concatenate(pair, axis=1) for pair in result]
-
-
-def forward_kernel(
-    place, from_prev, from_next, cov_hbm, obs_hbm, w_in_hbm, w_f_hbm, w_m_hbm, w_out_hbm,
-    tanh_hbm, gate_hbm, dpred_hbm, cov_t_hbm, gated_t_hbm, last_t_hbm, taps_t_hbm,
+    return [jnp.concatenate([scale * p0, scale * p1], axis=1) for p0, p1 in result]
+
+
+def step_kernel(
+    place, from_prev, from_next, sums, cov_hbm, obs_hbm, w_in_hbm, w_f_hbm, w_m_hbm, w_out_hbm,
+    cov_grad, send, keep,
     pred, target, cov, obs, w_in, w_f, w_m, w_out,
-    tanh_out, gate_out, dpred, cov_t, gated_t, last_t, taps_t, sems, out_sems,
+    tanh_act, gate_act, dpred, cov_t, gated_t, last_t, taps_t, sems,
 ):
     cov_copy = pltpu.make_async_copy(cov_hbm, cov, sems.at[0])
     w_in_copy = pltpu.make_async_copy(w_in_hbm, w_in, sems.at[1])
@@ -135,121 +138,67 @@
         taps_t[layer, 0] = turned(perm8, delayed_wide)
         taps_t[layer, 1] = turned(perm8, wide)
         preact = mm(delayed, w_f[layer, :NODES, :]) + mm(hidden, w_f[layer, NODES:, :])
-        filter_act = jnp.tanh(preact[:, :NODES])
-        gate_act = jax.nn.sigmoid(preact[:, NODES:])
-        tanh_out[layer] = filter_act
-        gate_out[layer] = gate_act
-        gated = (filter_act * gate_act).astype(BF16)
+        through = jnp.tanh(preact[:, :NODES])
+        gate = jax.nn.sigmoid(preact[:, NODES:])
+        tanh_act[layer] = through
+        gate_act[layer] = gate
+        gated = (through * gate).astype(BF16)
         gated_t[layer] = turned(perm4, gated.astype(F32))
         hidden = (wide + mm(gated, w_m[layer])).astype(BF16)
     wide = hidden.astype(F32)
     last_t[...] = turned(perm4, wide)
-    head = jnp.concatenate([wide[HALO:BLOCK], wide[BLOCK + HALO :]], axis=0).astype(BF16)
+    head = jnp.concatenate([own_rows(wide), after_rows(wide)], axis=0).astype(BF16)
     w_out_copy.wait()
     pred[...] = mm(head, w_out[...])
     obs_copy.wait()
     for b in range(SEQ):
-        target[b * HEAD : b * HEAD + ROWS, :] = obs[b]
-        target[b * HEAD + ROWS : (b + 1) * HEAD, :] = from_next[b, :, NODES:]
-
-    stores = [
-        pltpu.make_async_copy(tanh_out, tanh_hbm, out_sems.at[0]),
-        pltpu.make_async_copy(gate_out, gate_hbm, out_sems.at[1]),
-        pltpu.make_async_copy(cov_t, cov_t_hbm, out_sems.at[2]),
-        pltpu.make_async_copy(gated_t, gated_t_hbm, out_sems.at[3]),
-        pltpu.make_async_copy(last_t, last_t_hbm, out_sems.at[4]),
-        pltpu.make_async_copy(taps_t, taps_t_hbm, out_sems.at[5]),
-    ]
-    for copy in stores:
-        copy.start()
+        target[b * ROWS : (b + 1) * ROWS, :] = obs[b]
+        target[OWN + b * HALO : OWN + (b + 1) * HALO, :] = from_next[b, :, NODES:]
+
+    at_end = place[1]
+    steps = ROWS * place[2]
+    total = jnp.sum(sums[...], axis=0)
+    inv = lax.rsqrt(total / (steps * NODES).astype(F32) + epsilon)
+    inv = inv * (NODES**0.5 / (SCENARIOS * (SCENARIOS - 1) * NODES))
 
     def step(i, carry):
         halves = []
         for part in range(2):
-            at = pl.ds(pl.multiple_of(i * 16 + part * 8, 8), 8)
+            chunk = i * 2 + part
+            first = (chunk < ROWS // 8) | (chunk == OWN // 8)
+            beyond = (chunk >= OWN // 8) & (at_end == 1)
+            scale = jnp.where(beyond, 0.0, jnp.where(first, inv[0:1], inv[1:2]))
+            at = pl.ds(pl.multiple_of(chunk * 8, 8), 8)
             y = [
                 (pred[at, s * NODES : s * NODES + 128], pred[at, s * NODES + 128 : (s + 1) * NODES])
                 for s in range(SCENARIOS)
             ]
             o = (target[at, :128], target[at, 128:])
-            halves.append(energy_rows(y, o))
+            halves.append(energy_rows(y, o, scale))
         at = pl.ds(pl.multiple_of(i * 16, 16), 16)
         for s in range(SCENARIOS):
             both = jnp.concatenate([halves[0][s], halves[1][s]], axis=0)
             dpred[at, s * NODES : (s + 1) * NODES] = both.astype(BF16)
         return carry
 
-    first, last = 0, 0
-    for part, last in enumerate((12, ALL_HEAD // 16)):
-        lax.fori_loop(first, last, step, 0)
-        rows = pl.ds(first * 16, (last - first) * 16)
-        copy = pltpu.make_async_copy(dpred.at[rows], dpred_hbm.at[rows], out_sems.at[6 + part])
-        copy.start()
-        stores.append(copy)
-        first = last
-    for copy in stores:
-        copy.wait()
-
-
-def backward_kernel(
-    place, sums, tanh_hbm, gate_hbm, dpred_hbm, cov_t_hbm, gated_t_hbm, last_t_hbm, taps_t_hbm,
-    w_in_hbm, w_f_hbm, w_m_hbm, w_out_hbm,
-    cov_grad, send, keep,
-    tanh_in, gate_in, dpred, cov_t, gated_t, last_t, taps_t, w_in, w_f, w_m, w_out, sems,
-):
-    copies = [pltpu.make_async_copy(last_t_hbm, last_t, sems.at[0])]
+    lax.fori_loop(0, ALL_HEAD // 16, step, 0)
+
+    places = ((send, 0), (keep, 1))
     for x in range(4):
-        columns = pl.ds(x * 1024, 1024)
-        copies.append(
-            pltpu.make_async_copy(dpred_hbm.at[:, columns], dpred.at[:, columns], sems.at[1 + x])
-        )
-    copies.append(pltpu.make_async_copy(w_out_hbm, w_out, sems.at[5]))
-    later = (
-        (w_m_hbm, w_m),
-        (gated_t_hbm, gated_t),
-        (tanh_hbm, tanh_in),
-        (gate_hbm, gate_in),
-        (w_f_hbm, w_f),
-        (taps_t_hbm, taps_t),
-        (cov_t_hbm, cov_t),
-        (w_in_hbm, w_in),
-    )
-    for k, (source, target) in enumerate(later):
-        copies.append(pltpu.make_async_copy(source, target, sems.at[6 + k]))
-    for copy in copies:
-        copy.start()
-    copies[0].wait()
-    at_end = place[1]
-    steps = ROWS * place[2]
-    total = jnp.sum(sums[...], axis=0)
-    inv = lax.rsqrt(total / (steps * NODES).astype(F32) + epsilon)
-    inv = jnp.concatenate([inv, inv], axis=1)
-    for x in range(4):
-        columns = slice(x * 1024, (x + 1) * 1024)
-        out_grad = None
-        copies[1 + x].wait()
-        for b in range(SEQ):
-            part = mm(
-                last_t[:, b * ROWS : (b + 1) * ROWS],
-                dpred[b * HEAD : b * HEAD + ROWS, columns],
-            ) * inv[b : b + 1, :1]
-            out_grad = part if out_grad is None else out_grad + part
-        for ref, half in ((send, 0), (keep, 1)):
+        out_grad = mm(last_t[...], dpred[:OWN, x * 1024 : (x + 1) * 1024])
+        for ref, half in places:
             for y in range(4):
                 top = half * 128 + y * 32
                 ref[x, y, :, :1024] = out_grad[top : top + 32].astype(BF16)
-    copies[5].wait()
     head_grad = mm_nt(dpred[...], w_out[...])
     pieces = []
     for b in range(SEQ):
-        scaled = head_grad[b * HEAD : (b + 1) * HEAD] * inv[b : b + 1, :]
-        row = lax.broadcasted_iota(jnp.int32, (HEAD, NODES), 0)
-        scaled = jnp.where((row >= ROWS) & (at_end == 1), 0.0, scaled)
-        pieces += [jnp.zeros((HALO, NODES), F32), scaled]
+        pieces += [
+            jnp.zeros((HALO, NODES), F32),
+            head_grad[b * ROWS : (b + 1) * ROWS],
+            head_grad[OWN + b * HALO : OWN + (b + 1) * HALO],
+        ]
     grad = jnp.concatenate(pieces, axis=0).astype(BF16)
-    for copy in copies[6:]:
-        copy.wait()
-    places = ((send, 0), (keep, 1))
 
     def store_small(x, value):
         for ref, half in places:
@@ -261,12 +210,12 @@
         grad_wide = grad.astype(F32)
         store_small(layer, mm(gated_t[layer], own_rows(grad_wide).astype(BF16)))
         gated_cot = mm_nt(grad, w_m[layer]).astype(BF16).astype(F32)
-        filter_act = tanh_in[layer]
-        gate_act = gate_in[layer]
+        through = tanh_act[layer]
+        gate = gate_act[layer]
         grad_preact = jnp.concatenate(
             [
-                gated_cot * gate_act * (1.0 - filter_act * filter_act),
-                gated_cot * filter_act * gate_act * (1.0 - gate_act),
+                gated_cot * gate * (1.0 - through * through),
+                gated_cot * through * gate * (1.0 - gate),
             ],
             axis=1,
         )
@@ -337,19 +286,18 @@
             filter_grad[layer, :, x * 128 : (x + 1) * 128] = v[:, base : base + 128].astype(BF16)
 
 
-BACKWARD_LIMIT = 40
 HBM = pl.BlockSpec(memory_space=pltpu.HBM)
 ANY = pl.BlockSpec(memory_space=pl.ANY)
 SCALARS = pl.BlockSpec(memory_space=pltpu.SMEM)
 WHOLE = pl.BlockSpec(memory_space=VMEM)
 
 
-def call(kernel, out_shape, in_specs, scratch=(), limit=16, name=None, out_spec=WHOLE):
+def call(kernel, out_shape, in_specs, scratch=(), limit=16, name=None):
     return pl.pallas_call(
         kernel,
         out_shape=out_shape,
         in_specs=in_specs,
-        out_specs=jax.tree.map(lambda _: out_spec, out_shape),
+        out_specs=jax.tree.map(lambda _: WHOLE, out_shape),
         scratch_shapes=scratch,
         compiler_params=pltpu.CompilerParams(vmem_limit_bytes=limit * 1024 * 1024),
         name=name,
@@ -390,19 +338,11 @@
     from_prev = lax.ppermute(to_next, TM, [(i, i + 1) for i in range(count - 1)])
     from_next = lax.ppermute(to_prev, TM, [(i + 1, i) for i in range(count - 1)])
 
-    saved_shapes = (
-        pltpu.HBM((LAYERS, ALL_ROWS, NODES), F32),
-        pltpu.HBM((LAYERS, ALL_ROWS, NODES), F32),
-        pltpu.HBM((ALL_HEAD, SCENARIOS * NODES), BF16),
-        pltpu.HBM((NODES, SEQ * ROWS), BF16),
-        pltpu.HBM((LAYERS, NODES, SEQ * ROWS), BF16),
-        pltpu.HBM((NODES, SEQ * ROWS), BF16),
-        pltpu.HBM((LAYERS, 2, NODES, SEQ * ROWS), BF16),
-    )
-    saved = call(
-        forward_kernel,
-        saved_shapes,
-        [SCALARS, WHOLE, WHOLE] + [HBM] * 6,
+    piece = shape((4, 4, 32, 2048), BF16)
+    cov_grad, send, keep = call(
+        step_kernel,
+        (shape((SEQ, ROWS, NODES), BF16), piece, piece),
+        [SCALARS, WHOLE, WHOLE, WHOLE] + [HBM] * 6,
         scratch=[
             VMEM((ALL_HEAD, SCENARIOS * NODES), F32),
             VMEM((ALL_HEAD, NODES), F32),
@@ -412,29 +352,18 @@
             VMEM(w_f.shape, BF16),
             VMEM(w_m.shape, BF16),
             VMEM(w_out.shape, BF16),
-            *(VMEM(saved.shape, saved.dtype) for saved in saved_shapes),
+            VMEM((LAYERS, ALL_ROWS, NODES), F32),
+            VMEM((LAYERS, ALL_ROWS, NODES), F32),
+            VMEM((ALL_HEAD, SCENARIOS * NODES), BF16),
+            VMEM((NODES, OWN), BF16),
+            VMEM((LAYERS, NODES, OWN), BF16),
+            VMEM((NODES, OWN), BF16),
+            VMEM((LAYERS, 2, NODES, OWN), BF16),
             pltpu.SemaphoreType.DMA((6,)),
-            pltpu.SemaphoreType.DMA((8,)),
         ],
-        limit=40,
-        name="forward",
-        out_spec=HBM,
-    )(place, from_prev, from_next, cov, obs, w_in, w_f, w_m, w_out)
-
-    saved = [pltpu.with_memory_space_constraint(a, pltpu.HBM) for a in saved]
-    piece = shape((4, 4, 32, 2048), BF16)
-    cov_grad, send, keep = call(
-        backward_kernel,
-        (shape((SEQ, ROWS, NODES), BF16), piece, piece),
-        [SCALARS, WHOLE] + [HBM] * 11,
-        scratch=[
-            *(VMEM(saved.shape, saved.dtype) for saved in saved_shapes),
-            *(VMEM(w.shape, BF16) for w in (w_in, w_f, w_m, w_out)),
-            pltpu.SemaphoreType.DMA((14,)),
-        ],
-        limit=BACKWARD_LIMIT,
-        name="backward",
-    )(place, sums, *saved, w_in, w_f, w_m, w_out)
+        limit=44,
+        name="step",
+    )(place, from_prev, from_next, sums, cov, obs, w_in, w_f, w_m, w_out)
     got = lax.ppermute(send, "core", [(0, 1), (1, 0)])
     chip = call(add_kernel, piece, [WHOLE] * 2, limit=4, name="pair")(keep, got)
     plane = lax.all_to_all(chip.reshape(16, 32, 2048), ("x", "y"), 0, 0, tiled=True)

time: 114 us -> 110 us (0.965)
  Pallas kernels: 25.4 us -> 21.4 us
    pallas_call x2 -> x1, Pallas kernels: 22.5 us -> 18.5 us  [per_device(): call(step_kernel, (shape((SEQ, ROWS, NODES), BF16), piece, piece), [SCALA...]
  transfers between devices with their start and end apart: 4 -> 4, of which waited for: 2 -> 2; matrix products, arithmetic and copies ran while one was open for 0% -> 0% of each run, Pallas kernels for 13% -> 0%
where the time goes in v4:
time: 110 us; the launch traced here: 109 us
  blocking collectives  61.5 us (56%)
  Pallas kernels  21.4 us (19%)
  starting transfers between devices  19.9 us (18%)
  waiting for transfers between devices  5.64 us (5%)
    all_to_all x1, blocking collectives, per_device(): lax.all_to_all(chip.reshape(16, 32, 2048), ('x', 'y'), 0, 0, tiled=True)  34.5 us
    pallas_call x1, Pallas kernels, per_device(): call(step_kernel, (shape((SEQ, ROWS, NODES), BF16), piece, piece), [SCALA...  18.5 us
    all_to_all x1, blocking collectives, per_device(): line = lax.all_to_all(by_z, 'z', 0, 0, tiled=True)  15.2 us
    all_to_all x1, starting transfers between devices, per_device(): sums = lax.all_to_all(squares, TM, 0, 0, tiled=True)  12.1 us
    all_gather x1, blocking collectives, per_device(): whole = lax.all_gather(mine, 'x')  11.9 us
    ppermute x1, starting transfers between devices, per_device(): lax.ppermute(to_prev, TM, [(i + 1, i) for i in range(count - 1)])  5.61 us
    ppermute x1, waiting for transfers between devices, per_device(): got = lax.ppermute(send, 'core', [(0, 1), (1, 0)])  4.15 us
  transfers between devices with their start and end apart: 4, of which 2 were waited for; matrix products, arithmetic and copies ran while one was open for 0% of the time, Pallas kernels for 0%

profile of v4, /device:TPU:8, one launch (start us, length us, event | category | flops | bytes accessed | tf_op | source)
XLA Modules:
  0.0 109.3 jit_solution(17967740136530490725)
XLA Ops:
  0.6 1.7 %start.1 = (bf16[2,8,256]{2,1,0:T(8,128)(2,1)S(1)}, f32[2,8,512]{2,1,0:T(8,128)S(1)}, f32[64,2,128]{2,1,0:T(2,128)}) custom-call(bf16[2,128,256]{2,1,0:T(8,128)(2,1)} %cov_hbm.3, f32[2,128,256]{2,1,0:T(8,128)} %obs_hbm.3), custom_call_target="tpu_custom_call" | custom-call | tf_op jit(solution)/shard_map/start/pallas_call | solution.py:320
  2.4 12.1 %all-to-all-start = ((f32[64,2,128]{2,1,0:T(2,128)}), f32[64,2,128]{2,1,0:T(2,128)S(1)}, u32[]{:S(2)}, u32[]{:S(2)}) async-start(f32[64,2,128]{2,1,0:T(2,128)} %get-tuple-element.17), calls=%async_computation | async-start | bytes 131072 | tf_op jit(solution)/shard_map/all_to_all | solution.py:337
  14.5 2.1 %collective-permute-start = (bf16[2,8,256]{2,1,0:T(8,128)(2,1)S(1)}, bf16[2,8,256]{2,1,0:T(8,128)(2,1)S(1)}, u32[]{:S(2)}, u32[]{:S(2)}) collective-permute-start(bf16[2,8,256]{2,1,0:T(8,128)(2,1)S(1)} %get-tuple-element.15), channel_id=1, source_target_pairs={{0,4},{4,8},{8,12},{12,16},{16,20},{20,24},{24,28},{28,32},{32,36}... | collective-permute-start | bytes 24584 | tf_op jit(solution)/shard_map/ppermute | solution.py:338
  16.6 5.6 %collective-permute-start.1 = (f32[2,8,512]{2,1,0:T(8,128)S(1)}, f32[2,8,512]{2,1,0:T(8,128)S(1)}, u32[]{:S(2)}, u32[]{:S(2)}) collective-permute-start(f32[2,8,512]{2,1,0:T(8,128)S(1)} %get-tuple-element.16), channel_id=1, source_target_pairs={{4,0},{8,4},{12,8},{16,12},{20,16},{24,20},{28,24},{32,28},{36,32}... | collective-permute-start | bytes 98312 | tf_op jit(solution)/shard_map/ppermute | solution.py:339
  22.2 0.1 pad_add_fusion.place
  22.3 0.0 collective-permute-done.from_prev
  22.3 1.5 %collective-permute-done.1.from_next = f32[2,8,512]{2,1,0:T(8,128)S(1)} collective-permute-done((f32[2,8,512]{2,1,0:T(8,128)S(1)}, f32[2,8,512]{2,1,0:T(8,128)S(1)}, u32[]{:S(2)}, u32[]{:S(2)}) %collective-permute-start.1) | collective-permute-done | bytes 32800 | tf_op jit(solution)/shard_map/ppermute | solution.py:339
  23.8 0.0 all-to-all-done.sums
  23.8 18.5 %step.1 = (bf16[2,128,256]{2,1,0:T(8,128)(2,1)}, bf16[4,4,32,2048]{3,2,1,0:T(8,128)(2,1)S(1)}, bf16[4,4,32,2048]{3,2,1,0:T(8,128)(2,1)S(1)}) custom-call(s32[3]{0:T(128)S(1)} %pad_add_fusion.place, bf16[2,8,256]{2,1,0:T(8,128)(2,1)S(1)} %collective-permute-done.from_prev, f32[2,8,512]{2,1,0:T(8,128)S(1)} %collective-permute-done.1.from_next, ...), custom_call_target="tpu_custom_call" | custom-call | tf_op jit(solution)/shard_map/step/pallas_call | solution.py:342
  42.2 0.1 collective-permute-start.2
  42.4 4.1 %collective-permute-done.2.got = bf16[4,4,32,2048]{3,2,1,0:T(8,128)(2,1)S(1)} collective-permute-done((bf16[4,4,32,2048]{3,2,1,0:T(8,128)(2,1)S(1)}, bf16[4,4,32,2048]{3,2,1,0:T(8,128)(2,1)S(1)}, u32[]{:S(2)}, u32[]{:S(2)}) %collective-permute-start.2) | collective-permute-done | bytes 2097184 | tf_op jit(solution)/shard_map/ppermute | solution.py:367
  46.5 0.3 pair.1
  46.8 34.5 %all_to_all.15.pieces = bf16[16,32,2048]{2,1,0:T(8,128)(2,1)S(1)} all-to-all(bf16[16,32,2048]{2,1,0:T(8,128)(2,1)S(1)} %bitcast.4), channel_id=1, replica_groups=mesh['y'=4,'z'=8,'core'=2,'x'=4] {'x','y'}, dimensions={0} | all-to-all | bytes 4194304 | tf_op jit(solution)/shard_map/all_to_all | solution.py:369
  81.3 0.3 plane.1
  81.5 15.2 %all_to_all.16.pieces = bf16[8,8,1024]{2,1,0:T(8,128)(2,1)S(1)} all-to-all(bf16[8,8,1024]{2,1,0:T(8,128)(2,1)S(1)} %plane.1), channel_id=1, replica_groups=mesh['y'=4,'z'=8,'core'=2,'x'=4] {'z'}, dimensions={0} | all-to-all | bytes 262144 | tf_op jit(solution)/shard_map/all_to_all | solution.py:371
  96.8 11.9 %all-gather = bf16[32,1024]{1,0:T(8,128)(2,1)S(1)} all-gather(bf16[8,1024]{1,0:T(8,128)(2,1)S(1)} %line.1), channel_id=2, replica_groups=mesh['y'=4,'z'=8,'core'=2,'x'=4] {'x'}, dimensions={0}, use_global_device_ids=true | all-gather | bytes 81920 | tf_op jit(solution)/shard_map/all_gather | solution.py:373
  108.6 0.6 finish.1
  (1 shorter events, 0.0 us)
Async XLA Ops:
  2.4 21.4 %all-to-all-start = ((f32[64,2,128]{2,1,0:T(2,128)}), f32[64,2,128]{2,1,0:T(2,128)S(1)}, u32[]{:S(2)}, u32[]{:S(2)}) async-start(f32[64,2,128]{2,1,0:T(2,128)} %get-tuple-element.17), calls=%async_computation | async-start | bytes 131072 | tf_op jit(solution)/shard_map/all_to_all | solution.py:337
  14.5 7.8 %collective-permute-start = (bf16[2,8,256]{2,1,0:T(8,128)(2,1)S(1)}, bf16[2,8,256]{2,1,0:T(8,128)(2,1)S(1)}, u32[]{:S(2)}, u32[]{:S(2)}) collective-permute-start(bf16[2,8,256]{2,1,0:T(8,128)(2,1)S(1)} %get-tuple-element.15), channel_id=1, source_target_pairs={{0,4},{4,8},{8,12},{12,16},{16,20},{20,24},{24,28},{28,32},{32,36}... | collective-permute-start | bytes 24584 | tf_op jit(solution)/shard_map/ppermute | solution.py:338
  16.6 7.2 %collective-permute-start.1 = (f32[2,8,512]{2,1,0:T(8,128)S(1)}, f32[2,8,512]{2,1,0:T(8,128)S(1)}, u32[]{:S(2)}, u32[]{:S(2)}) collective-permute-start(f32[2,8,512]{2,1,0:T(8,128)S(1)} %get-tuple-element.16), channel_id=1, source_target_pairs={{4,0},{8,4},{12,8},{16,12},{20,16},{24,20},{28,24},{32,28},{36,32}... | collective-permute-start | bytes 98312 | tf_op jit(solution)/shard_map/ppermute | solution.py:339
  42.2 4.2 %collective-permute-start.2 = (bf16[4,4,32,2048]{3,2,1,0:T(8,128)(2,1)S(1)}, bf16[4,4,32,2048]{3,2,1,0:T(8,128)(2,1)S(1)}, u32[]{:S(2)}, u32[]{:S(2)}) collective-permute-start(bf16[4,4,32,2048]{3,2,1,0:T(8,128)(2,1)S(1)} %get-tuple-element.20), channel_id=1, source_target_pairs={{0,4},{4,0},{1,5},{5,1},{2,6},{6,2},{3,7},{7,3},{8,12},{12,8},{9,1... | collective-permute-start | bytes 6291464 | tf_op jit(solution)/shard_map/ppermute | solution.py:367

commit v5 on v4

--- a/solution.py
+++ b/solution.py
@@ -13,11 +13,11 @@
 LAYERS = 3
 HALO = 8
 ROWS = 128
-BLOCK = ROWS + 2 * HALO
+BLOCK = HALO + ROWS
 SEQ = 2
 ALL_ROWS = SEQ * BLOCK
 OWN = SEQ * ROWS
-ALL_HEAD = OWN + SEQ * HALO
+EDGE = 16
 TM = ("y", "z", "core")
 F32 = jnp.float32
 BF16 = jnp.bfloat16
@@ -36,32 +36,30 @@
     return jax.ShapeDtypeStruct(dims, dtype)
 
 
-def start_kernel(cov_hbm, obs_hbm, to_next, to_prev, squares, tail, head, obs, sems):
+def start_kernel(cov_hbm, obs_hbm, to_next, squares, tail, obs, sems):
     copies = [
         pltpu.make_async_copy(obs_hbm, obs, sems.at[0]),
-        pltpu.make_async_copy(cov_hbm.at[:, pl.ds(ROWS - 16, 16), :], tail, sems.at[1]),
-        pltpu.make_async_copy(cov_hbm.at[:, pl.ds(0, 16), :], head, sems.at[2]),
+        pltpu.make_async_copy(cov_hbm.at[:, pl.ds(ROWS - EDGE, EDGE), :], tail, sems.at[1]),
     ]
     for copy in copies:
         copy.start()
     for copy in copies:
         copy.wait()
     for b in range(SEQ):
-        to_next[b] = tail[b].astype(F32)[16 - HALO :].astype(BF16)
-        to_prev[b, :, :NODES] = head[b].astype(F32)[:HALO]
-        to_prev[b, :, NODES:] = obs[b, :HALO, :]
-        sq = obs[b] * obs[b]
+        to_next[b] = tail[b].astype(F32)[EDGE - HALO :].astype(BF16)
+        mine = obs[b * ROWS : (b + 1) * ROWS]
+        sq = mine * mine
         by_lane = jnp.sum(sq, axis=0, keepdims=True)
         total = jnp.sum(by_lane, axis=1, keepdims=True)
         squares[:, b, :] = jnp.broadcast_to(total, (squares.shape[0], 128))
 
 
 def own_rows(x):
-    return jnp.concatenate([x[HALO : HALO + ROWS], x[BLOCK + HALO : BLOCK + HALO + ROWS]], axis=0)
-
-
-def after_rows(x):
-    return jnp.concatenate([x[BLOCK - HALO : BLOCK], x[2 * BLOCK - HALO :]], axis=0)
+    return jnp.concatenate([x[HALO:BLOCK], x[BLOCK + HALO :]], axis=0)
+
+
+def arranged(x):
+    return jnp.concatenate([own_rows(x), x[:HALO], x[BLOCK : BLOCK + HALO]], axis=0)
 
 
 def permutation(core, group):
@@ -97,9 +95,9 @@
 
 
 def step_kernel(
-    place, from_prev, from_next, sums, cov_hbm, obs_hbm, w_in_hbm, w_f_hbm, w_m_hbm, w_out_hbm,
-    cov_grad, send, keep,
-    pred, target, cov, obs, w_in, w_f, w_m, w_out,
+    place, from_prev, sums, cov_hbm, obs_hbm, w_in_hbm, w_f_hbm, w_m_hbm, w_out_hbm,
+    cov_grad, last_grad, back, send, keep,
+    pred, cov, obs, w_in, w_f, w_m, w_out,
     tanh_act, gate_act, dpred, cov_t, gated_t, last_t, taps_t, sems,
 ):
     cov_copy = pltpu.make_async_copy(cov_hbm, cov, sems.at[0])
@@ -115,16 +113,12 @@
     perm8 = permutation(core, 8)
 
     def turned(perm, x):
-        return mm_nt(perm, own_rows(x).astype(BF16)).astype(BF16)
+        return mm_nt(perm, arranged(x).astype(BF16)).astype(BF16)
 
     cov_copy.wait()
     pieces = []
     for b in range(SEQ):
-        pieces += [
-            from_prev[b].astype(F32),
-            cov[b].astype(F32),
-            from_next[b, :, :NODES],
-        ]
+        pieces += [from_prev[b].astype(F32), cov[b].astype(F32)]
     x = jnp.concatenate(pieces, axis=0)
     cov_t[...] = turned(perm4, x)
     w_in_copy.wait()
@@ -146,17 +140,13 @@
         gated_t[layer] = turned(perm4, gated.astype(F32))
         hidden = (wide + mm(gated, w_m[layer])).astype(BF16)
     wide = hidden.astype(F32)
-    last_t[...] = turned(perm4, wide)
-    head = jnp.concatenate([own_rows(wide), after_rows(wide)], axis=0).astype(BF16)
+    head = own_rows(wide).astype(BF16)
+    last_t[...] = mm_nt(perm4, head).astype(BF16)
     w_out_copy.wait()
     pred[...] = mm(head, w_out[...])
     obs_copy.wait()
-    for b in range(SEQ):
-        target[b * ROWS : (b + 1) * ROWS, :] = obs[b]
-        target[OWN + b * HALO : OWN + (b + 1) * HALO, :] = from_next[b, :, NODES:]
-
-    at_end = place[1]
-    steps = ROWS * place[2]
+
+    steps = ROWS * place[1]
     total = jnp.sum(sums[...], axis=0)
     inv = lax.rsqrt(total / (steps * NODES).astype(F32) + epsilon)
     inv = inv * (NODES**0.5 / (SCENARIOS * (SCENARIOS - 1) * NODES))
@@ -165,15 +155,13 @@
         halves = []
         for part in range(2):
             chunk = i * 2 + part
-            first = (chunk < ROWS // 8) | (chunk == OWN // 8)
-            beyond = (chunk >= OWN // 8) & (at_end == 1)
-            scale = jnp.where(beyond, 0.0, jnp.where(first, inv[0:1], inv[1:2]))
+            scale = jnp.where(chunk < ROWS // 8, inv[0:1], inv[1:2])
             at = pl.ds(pl.multiple_of(chunk * 8, 8), 8)
             y = [
                 (pred[at, s * NODES : s * NODES + 128], pred[at, s * NODES + 128 : (s + 1) * NODES])
                 for s in range(SCENARIOS)
             ]
-            o = (target[at, :128], target[at, 128:])
+            o = (obs[at, :128], obs[at, 128:])
             halves.append(energy_rows(y, o, scale))
         at = pl.ds(pl.multiple_of(i * 16, 16), 16)
         for s in range(SCENARIOS):
@@ -181,11 +169,11 @@
             dpred[at, s * NODES : (s + 1) * NODES] = both.astype(BF16)
         return carry
 
-    lax.fori_loop(0, ALL_HEAD // 16, step, 0)
+    lax.fori_loop(0, OWN // 16, step, 0)
 
     places = ((send, 0), (keep, 1))
     for x in range(4):
-        out_grad = mm(last_t[...], dpred[:OWN, x * 1024 : (x + 1) * 1024])
+        out_grad = mm(last_t[...], dpred[:, x * 1024 : (x + 1) * 1024])
         for ref, half in places:
             for y in range(4):
                 top = half * 128 + y * 32
@@ -193,11 +181,7 @@
     head_grad = mm_nt(dpred[...], w_out[...])
     pieces = []
     for b in range(SEQ):
-        pieces += [
-            jnp.zeros((HALO, NODES), F32),
-            head_grad[b * ROWS : (b + 1) * ROWS],
-            head_grad[OWN + b * HALO : OWN + (b + 1) * HALO],
-        ]
+        pieces += [jnp.zeros((HALO, NODES), F32), head_grad[b * ROWS : (b + 1) * ROWS]]
     grad = jnp.concatenate(pieces, axis=0).astype(BF16)
 
     def store_small(x, value):
@@ -208,7 +192,8 @@
 
     for layer in reversed(range(LAYERS)):
         grad_wide = grad.astype(F32)
-        store_small(layer, mm(gated_t[layer], own_rows(grad_wide).astype(BF16)))
+        used = OWN if layer == LAYERS - 1 else ALL_ROWS
+        store_small(layer, mm(gated_t[layer, :, :used], arranged(grad_wide)[:used].astype(BF16)))
         gated_cot = mm_nt(grad, w_m[layer]).astype(BF16).astype(F32)
         through = tanh_act[layer]
         gate = gate_act[layer]
@@ -219,10 +204,10 @@
             ],
             axis=1,
         )
-        own_preact = own_rows(grad_preact).astype(BF16)
+        used_preact = arranged(grad_preact)[:used].astype(BF16)
         grad_preact = grad_preact.astype(BF16)
         for tap in range(2):
-            tap_grad = mm(taps_t[layer, tap], own_preact)
+            tap_grad = mm(taps_t[layer, tap, :, :used], used_preact)
             for ref, half in places:
                 for y_low in range(2):
                     top = half * 128 + y_low * 64
@@ -238,11 +223,13 @@
         now = grad_joined[:, NODES:].astype(F32)
         earlier = pltpu.roll(past, ALL_ROWS - 2**layer, 0)
         grad = ((grad_wide + now).astype(BF16).astype(F32) + earlier).astype(BF16)
-    own = own_rows(grad.astype(F32)).astype(BF16)
-    store_small(3, mm(cov_t[...], own))
-    result = mm_nt(own, w_in[...]).astype(BF16)
+    wide = arranged(grad.astype(F32))
+    store_small(3, mm(cov_t[...], wide.astype(BF16)))
+    result = mm_nt(wide[:OWN].astype(BF16), w_in[...]).astype(BF16)
     for b in range(SEQ):
         cov_grad[b] = result[b * ROWS : (b + 1) * ROWS]
+        last_grad[b] = wide[(b + 1) * ROWS - EDGE : (b + 1) * ROWS].astype(BF16)
+        back[b] = wide[OWN + b * HALO : OWN + (b + 1) * HALO].astype(BF16)
 
 
 def add_kernel(keep, got, out):
@@ -268,10 +255,23 @@
     total = pieces[0].astype(F32)
     for i in range(1, pieces.shape[0]):
         total = total + pieces[i].astype(F32)
-    out[...] = total.astype(BF16)
-
-
-def finish_kernel(g, input_grad, filter_grad, mixing_grad, output_grad):
+    for x in range(out.shape[0]):
+        out[x] = total.astype(BF16)
+
+
+def finish_kernel(
+    g, last_grad, returned, w_in, cov_part, input_grad, filter_grad, mixing_grad, output_grad, cov_grad,
+    edge, sem,
+):
+    rows = []
+    for b in range(SEQ):
+        late = last_grad[b].astype(F32)
+        rows += [late[: EDGE - HALO], late[EDGE - HALO :] + returned[b].astype(F32)]
+    result = mm_nt(jnp.concatenate(rows, axis=0).astype(BF16), w_in[...]).astype(BF16)
+    for b in range(SEQ):
+        edge[b] = result[b * EDGE : (b + 1) * EDGE]
+    copy = pltpu.make_async_copy(edge, cov_grad.at[:, pl.ds(ROWS - EDGE, EDGE), :], sem)
+    copy.start()
     for x in range(4):
         v = g[x].astype(F32)
         output_grad[:, x * 1024 : x * 1024 + 512] = v[:4, :512].astype(BF16)
@@ -284,6 +284,7 @@
         for layer in range(LAYERS):
             base = 640 + layer * 128
             filter_grad[layer, :, x * 128 : (x + 1) * 128] = v[:, base : base + 128].astype(BF16)
+    copy.wait()
 
 
 HBM = pl.BlockSpec(memory_space=pltpu.HBM)
@@ -292,13 +293,16 @@
 WHOLE = pl.BlockSpec(memory_space=VMEM)
 
 
-def call(kernel, out_shape, in_specs, scratch=(), limit=16, name=None):
+def call(kernel, out_shape, in_specs, scratch=(), limit=16, name=None, out_specs=None, aliases={}):
+    if out_specs is None:
+        out_specs = jax.tree.map(lambda _: WHOLE, out_shape)
     return pl.pallas_call(
         kernel,
         out_shape=out_shape,
         in_specs=in_specs,
-        out_specs=jax.tree.map(lambda _: WHOLE, out_shape),
+        out_specs=out_specs,
         scratch_shapes=scratch,
+        input_output_aliases=aliases,
         compiler_params=pltpu.CompilerParams(vmem_limit_bytes=limit * 1024 * 1024),
         name=name,
     )
@@ -306,83 +310,82 @@
 
 def per_device(cov, obs, w_in, w_f, w_m, w_out):
     count = lax.axis_size(TM)
-    me = lax.axis_index(TM)
-    place = jnp.stack(
-        [
-            lax.axis_index("core"),
-            jnp.where(me == count - 1, 1, 0),
-            jnp.int32(count),
-        ]
-    ).astype(jnp.int32)
+    place = jnp.stack([lax.axis_index("core"), jnp.int32(count)]).astype(jnp.int32)
+    obs = obs.reshape(OWN, NODES)
     cov, obs, w_in, w_f, w_m, w_out = (
         pltpu.with_memory_space_constraint(a, pltpu.HBM) for a in (cov, obs, w_in, w_f, w_m, w_out)
     )
-    to_next, to_prev, squares = call(
+    to_next, squares = call(
         start_kernel,
-        (
-            shape((SEQ, HALO, NODES), BF16),
-            shape((SEQ, HALO, 2 * NODES), F32),
-            shape((count, SEQ, 128), F32),
-        ),
+        (shape((SEQ, HALO, NODES), BF16), shape((count, SEQ, 128), F32)),
         [HBM, HBM],
         scratch=[
-            VMEM((SEQ, 16, NODES), BF16),
-            VMEM((SEQ, 16, NODES), BF16),
+            VMEM((SEQ, EDGE, NODES), BF16),
             VMEM(obs.shape, F32),
-            pltpu.SemaphoreType.DMA((3,)),
+            pltpu.SemaphoreType.DMA((2,)),
         ],
         limit=4,
         name="start",
     )(cov, obs)
     sums = lax.all_to_all(squares, TM, 0, 0, tiled=True)
     from_prev = lax.ppermute(to_next, TM, [(i, i + 1) for i in range(count - 1)])
-    from_next = lax.ppermute(to_prev, TM, [(i + 1, i) for i in range(count - 1)])
 
     piece = shape((4, 4, 32, 2048), BF16)
-    cov_grad, send, keep = call(
+    cov_part, last_grad, back, send, keep = call(
         step_kernel,
-        (shape((SEQ, ROWS, NODES), BF16), piece, piece),
-        [SCALARS, WHOLE, WHOLE, WHOLE] + [HBM] * 6,
+        (
+            shape((SEQ, ROWS, NODES), BF16),
+            shape((SEQ, EDGE, NODES), BF16),
+            shape((SEQ, HALO, NODES), BF16),
+            piece,
+            piece,
+        ),
+        [SCALARS, WHOLE, WHOLE] + [HBM] * 6,
         scratch=[
-            VMEM((ALL_HEAD, SCENARIOS * NODES), F32),
-            VMEM((ALL_HEAD, NODES), F32),
+            VMEM((OWN, SCENARIOS * NODES), F32),
             VMEM(cov.shape, BF16),
-            VMEM(obs.shape, F32),
+            VMEM((OWN, NODES), F32),
             VMEM(w_in.shape, BF16),
             VMEM(w_f.shape, BF16),
             VMEM(w_m.shape, BF16),
             VMEM(w_out.shape, BF16),
             VMEM((LAYERS, ALL_ROWS, NODES), F32),
             VMEM((LAYERS, ALL_ROWS, NODES), F32),
-            VMEM((ALL_HEAD, SCENARIOS * NODES), BF16),
+            VMEM((OWN, SCENARIOS * NODES), BF16),
+            VMEM((NODES, ALL_ROWS), BF16),
+            VMEM((LAYERS, NODES, ALL_ROWS), BF16),
             VMEM((NODES, OWN), BF16),
-            VMEM((LAYERS, NODES, OWN), BF16),
-            VMEM((NODES, OWN), BF16),
-            VMEM((LAYERS, 2, NODES, OWN), BF16),
+            VMEM((LAYERS, 2, NODES, ALL_ROWS), BF16),
             pltpu.SemaphoreType.DMA((6,)),
         ],
         limit=44,
         name="step",
-    )(place, from_prev, from_next, sums, cov, obs, w_in, w_f, w_m, w_out)
+    )(place, from_prev, sums, cov, obs, w_in, w_f, w_m, w_out)
     got = lax.ppermute(send, "core", [(0, 1), (1, 0)])
+    returned = lax.ppermute(back, TM, [(i + 1, i) for i in range(count - 1)])
     chip = call(add_kernel, piece, [WHOLE] * 2, limit=4, name="pair")(keep, got)
     plane = lax.all_to_all(chip.reshape(16, 32, 2048), ("x", "y"), 0, 0, tiled=True)
     by_z = call(plane_kernel, shape((8, 8, 1024), BF16), [WHOLE], limit=4, name="plane")(plane)
     line = lax.all_to_all(by_z, "z", 0, 0, tiled=True)
-    mine = call(line_kernel, shape((8, 1024), BF16), [WHOLE], limit=4, name="line")(line)
-    whole = lax.all_gather(mine, "x")
-    input_grad, filter_grad, mixing_grad, output_grad = call(
+    mine = call(line_kernel, shape((4, 8, 1024), BF16), [WHOLE], limit=4, name="line")(line)
+    whole = lax.all_to_all(mine, "x", 0, 0, tiled=True)
+    cov_part = pltpu.with_memory_space_constraint(cov_part, pltpu.HBM)
+    input_grad, filter_grad, mixing_grad, output_grad, cov_grad = call(
         finish_kernel,
         (
             shape((4, NODES), BF16),
             shape((LAYERS, 8, 2 * NODES), BF16),
             shape((LAYERS, 4, NODES), BF16),
             shape((4, SCENARIOS * NODES), BF16),
+            pltpu.HBM((SEQ, ROWS, NODES), BF16),
         ),
-        [WHOLE],
+        [WHOLE, WHOLE, WHOLE, WHOLE, HBM],
+        scratch=[VMEM((SEQ, EDGE, NODES), BF16), pltpu.SemaphoreType.DMA],
         limit=4,
         name="finish",
-    )(whole)
+        out_specs=(WHOLE, WHOLE, WHOLE, WHOLE, HBM),
+        aliases={4: 4},
+    )(whole, last_grad, returned, w_in, cov_part)
     return (cov_grad, input_grad, filter_grad, mixing_grad, output_grad)
 
 

time: 110 us -> 107 us (0.973)
  blocking collectives: 61.5 us -> 47.4 us
  waiting for transfers between devices: 5.64 us -> 14.4 us
  Pallas kernels: 21.4 us -> 23.8 us
    all_gather x1 -> x0, blocking collectives: 11.9 us -> none  [per_device(): whole = lax.all_gather(mine, 'x')]
    ppermute x1, waiting for transfers between devices: 0.01 us -> 4.94 us  [per_device(): lax.ppermute(to_next, TM, [(i, i + 1) for i in range(count - 1)])]
    ppermute x1, starting transfers between devices: 5.61 us -> 1.92 us  [per_device(): returned = lax.ppermute(back, TM, [(i + 1, i) for i in range(count - 1)])]
    all_to_all x0 -> x1, starting transfers between devices: none -> 3.28 us  [per_device(): whole = lax.all_to_all(mine, 'x', 0, 0, tiled=True)]
    all_to_all x0 -> x1, waiting for transfers between devices: none -> 2.32 us  [per_device(): whole = lax.all_to_all(mine, 'x', 0, 0, tiled=True)]
    all_to_all x1, waiting for transfers between devices: 0.01 us -> 1.73 us  [per_device(): sums = lax.all_to_all(squares, TM, 0, 0, tiled=True)]
    pallas_call x1, Pallas kernels: 0.63 us -> 2.34 us  [per_device(): call(finish_kernel, (shape((4, NODES), BF16), shape((LAYERS, 8, 2 * NODES...]
    all_to_all x1, blocking collectives: 15.2 us -> 13.8 us  [per_device(): line = lax.all_to_all(by_z, 'z', 0, 0, tiled=True)]
  transfers between devices with their start and end apart: 4 -> 5, of which waited for: 2 -> 5; matrix products, arithmetic and copies ran while one was open for 0% -> 0% of each run, Pallas kernels for 0% -> 0%
where the time goes in v5:
time: 107 us; the launch traced here: 106 us
  blocking collectives  47.4 us (44%)
  Pallas kernels  23.8 us (22%)
  starting transfers between devices  19.6 us (18%)
  waiting for transfers between devices  14.4 us (13%)
    all_to_all x1, blocking collectives, per_device(): lax.all_to_all(chip.reshape(16, 32, 2048), ('x', 'y'), 0, 0, tiled=True)  33.6 us
    pallas_call x1, Pallas kernels, per_device(): call(step_kernel, (shape((SEQ, ROWS, NODES), BF16), shape((SEQ, EDGE, NOD...  18.6 us
    all_to_all x1, blocking collectives, per_device(): line = lax.all_to_all(by_z, 'z', 0, 0, tiled=True)  13.8 us
    all_to_all x1, starting transfers between devices, per_device(): sums = lax.all_to_all(squares, TM, 0, 0, tiled=True)  12.1 us
    ppermute x1, waiting for transfers between devices, per_device(): lax.ppermute(to_next, TM, [(i, i + 1) for i in range(count - 1)])  4.94 us
    ppermute x1, waiting for transfers between devices, per_device(): got = lax.ppermute(send, 'core', [(0, 1), (1, 0)])  4.05 us
    all_to_all x1, starting transfers between devices, per_device(): whole = lax.all_to_all(mine, 'x', 0, 0, tiled=True)  3.28 us
    pallas_call x1, Pallas kernels, per_device(): call(finish_kernel, (shape((4, NODES), BF16), shape((LAYERS, 8, 2 * NODES...  2.34 us
  transfers between devices with their start and end apart: 5, of which 5 were waited for; matrix products, arithmetic and copies ran while one was open for 0% of the time, Pallas kernels for 0%

profile of v5, /device:TPU:8, one launch (start us, length us, event | category | flops | bytes accessed | tf_op | source)
XLA Modules:
  0.0 105.9 jit_solution(7859688113067316614)
XLA Ops:
  0.6 1.7 %start.1 = (bf16[2,8,256]{2,1,0:T(8,128)(2,1)S(1)}, f32[64,2,128]{2,1,0:T(2,128)}) custom-call(bf16[2,128,256]{2,1,0:T(8,128)(2,1)} %cov_hbm.3, f32[256,256]{1,0:T(8,128)} %bitcast.4), custom_call_target="tpu_custom_call" | custom-call | tf_op jit(solution)/shard_map/start/pallas_call | solution.py:318
  2.4 12.1 %all-to-all-start = ((f32[64,2,128]{2,1,0:T(2,128)}), f32[64,2,128]{2,1,0:T(2,128)S(1)}, u32[]{:S(2)}, u32[]{:S(2)}) async-start(f32[64,2,128]{2,1,0:T(2,128)} %get-tuple-element.18), calls=%async_computation | async-start | bytes 131072 | tf_op jit(solution)/shard_map/all_to_all | solution.py:330
  14.5 2.1 %collective-permute-start = (bf16[2,8,256]{2,1,0:T(8,128)(2,1)S(1)}, bf16[2,8,256]{2,1,0:T(8,128)(2,1)S(1)}, u32[]{:S(2)}, u32[]{:S(2)}) collective-permute-start(bf16[2,8,256]{2,1,0:T(8,128)(2,1)S(1)} %get-tuple-element.17), channel_id=1, source_target_pairs={{0,4},{4,8},{8,12},{12,16},{16,20},{20,24},{24,28},{28,32},{32,36}... | collective-permute-start | bytes 24584 | tf_op jit(solution)/shard_map/ppermute | solution.py:331
  16.6 0.1 pad_add_fusion.place
  16.6 4.9 %collective-permute-done.from_prev = bf16[2,8,256]{2,1,0:T(8,128)(2,1)S(1)} collective-permute-done((bf16[2,8,256]{2,1,0:T(8,128)(2,1)S(1)}, bf16[2,8,256]{2,1,0:T(8,128)(2,1)S(1)}, u32[]{:S(2)}, u32[]{:S(2)}) %collective-permute-start) | collective-permute-done | bytes 8224 | tf_op jit(solution)/shard_map/ppermute | solution.py:331
  21.6 1.7 %all-to-all-done.sums = f32[64,2,128]{2,1,0:T(2,128)S(1)} async-done(((f32[64,2,128]{2,1,0:T(2,128)}), f32[64,2,128]{2,1,0:T(2,128)S(1)}, u32[]{:S(2)}, u32[]{:S(2)}) %all-to-all-start) | async-done | bytes 65568 | tf_op jit(solution)/shard_map/all_to_all | solution.py:330
  23.3 18.6 %step.1 = (bf16[2,128,256]{2,1,0:T(8,128)(2,1)}, bf16[2,16,256]{2,1,0:T(8,128)(2,1)S(1)}, bf16[2,8,256]{2,1,0:T(8,128)(2,1)S(1)}, bf16[4,4,32,2048]{3,2,1,0:T(8,128)(2,1)S(1)}, bf16[4,4,32,2048]{3,2,1,0:T(8,128)(2,1)S(1)}) custom-call(s32[2]{0:T(128)S(1)} %pad_add_fusion.place, bf16[2,8,256]{2,1,0:T(8,128)(2,1)S(1)} %collective-permute-done.from_prev, ...), custom_call_target="tpu_custom_call" | custom-call | tf_op jit(solution)/shard_map/step/pallas_call | solution.py:334
  41.9 0.2 collective-permute-start.1
  42.1 4.1 %collective-permute-done.1.got = bf16[4,4,32,2048]{3,2,1,0:T(8,128)(2,1)S(1)} collective-permute-done((bf16[4,4,32,2048]{3,2,1,0:T(8,128)(2,1)S(1)}, bf16[4,4,32,2048]{3,2,1,0:T(8,128)(2,1)S(1)}, u32[]{:S(2)}, u32[]{:S(2)}) %collective-permute-start.1) | collective-permute-done | bytes 2097184 | tf_op jit(solution)/shard_map/ppermute | solution.py:364
  46.2 0.2 pair.1
  46.4 33.6 %all_to_all.20.pieces = bf16[16,32,2048]{2,1,0:T(8,128)(2,1)S(1)} all-to-all(bf16[16,32,2048]{2,1,0:T(8,128)(2,1)S(1)} %bitcast.3), channel_id=1, replica_groups=mesh['y'=4,'z'=8,'core'=2,'x'=4] {'x','y'}, dimensions={0} | all-to-all | bytes 4194304 | tf_op jit(solution)/shard_map/all_to_all | solution.py:367
  80.0 0.3 plane.1
  80.3 13.8 %all_to_all.21.pieces = bf16[8,8,1024]{2,1,0:T(8,128)(2,1)S(1)} all-to-all(bf16[8,8,1024]{2,1,0:T(8,128)(2,1)S(1)} %plane.1), channel_id=1, replica_groups=mesh['y'=4,'z'=8,'core'=2,'x'=4] {'z'}, dimensions={0} | all-to-all | bytes 262144 | tf_op jit(solution)/shard_map/all_to_all | solution.py:369
  94.0 0.6 line.1
  94.7 3.3 %all-to-all-start.3 = ((bf16[4,8,1024]{2,1,0:T(8,128)(2,1)}), bf16[4,8,1024]{2,1,0:T(8,128)(2,1)S(1)}, u32[]{:S(2)}, u32[]{:S(2)}) async-start(bf16[4,8,1024]{2,1,0:T(8,128)(2,1)} %line.1), calls=%async_computation.3 | async-start | bytes 131072 | tf_op jit(solution)/shard_map/all_to_all | solution.py:371
  98.0 1.9 %collective-permute-start.2 = (bf16[2,8,256]{2,1,0:T(8,128)(2,1)S(1)}, bf16[2,8,256]{2,1,0:T(8,128)(2,1)S(1)}, u32[]{:S(2)}, u32[]{:S(2)}) collective-permute-start(bf16[2,8,256]{2,1,0:T(8,128)(2,1)S(1)} %get-tuple-element.22), channel_id=1, source_target_pairs={{4,0},{8,4},{12,8},{16,12},{20,16},{24,20},{28,24},{32,28},{36,32}... | collective-permute-start | bytes 24584 | tf_op jit(solution)/shard_map/ppermute | solution.py:365
  99.9 1.3 %collective-permute-done.2.returned = bf16[2,8,256]{2,1,0:T(8,128)(2,1)S(1)} collective-permute-done((bf16[2,8,256]{2,1,0:T(8,128)(2,1)S(1)}, bf16[2,8,256]{2,1,0:T(8,128)(2,1)S(1)}, u32[]{:S(2)}, u32[]{:S(2)}) %collective-permute-start.2) | collective-permute-done | bytes 8224 | tf_op jit(solution)/shard_map/ppermute | solution.py:365
  101.2 2.3 %all-to-all-done.3.g = bf16[4,8,1024]{2,1,0:T(8,128)(2,1)S(1)} async-done(((bf16[4,8,1024]{2,1,0:T(8,128)(2,1)}), bf16[4,8,1024]{2,1,0:T(8,128)(2,1)S(1)}, u32[]{:S(2)}, u32[]{:S(2)}) %all-to-all-start.3) | async-done | bytes 65568 | tf_op jit(solution)/shard_map/all_to_all | solution.py:371
  103.6 2.3 %finish.1 = (bf16[4,256]{1,0:T(4,128)(2,1)}, bf16[3,8,512]{2,1,0:T(8,128)(2,1)}, bf16[3,4,256]{2,1,0:T(4,128)(2,1)}, bf16[4,4096]{1,0:T(4,128)(2,1)}, bf16[2,128,256]{2,1,0:T(8,128)(2,1)}) custom-call(bf16[4,8,1024]{2,1,0:T(8,128)(2,1)S(1)} %all-to-all-done.3.g, ...), custom_call_target="tpu_custom_call", output_to_operand_aliasing={{4}: (4, {})} | custom-call | tf_op jit(solution)/shard_map/finish/pallas_call | solution.py:373
Async XLA Ops:
  2.4 20.9 %all-to-all-start = ((f32[64,2,128]{2,1,0:T(2,128)}), f32[64,2,128]{2,1,0:T(2,128)S(1)}, u32[]{:S(2)}, u32[]{:S(2)}) async-start(f32[64,2,128]{2,1,0:T(2,128)} %get-tuple-element.18), calls=%async_computation | async-start | bytes 131072 | tf_op jit(solution)/shard_map/all_to_all | solution.py:330
  14.5 7.1 %collective-permute-start = (bf16[2,8,256]{2,1,0:T(8,128)(2,1)S(1)}, bf16[2,8,256]{2,1,0:T(8,128)(2,1)S(1)}, u32[]{:S(2)}, u32[]{:S(2)}) collective-permute-start(bf16[2,8,256]{2,1,0:T(8,128)(2,1)S(1)} %get-tuple-element.17), channel_id=1, source_target_pairs={{0,4},{4,8},{8,12},{12,16},{16,20},{20,24},{24,28},{28,32},{32,36}... | collective-permute-start | bytes 24584 | tf_op jit(solution)/shard_map/ppermute | solution.py:331
  41.9 4.2 %collective-permute-start.1 = (bf16[4,4,32,2048]{3,2,1,0:T(8,128)(2,1)S(1)}, bf16[4,4,32,2048]{3,2,1,0:T(8,128)(2,1)S(1)}, u32[]{:S(2)}, u32[]{:S(2)}) collective-permute-start(bf16[4,4,32,2048]{3,2,1,0:T(8,128)(2,1)S(1)} %get-tuple-element.20), channel_id=1, source_target_pairs={{0,4},{4,0},{1,5},{5,1},{2,6},{6,2},{3,7},{7,3},{8,12},{12,8},{9,1... | collective-permute-start | bytes 6291464 | tf_op jit(solution)/shard_map/ppermute | solution.py:364
  94.7 8.9 %all-to-all-start.3 = ((bf16[4,8,1024]{2,1,0:T(8,128)(2,1)}), bf16[4,8,1024]{2,1,0:T(8,128)(2,1)S(1)}, u32[]{:S(2)}, u32[]{:S(2)}) async-start(bf16[4,8,1024]{2,1,0:T(8,128)(2,1)} %line.1), calls=%async_computation.3 | async-start | bytes 131072 | tf_op jit(solution)/shard_map/all_to_all | solution.py:371
  98.0 3.3 %collective-permute-start.2 = (bf16[2,8,256]{2,1,0:T(8,128)(2,1)S(1)}, bf16[2,8,256]{2,1,0:T(8,128)(2,1)S(1)}, u32[]{:S(2)}, u32[]{:S(2)}) collective-permute-start(bf16[2,8,256]{2,1,0:T(8,128)(2,1)S(1)} %get-tuple-element.22), channel_id=1, source_target_pairs={{4,0},{8,4},{12,8},{16,12},{20,16},{24,20},{28,24},{32,28},{36,32}... | collective-permute-start | bytes 24584 | tf_op jit(solution)/shard_map/ppermute | solution.py:365

commit v6 on v5

--- a/solution.py
+++ b/solution.py
@@ -232,8 +232,18 @@
         back[b] = wide[OWN + b * HALO : OWN + (b + 1) * HALO].astype(BF16)
 
 
-def add_kernel(keep, got, out):
+def pair_kernel(keep, got, last_grad, returned, w_in, cov_part, out, cov_grad, edge, sem):
+    rows = []
+    for b in range(SEQ):
+        late = last_grad[b].astype(F32)
+        rows += [late[: EDGE - HALO], late[EDGE - HALO :] + returned[b].astype(F32)]
+    result = mm_nt(jnp.concatenate(rows, axis=0).astype(BF16), w_in[...]).astype(BF16)
+    for b in range(SEQ):
+        edge[b] = result[b * EDGE : (b + 1) * EDGE]
+    copy = pltpu.make_async_copy(edge, cov_grad.at[:, pl.ds(ROWS - EDGE, EDGE), :], sem)
+    copy.start()
     out[...] = keep[...] + got[...]
+    copy.wait()
 
 
 def plane_kernel(pieces, out):
@@ -259,19 +269,7 @@
         out[x] = total.astype(BF16)
 
 
-def finish_kernel(
-    g, last_grad, returned, w_in, cov_part, input_grad, filter_grad, mixing_grad, output_grad, cov_grad,
-    edge, sem,
-):
-    rows = []
-    for b in range(SEQ):
-        late = last_grad[b].astype(F32)
-        rows += [late[: EDGE - HALO], late[EDGE - HALO :] + returned[b].astype(F32)]
-    result = mm_nt(jnp.concatenate(rows, axis=0).astype(BF16), w_in[...]).astype(BF16)
-    for b in range(SEQ):
-        edge[b] = result[b * EDGE : (b + 1) * EDGE]
-    copy = pltpu.make_async_copy(edge, cov_grad.at[:, pl.ds(ROWS - EDGE, EDGE), :], sem)
-    copy.start()
+def finish_kernel(g, input_grad, filter_grad, mixing_grad, output_grad):
     for x in range(4):
         v = g[x].astype(F32)
         output_grad[:, x * 1024 : x * 1024 + 512] = v[:4, :512].astype(BF16)
@@ -284,7 +282,6 @@
         for layer in range(LAYERS):
             base = 640 + layer * 128
             filter_grad[layer, :, x * 128 : (x + 1) * 128] = v[:, base : base + 128].astype(BF16)
-    copy.wait()
 
 
 HBM = pl.BlockSpec(memory_space=pltpu.HBM)
@@ -363,29 +360,34 @@
     )(place, from_prev, sums, cov, obs, w_in, w_f, w_m, w_out)
     got = lax.ppermute(send, "core", [(0, 1), (1, 0)])
     returned = lax.ppermute(back, TM, [(i + 1, i) for i in range(count - 1)])
-    chip = call(add_kernel, piece, [WHOLE] * 2, limit=4, name="pair")(keep, got)
+    cov_part = pltpu.with_memory_space_constraint(cov_part, pltpu.HBM)
+    chip, cov_grad = call(
+        pair_kernel,
+        (piece, pltpu.HBM((SEQ, ROWS, NODES), BF16)),
+        [WHOLE] * 5 + [HBM],
+        scratch=[VMEM((SEQ, EDGE, NODES), BF16), pltpu.SemaphoreType.DMA],
+        limit=4,
+        name="pair",
+        out_specs=(WHOLE, HBM),
+        aliases={5: 1},
+    )(keep, got, last_grad, returned, w_in, cov_part)
     plane = lax.all_to_all(chip.reshape(16, 32, 2048), ("x", "y"), 0, 0, tiled=True)
     by_z = call(plane_kernel, shape((8, 8, 1024), BF16), [WHOLE], limit=4, name="plane")(plane)
     line = lax.all_to_all(by_z, "z", 0, 0, tiled=True)
     mine = call(line_kernel, shape((4, 8, 1024), BF16), [WHOLE], limit=4, name="line")(line)
     whole = lax.all_to_all(mine, "x", 0, 0, tiled=True)
-    cov_part = pltpu.with_memory_space_constraint(cov_part, pltpu.HBM)
-    input_grad, filter_grad, mixing_grad, output_grad, cov_grad = call(
+    input_grad, filter_grad, mixing_grad, output_grad = call(
         finish_kernel,
         (
             shape((4, NODES), BF16),
             shape((LAYERS, 8, 2 * NODES), BF16),
             shape((LAYERS, 4, NODES), BF16),
             shape((4, SCENARIOS * NODES), BF16),
-            pltpu.HBM((SEQ, ROWS, NODES), BF16),
         ),
-        [WHOLE, WHOLE, WHOLE, WHOLE, HBM],
-        scratch=[VMEM((SEQ, EDGE, NODES), BF16), pltpu.SemaphoreType.DMA],
+        [WHOLE],
         limit=4,
         name="finish",
-        out_specs=(WHOLE, WHOLE, WHOLE, WHOLE, HBM),
-        aliases={4: 4},
-    )(whole, last_grad, returned, w_in, cov_part)
+    )(whole)
     return (cov_grad, input_grad, filter_grad, mixing_grad, output_grad)
 
 

time: 107 us -> 106 us (level)
  blocking collectives: 47.4 us -> 56 us
  waiting for transfers between devices: 14.4 us -> 8.02 us
  starting transfers between devices: 19.6 us -> 17.7 us
    all_to_all x0 -> x1, blocking collectives: none -> 8.85 us  [per_device(): whole = lax.all_to_all(mine, 'x', 0, 0, tiled=True)]
    ppermute x1, waiting for transfers between devices: 4.05 us -> 0.01 us  [per_device(): got = lax.ppermute(send, 'core', [(0, 1), (1, 0)])]
    all_to_all x1 -> x0, starting transfers between devices: 3.28 us -> none  [per_device(): whole = lax.all_to_all(mine, 'x', 0, 0, tiled=True)]
    all_to_all x1 -> x0, waiting for transfers between devices: 2.32 us -> none  [per_device(): whole = lax.all_to_all(mine, 'x', 0, 0, tiled=True)]
    pallas_call x1, Pallas kernels: 0.21 us -> 1.96 us  [per_device(): call(pair_kernel, (piece, pltpu.HBM((SEQ, ROWS, NODES), BF16)), [WHOLE] *...]
    pallas_call x1, Pallas kernels: 2.34 us -> 0.63 us  [per_device(): call(finish_kernel, (shape((4, NODES), BF16), shape((LAYERS, 8, 2 * NODES...]
    ppermute x1, starting transfers between devices: 1.92 us -> 3.31 us  [per_device(): returned = lax.ppermute(back, TM, [(i + 1, i) for i in range(count - 1)])]
  transfers between devices with their start and end apart: 5 -> 4, of which waited for: 5 -> 3; matrix products, arithmetic and copies ran while one was open for 0% -> 0% of each run, Pallas kernels for 0% -> 0%
where the time goes in v6:
time: 106 us
  blocking collectives  56 us (53%)
  Pallas kernels  23.2 us (22%)
  starting transfers between devices  17.7 us (17%)
  waiting for transfers between devices  8.02 us (8%)
    all_to_all x1, blocking collectives, per_device(): lax.all_to_all(chip.reshape(16, 32, 2048), ('x', 'y'), 0, 0, tiled=True)  34.2 us
    pallas_call x1, Pallas kernels, per_device(): call(step_kernel, (shape((SEQ, ROWS, NODES), BF16), shape((SEQ, EDGE, NOD...  18.6 us
    all_to_all x1, blocking collectives, per_device(): line = lax.all_to_all(by_z, 'z', 0, 0, tiled=True)  13 us
    all_to_all x1, starting transfers between devices, per_device(): sums = lax.all_to_all(squares, TM, 0, 0, tiled=True)  12.1 us
    all_to_all x1, blocking collectives, per_device(): whole = lax.all_to_all(mine, 'x', 0, 0, tiled=True)  8.85 us
    ppermute x1, waiting for transfers between devices, per_device(): lax.ppermute(to_next, TM, [(i, i + 1) for i in range(count - 1)])  4.94 us
    ppermute x1, starting transfers between devices, per_device(): returned = lax.ppermute(back, TM, [(i + 1, i) for i in range(count - 1)])  3.31 us
  transfers between devices with their start and end apart: 4, of which 3 were waited for; matrix products, arithmetic and copies ran while one was open for 0% of the time, Pallas kernels for 0%

profile of v6, /device:TPU:8, one launch (start us, length us, event | category | flops | bytes accessed | tf_op | source)
XLA Modules:
  0.0 105.7 jit_solution(3596244650025781423)
XLA Ops:
  0.6 1.7 %start.1 = (bf16[2,8,256]{2,1,0:T(8,128)(2,1)S(1)}, f32[64,2,128]{2,1,0:T(2,128)}) custom-call(bf16[2,128,256]{2,1,0:T(8,128)(2,1)} %cov_hbm.3, f32[256,256]{1,0:T(8,128)} %bitcast.4), custom_call_target="tpu_custom_call" | custom-call | tf_op jit(solution)/shard_map/start/pallas_call | solution.py:315
  2.4 12.1 %all-to-all-start = ((f32[64,2,128]{2,1,0:T(2,128)}), f32[64,2,128]{2,1,0:T(2,128)S(1)}, u32[]{:S(2)}, u32[]{:S(2)}) async-start(f32[64,2,128]{2,1,0:T(2,128)} %get-tuple-element.19), calls=%async_computation | async-start | bytes 131072 | tf_op jit(solution)/shard_map/all_to_all | solution.py:327
  14.5 2.1 %collective-permute-start = (bf16[2,8,256]{2,1,0:T(8,128)(2,1)S(1)}, bf16[2,8,256]{2,1,0:T(8,128)(2,1)S(1)}, u32[]{:S(2)}, u32[]{:S(2)}) collective-permute-start(bf16[2,8,256]{2,1,0:T(8,128)(2,1)S(1)} %get-tuple-element.18), channel_id=1, source_target_pairs={{0,4},{4,8},{8,12},{12,16},{16,20},{20,24},{24,28},{28,32},{32,36}... | collective-permute-start | bytes 24584 | tf_op jit(solution)/shard_map/ppermute | solution.py:328
  16.6 0.1 pad_add_fusion.place
  16.6 4.9 %collective-permute-done.from_prev = bf16[2,8,256]{2,1,0:T(8,128)(2,1)S(1)} collective-permute-done((bf16[2,8,256]{2,1,0:T(8,128)(2,1)S(1)}, bf16[2,8,256]{2,1,0:T(8,128)(2,1)S(1)}, u32[]{:S(2)}, u32[]{:S(2)}) %collective-permute-start) | collective-permute-done | bytes 8224 | tf_op jit(solution)/shard_map/ppermute | solution.py:328
  21.6 1.7 %all-to-all-done.sums = f32[64,2,128]{2,1,0:T(2,128)S(1)} async-done(((f32[64,2,128]{2,1,0:T(2,128)}), f32[64,2,128]{2,1,0:T(2,128)S(1)}, u32[]{:S(2)}, u32[]{:S(2)}) %all-to-all-start) | async-done | bytes 65568 | tf_op jit(solution)/shard_map/all_to_all | solution.py:327
  23.3 18.6 %step.1 = (bf16[2,128,256]{2,1,0:T(8,128)(2,1)}, bf16[2,16,256]{2,1,0:T(8,128)(2,1)S(1)}, bf16[2,8,256]{2,1,0:T(8,128)(2,1)S(1)}, bf16[4,4,32,2048]{3,2,1,0:T(8,128)(2,1)S(1)}, bf16[4,4,32,2048]{3,2,1,0:T(8,128)(2,1)S(1)}) custom-call(s32[2]{0:T(128)S(1)} %pad_add_fusion.place, bf16[2,8,256]{2,1,0:T(8,128)(2,1)S(1)} %collective-permute-done.from_prev, ...), custom_call_target="tpu_custom_call" | custom-call | tf_op jit(solution)/shard_map/step/pallas_call | solution.py:331
  41.9 0.2 collective-permute-start.1
  42.1 3.3 %collective-permute-start.2 = (bf16[2,8,256]{2,1,0:T(8,128)(2,1)S(1)}, bf16[2,8,256]{2,1,0:T(8,128)(2,1)S(1)}, u32[]{:S(2)}, u32[]{:S(2)}) collective-permute-start(bf16[2,8,256]{2,1,0:T(8,128)(2,1)S(1)} %get-tuple-element.23), channel_id=1, source_target_pairs={{4,0},{8,4},{12,8},{16,12},{20,16},{24,20},{28,24},{32,28},{36,32}... | collective-permute-start | bytes 24584 | tf_op jit(solution)/shard_map/ppermute | solution.py:362
  45.4 1.3 %collective-permute-done.2.returned = bf16[2,8,256]{2,1,0:T(8,128)(2,1)S(1)} collective-permute-done((bf16[2,8,256]{2,1,0:T(8,128)(2,1)S(1)}, bf16[2,8,256]{2,1,0:T(8,128)(2,1)S(1)}, u32[]{:S(2)}, u32[]{:S(2)}) %collective-permute-start.2) | collective-permute-done | bytes 8224 | tf_op jit(solution)/shard_map/ppermute | solution.py:362
  46.8 0.0 collective-permute-done.1.got
  46.8 2.0 %pair.1 = (bf16[4,4,32,2048]{3,2,1,0:T(8,128)(2,1)S(1)}, bf16[2,128,256]{2,1,0:T(8,128)(2,1)}) custom-call(bf16[4,4,32,2048]{3,2,1,0:T(8,128)(2,1)S(1)} %get-tuple-element.20.keep, bf16[4,4,32,2048]{3,2,1,0:T(8,128)(2,1)S(1)} %collective-permute-done.1.got, bf16[2,16,256]{2,1,0:T(8,128)(2,1)S(1)} %get-tuple-element.22.last_grad, ...), custom_call_target="tpu_custom_call", output_to_operand_aliasing={{1}: (5, {})} | custom-call | tf_op jit(solution)/shard_map/pair/pallas_call | solution.py:364
  48.7 34.2 %all_to_all.20.pieces = bf16[16,32,2048]{2,1,0:T(8,128)(2,1)S(1)} all-to-all(bf16[16,32,2048]{2,1,0:T(8,128)(2,1)S(1)} %bitcast.3), channel_id=1, replica_groups=mesh['y'=4,'z'=8,'core'=2,'x'=4] {'x','y'}, dimensions={0} | all-to-all | bytes 4194304 | tf_op jit(solution)/shard_map/all_to_all | solution.py:374
  82.9 0.3 plane.1
  83.2 13.0 %all_to_all.21.pieces = bf16[8,8,1024]{2,1,0:T(8,128)(2,1)S(1)} all-to-all(bf16[8,8,1024]{2,1,0:T(8,128)(2,1)S(1)} %plane.1), channel_id=1, replica_groups=mesh['y'=4,'z'=8,'core'=2,'x'=4] {'z'}, dimensions={0} | all-to-all | bytes 262144 | tf_op jit(solution)/shard_map/all_to_all | solution.py:376
  96.2 8.9 %all_to_all.22.g = bf16[4,8,1024]{2,1,0:T(8,128)(2,1)S(1)} all-to-all(bf16[4,8,1024]{2,1,0:T(8,128)(2,1)S(1)} %line.1), channel_id=1, replica_groups=mesh['y'=4,'z'=8,'core'=2,'x'=4] {'x'}, dimensions={0} | all-to-all | bytes 131072 | tf_op jit(solution)/shard_map/all_to_all | solution.py:378
  105.1 0.6 finish.1
  (1 shorter events, 0.0 us)
Async XLA Ops:
  2.4 20.9 %all-to-all-start = ((f32[64,2,128]{2,1,0:T(2,128)}), f32[64,2,128]{2,1,0:T(2,128)S(1)}, u32[]{:S(2)}, u32[]{:S(2)}) async-start(f32[64,2,128]{2,1,0:T(2,128)} %get-tuple-element.19), calls=%async_computation | async-start | bytes 131072 | tf_op jit(solution)/shard_map/all_to_all | solution.py:327
  14.5 7.1 %collective-permute-start = (bf16[2,8,256]{2,1,0:T(8,128)(2,1)S(1)}, bf16[2,8,256]{2,1,0:T(8,128)(2,1)S(1)}, u32[]{:S(2)}, u32[]{:S(2)}) collective-permute-start(bf16[2,8,256]{2,1,0:T(8,128)(2,1)S(1)} %get-tuple-element.18), channel_id=1, source_target_pairs={{0,4},{4,8},{8,12},{12,16},{16,20},{20,24},{24,28},{28,32},{32,36}... | collective-permute-start | bytes 24584 | tf_op jit(solution)/shard_map/ppermute | solution.py:328
  41.9 4.9 %collective-permute-start.1 = (bf16[4,4,32,2048]{3,2,1,0:T(8,128)(2,1)S(1)}, bf16[4,4,32,2048]{3,2,1,0:T(8,128)(2,1)S(1)}, u32[]{:S(2)}, u32[]{:S(2)}) collective-permute-start(bf16[4,4,32,2048]{3,2,1,0:T(8,128)(2,1)S(1)} %get-tuple-element.21), channel_id=1, source_target_pairs={{0,4},{4,0},{1,5},{5,1},{2,6},{6,2},{3,7},{7,3},{8,12},{12,8},{9,1... | collective-permute-start | bytes 6291464 | tf_op jit(solution)/shard_map/ppermute | solution.py:361
  42.1 4.7 %collective-permute-start.2 = (bf16[2,8,256]{2,1,0:T(8,128)(2,1)S(1)}, bf16[2,8,256]{2,1,0:T(8,128)(2,1)S(1)}, u32[]{:S(2)}, u32[]{:S(2)}) collective-permute-start(bf16[2,8,256]{2,1,0:T(8,128)(2,1)S(1)} %get-tuple-element.23), channel_id=1, source_target_pairs={{4,0},{8,4},{12,8},{16,12},{20,16},{24,20},{28,24},{32,28},{36,32}... | collective-permute-start | bytes 24584 | tf_op jit(solution)/shard_map/ppermute | solution.py:362

commit v7 on v4

--- a/solution.py
+++ b/solution.py
@@ -36,7 +36,7 @@
     return jax.ShapeDtypeStruct(dims, dtype)
 
 
-def start_kernel(cov_hbm, obs_hbm, to_next, to_prev, squares, tail, head, obs, sems):
+def start_kernel(place, cov_hbm, obs_hbm, to_pair, to_far, squares, tail, head, obs, sems):
     copies = [
         pltpu.make_async_copy(obs_hbm, obs, sems.at[0]),
         pltpu.make_async_copy(cov_hbm.at[:, pl.ds(ROWS - 16, 16), :], tail, sems.at[1]),
@@ -46,10 +46,12 @@
         copy.start()
     for copy in copies:
         copy.wait()
+    first_core = place[0] == 0
     for b in range(SEQ):
-        to_next[b] = tail[b].astype(F32)[16 - HALO :].astype(BF16)
-        to_prev[b, :, :NODES] = head[b].astype(F32)[:HALO]
-        to_prev[b, :, NODES:] = obs[b, :HALO, :]
+        late = jnp.concatenate([tail[b].astype(F32)[16 - HALO :], obs[b, ROWS - HALO :, :]], axis=1)
+        early = jnp.concatenate([head[b].astype(F32)[:HALO], obs[b, :HALO, :]], axis=1)
+        to_pair[b] = jnp.where(first_core, late, early)
+        to_far[b] = jnp.where(first_core, early, late)
         sq = obs[b] * obs[b]
         by_lane = jnp.sum(sq, axis=0, keepdims=True)
         total = jnp.sum(by_lane, axis=1, keepdims=True)
@@ -97,7 +99,7 @@
 
 
 def step_kernel(
-    place, from_prev, from_next, sums, cov_hbm, obs_hbm, w_in_hbm, w_f_hbm, w_m_hbm, w_out_hbm,
+    place, from_pair, from_far, sums, cov_hbm, obs_hbm, w_in_hbm, w_f_hbm, w_m_hbm, w_out_hbm,
     cov_grad, send, keep,
     pred, target, cov, obs, w_in, w_f, w_m, w_out,
     tanh_act, gate_act, dpred, cov_t, gated_t, last_t, taps_t, sems,
@@ -118,13 +120,12 @@
         return mm_nt(perm, own_rows(x).astype(BF16)).astype(BF16)
 
     cov_copy.wait()
+    first_core = core == 0
     pieces = []
     for b in range(SEQ):
-        pieces += [
-            from_prev[b].astype(F32),
-            cov[b].astype(F32),
-            from_next[b, :, :NODES],
-        ]
+        before = jnp.where(first_core, from_far[b, :, :NODES], from_pair[b, :, :NODES])
+        after = jnp.where(first_core, from_pair[b, :, :NODES], from_far[b, :, :NODES])
+        pieces += [before, cov[b].astype(F32), after]
     x = jnp.concatenate(pieces, axis=0)
     cov_t[...] = turned(perm4, x)
     w_in_copy.wait()
@@ -153,7 +154,9 @@
     obs_copy.wait()
     for b in range(SEQ):
         target[b * ROWS : (b + 1) * ROWS, :] = obs[b]
-        target[OWN + b * HALO : OWN + (b + 1) * HALO, :] = from_next[b, :, NODES:]
+        target[OWN + b * HALO : OWN + (b + 1) * HALO, :] = jnp.where(
+            first_core, from_pair[b, :, NODES:], from_far[b, :, NODES:]
+        )
 
     at_end = place[1]
     steps = ROWS * place[2]
@@ -268,7 +271,8 @@
     total = pieces[0].astype(F32)
     for i in range(1, pieces.shape[0]):
         total = total + pieces[i].astype(F32)
-    out[...] = total.astype(BF16)
+    for x in range(out.shape[0]):
+        out[x] = total.astype(BF16)
 
 
 def finish_kernel(g, input_grad, filter_grad, mixing_grad, output_grad):
@@ -317,14 +321,11 @@
     cov, obs, w_in, w_f, w_m, w_out = (
         pltpu.with_memory_space_constraint(a, pltpu.HBM) for a in (cov, obs, w_in, w_f, w_m, w_out)
     )
-    to_next, to_prev, squares = call(
+    edge = shape((SEQ, HALO, 2 * NODES), F32)
+    to_pair, to_far, squares = call(
         start_kernel,
-        (
-            shape((SEQ, HALO, NODES), BF16),
-            shape((SEQ, HALO, 2 * NODES), F32),
-            shape((count, SEQ, 128), F32),
-        ),
-        [HBM, HBM],
+        (edge, edge, shape((count, SEQ, 128), F32)),
+        [SCALARS, HBM, HBM],
         scratch=[
             VMEM((SEQ, 16, NODES), BF16),
             VMEM((SEQ, 16, NODES), BF16),
@@ -333,10 +334,11 @@
         ],
         limit=4,
         name="start",
-    )(cov, obs)
+    )(place, cov, obs)
     sums = lax.all_to_all(squares, TM, 0, 0, tiled=True)
-    from_prev = lax.ppermute(to_next, TM, [(i, i + 1) for i in range(count - 1)])
-    from_next = lax.ppermute(to_prev, TM, [(i + 1, i) for i in range(count - 1)])
+    from_pair = lax.ppermute(to_pair, "core", [(0, 1), (1, 0)])
+    seams = [(i, i + 1) for i in range(1, count - 1, 2)]
+    from_far = lax.ppermute(to_far, TM, seams + [(j, i) for i, j in seams])
 
     piece = shape((4, 4, 32, 2048), BF16)
     cov_grad, send, keep = call(
@@ -363,14 +365,14 @@
         ],
         limit=44,
         name="step",
-    )(place, from_prev, from_next, sums, cov, obs, w_in, w_f, w_m, w_out)
+    )(place, from_pair, from_far, sums, cov, obs, w_in, w_f, w_m, w_out)
     got = lax.ppermute(send, "core", [(0, 1), (1, 0)])
     chip = call(add_kernel, piece, [WHOLE] * 2, limit=4, name="pair")(keep, got)
     plane = lax.all_to_all(chip.reshape(16, 32, 2048), ("x", "y"), 0, 0, tiled=True)
     by_z = call(plane_kernel, shape((8, 8, 1024), BF16), [WHOLE], limit=4, name="plane")(plane)
     line = lax.all_to_all(by_z, "z", 0, 0, tiled=True)
-    mine = call(line_kernel, shape((8, 1024), BF16), [WHOLE], limit=4, name="line")(line)
-    whole = lax.all_gather(mine, "x")
+    mine = call(line_kernel, shape((4, 8, 1024), BF16), [WHOLE], limit=4, name="line")(line)
+    whole = lax.all_to_all(mine, "x", 0, 0, tiled=True)
     input_grad, filter_grad, mixing_grad, output_grad = call(
         finish_kernel,
         (

time: 110 us -> 104 us (0.945)
  blocking collectives: 61.5 us -> 55.9 us
  starting transfers between devices: 19.9 us -> 17.1 us
  waiting for transfers between devices: 5.64 us -> 8.08 us
    all_gather x1 -> x0, blocking collectives: 11.9 us -> none  [per_device(): whole = lax.all_gather(mine, 'x')]
    all_to_all x0 -> x1, blocking collectives: none -> 7.99 us  [per_device(): whole = lax.all_to_all(mine, 'x', 0, 0, tiled=True)]
    ppermute x2, starting transfers between devices: 7.67 us -> 4.77 us  [the longest x1 4.53 us: per_device(): from_far = lax.ppermute(to_far, TM, seams + [(j, i) for i, j in seams])]
    ppermute x2, waiting for transfers between devices: 1.49 us -> 2.81 us  [the longest x1 2.81 us: per_device(): from_far = lax.ppermute(to_far, TM, seams + [(j, i) for i, j in seams])]
    all_to_all x1, waiting for transfers between devices: 0.01 us -> 1.22 us  [per_device(): sums = lax.all_to_all(squares, TM, 0, 0, tiled=True)]
  transfers between devices with their start and end apart: 4 -> 4, of which waited for: 2 -> 3; matrix products, arithmetic and copies ran while one was open for 0% -> 0% of each run, Pallas kernels for 0% -> 0%
where the time goes in v7:
time: 104 us
  blocking collectives  55.9 us (54%)
  Pallas kernels  21.9 us (21%)
  starting transfers between devices  17.1 us (16%)
  waiting for transfers between devices  8.08 us (8%)
    all_to_all x1, blocking collectives, per_device(): lax.all_to_all(chip.reshape(16, 32, 2048), ('x', 'y'), 0, 0, tiled=True)  33.6 us
    pallas_call x1, Pallas kernels, per_device(): call(step_kernel, (shape((SEQ, ROWS, NODES), BF16), piece, piece), [SCALA...  18.5 us
    all_to_all x1, blocking collectives, per_device(): line = lax.all_to_all(by_z, 'z', 0, 0, tiled=True)  14.3 us
    all_to_all x1, starting transfers between devices, per_device(): sums = lax.all_to_all(squares, TM, 0, 0, tiled=True)  12.1 us
    all_to_all x1, blocking collectives, per_device(): whole = lax.all_to_all(mine, 'x', 0, 0, tiled=True)  7.99 us
    ppermute x1, starting transfers between devices, per_device(): from_far = lax.ppermute(to_far, TM, seams + [(j, i) for i, j in seams])  4.53 us
    ppermute x1, waiting for transfers between devices, per_device(): got = lax.ppermute(send, 'core', [(0, 1), (1, 0)])  4.05 us
    ppermute x1, waiting for transfers between devices, per_device(): from_far = lax.ppermute(to_far, TM, seams + [(j, i) for i, j in seams])  2.81 us
  transfers between devices with their start and end apart: 4, of which 3 were waited for; matrix products, arithmetic and copies ran while one was open for 0% of the time, Pallas kernels for 0%

profile of v7, /device:TPU:8, one launch (start us, length us, event | category | flops | bytes accessed | tf_op | source)
XLA Modules:
  0.0 103.7 jit_solution(1166139860438326750)
XLA Ops:
  0.6 0.1 pad_add_fusion.place
  0.7 2.3 %start.1 = (f32[2,8,512]{2,1,0:T(8,128)S(1)}, f32[2,8,512]{2,1,0:T(8,128)S(1)}, f32[64,2,128]{2,1,0:T(2,128)}) custom-call(s32[3]{0:T(128)S(1)} %pad_add_fusion.place, bf16[2,128,256]{2,1,0:T(8,128)(2,1)} %cov_hbm.3, f32[2,128,256]{2,1,0:T(8,128)} %obs_hbm.3), custom_call_target="tpu_custom_call" | custom-call | tf_op jit(solution)/shard_map/start/pallas_call | solution.py:325
  3.0 12.1 %all-to-all-start = ((f32[64,2,128]{2,1,0:T(2,128)}), f32[64,2,128]{2,1,0:T(2,128)S(1)}, u32[]{:S(2)}, u32[]{:S(2)}) async-start(f32[64,2,128]{2,1,0:T(2,128)} %get-tuple-element.17), calls=%async_computation | async-start | bytes 131072 | tf_op jit(solution)/shard_map/all_to_all | solution.py:338
  15.1 0.2 collective-permute-start
  15.4 4.5 %collective-permute-start.1 = (f32[2,8,512]{2,1,0:T(8,128)S(1)}, f32[2,8,512]{2,1,0:T(8,128)S(1)}, u32[]{:S(2)}, u32[]{:S(2)}) collective-permute-start(f32[2,8,512]{2,1,0:T(8,128)S(1)} %get-tuple-element.16), channel_id=1, source_target_pairs={{4,8},{12,16},{20,24},{28,32},{36,40},{44,48},{52,56},{60,64},{68,... | collective-permute-start | bytes 98312 | tf_op jit(solution)/shard_map/ppermute | solution.py:341
  19.9 0.0 collective-permute-done.from_pair
  19.9 2.8 %collective-permute-done.1.from_far = f32[2,8,512]{2,1,0:T(8,128)S(1)} collective-permute-done((f32[2,8,512]{2,1,0:T(8,128)S(1)}, f32[2,8,512]{2,1,0:T(8,128)S(1)}, u32[]{:S(2)}, u32[]{:S(2)}) %collective-permute-start.1) | collective-permute-done | bytes 32800 | tf_op jit(solution)/shard_map/ppermute | solution.py:341
  22.7 1.2 %all-to-all-done.sums = f32[64,2,128]{2,1,0:T(2,128)S(1)} async-done(((f32[64,2,128]{2,1,0:T(2,128)}), f32[64,2,128]{2,1,0:T(2,128)S(1)}, u32[]{:S(2)}, u32[]{:S(2)}) %all-to-all-start) | async-done | bytes 65568 | tf_op jit(solution)/shard_map/all_to_all | solution.py:338
  24.0 18.5 %step.1 = (bf16[2,128,256]{2,1,0:T(8,128)(2,1)}, bf16[4,4,32,2048]{3,2,1,0:T(8,128)(2,1)S(1)}, bf16[4,4,32,2048]{3,2,1,0:T(8,128)(2,1)S(1)}) custom-call(s32[3]{0:T(128)S(1)} %pad_add_fusion.place, f32[2,8,512]{2,1,0:T(8,128)S(1)} %collective-permute-done.from_pair, f32[2,8,512]{2,1,0:T(8,128)S(1)} %collective-permute-done.1.from_far, ...), custom_call_target="tpu_custom_call" | custom-call | tf_op jit(solution)/shard_map/step/pallas_call | solution.py:344
  42.4 0.2 collective-permute-start.2
  42.6 4.0 %collective-permute-done.2.got = bf16[4,4,32,2048]{3,2,1,0:T(8,128)(2,1)S(1)} collective-permute-done((bf16[4,4,32,2048]{3,2,1,0:T(8,128)(2,1)S(1)}, bf16[4,4,32,2048]{3,2,1,0:T(8,128)(2,1)S(1)}, u32[]{:S(2)}, u32[]{:S(2)}) %collective-permute-start.2) | collective-permute-done | bytes 2097184 | tf_op jit(solution)/shard_map/ppermute | solution.py:369
  46.7 0.2 pair.1
  46.9 33.6 %all_to_all.20.pieces = bf16[16,32,2048]{2,1,0:T(8,128)(2,1)S(1)} all-to-all(bf16[16,32,2048]{2,1,0:T(8,128)(2,1)S(1)} %bitcast.3), channel_id=1, replica_groups=mesh['y'=4,'z'=8,'core'=2,'x'=4] {'x','y'}, dimensions={0} | all-to-all | bytes 4194304 | tf_op jit(solution)/shard_map/all_to_all | solution.py:371
  80.5 0.3 plane.1
  80.8 14.3 %all_to_all.21.pieces = bf16[8,8,1024]{2,1,0:T(8,128)(2,1)S(1)} all-to-all(bf16[8,8,1024]{2,1,0:T(8,128)(2,1)S(1)} %plane.1), channel_id=1, replica_groups=mesh['y'=4,'z'=8,'core'=2,'x'=4] {'z'}, dimensions={0} | all-to-all | bytes 262144 | tf_op jit(solution)/shard_map/all_to_all | solution.py:373
  95.1 8.0 %all_to_all.22.g = bf16[4,8,1024]{2,1,0:T(8,128)(2,1)S(1)} all-to-all(bf16[4,8,1024]{2,1,0:T(8,128)(2,1)S(1)} %line.1), channel_id=1, replica_groups=mesh['y'=4,'z'=8,'core'=2,'x'=4] {'x'}, dimensions={0} | all-to-all | bytes 131072 | tf_op jit(solution)/shard_map/all_to_all | solution.py:375
  103.1 0.6 finish.1
  (1 shorter events, 0.0 us)
Async XLA Ops:
  3.0 20.9 %all-to-all-start = ((f32[64,2,128]{2,1,0:T(2,128)}), f32[64,2,128]{2,1,0:T(2,128)S(1)}, u32[]{:S(2)}, u32[]{:S(2)}) async-start(f32[64,2,128]{2,1,0:T(2,128)} %get-tuple-element.17), calls=%async_computation | async-start | bytes 131072 | tf_op jit(solution)/shard_map/all_to_all | solution.py:338
  15.1 4.8 %collective-permute-start = (f32[2,8,512]{2,1,0:T(8,128)S(1)}, f32[2,8,512]{2,1,0:T(8,128)S(1)}, u32[]{:S(2)}, u32[]{:S(2)}) collective-permute-start(f32[2,8,512]{2,1,0:T(8,128)S(1)} %get-tuple-element.15), channel_id=1, source_target_pairs={{0,4},{4,0},{1,5},{5,1},{2,6},{6,2},{3,7},{7,3},{8,12},{12,8},{9,1... | collective-permute-start | bytes 98312 | tf_op jit(solution)/shard_map/ppermute | solution.py:339
  15.4 7.4 %collective-permute-start.1 = (f32[2,8,512]{2,1,0:T(8,128)S(1)}, f32[2,8,512]{2,1,0:T(8,128)S(1)}, u32[]{:S(2)}, u32[]{:S(2)}) collective-permute-start(f32[2,8,512]{2,1,0:T(8,128)S(1)} %get-tuple-element.16), channel_id=1, source_target_pairs={{4,8},{12,16},{20,24},{28,32},{36,40},{44,48},{52,56},{60,64},{68,... | collective-permute-start | bytes 98312 | tf_op jit(solution)/shard_map/ppermute | solution.py:341
  42.4 4.2 %collective-permute-start.2 = (bf16[4,4,32,2048]{3,2,1,0:T(8,128)(2,1)S(1)}, bf16[4,4,32,2048]{3,2,1,0:T(8,128)(2,1)S(1)}, u32[]{:S(2)}, u32[]{:S(2)}) collective-permute-start(bf16[4,4,32,2048]{3,2,1,0:T(8,128)(2,1)S(1)} %get-tuple-element.20), channel_id=1, source_target_pairs={{0,4},{4,0},{1,5},{5,1},{2,6},{6,2},{3,7},{7,3},{8,12},{12,8},{9,1... | collective-permute-start | bytes 6291464 | tf_op jit(solution)/shard_map/ppermute | solution.py:369

commit v8 on v7

--- a/solution.py
+++ b/solution.py
@@ -36,7 +36,7 @@
     return jax.ShapeDtypeStruct(dims, dtype)
 
 
-def start_kernel(place, cov_hbm, obs_hbm, to_pair, to_far, squares, tail, head, obs, sems):
+def start_kernel(cov_hbm, obs_hbm, to_pair, to_far, squares, tail, head, obs, sems):
     copies = [
         pltpu.make_async_copy(obs_hbm, obs, sems.at[0]),
         pltpu.make_async_copy(cov_hbm.at[:, pl.ds(ROWS - 16, 16), :], tail, sems.at[1]),
@@ -46,7 +46,7 @@
         copy.start()
     for copy in copies:
         copy.wait()
-    first_core = place[0] == 0
+    first_core = lax.axis_index("core") == 0
     for b in range(SEQ):
         late = jnp.concatenate([tail[b].astype(F32)[16 - HALO :], obs[b, ROWS - HALO :, :]], axis=1)
         early = jnp.concatenate([head[b].astype(F32)[:HALO], obs[b, :HALO, :]], axis=1)
@@ -98,11 +98,10 @@
     return [jnp.concatenate([scale * p0, scale * p1], axis=1) for p0, p1 in result]
 
 
-def step_kernel(
-    place, from_pair, from_far, sums, cov_hbm, obs_hbm, w_in_hbm, w_f_hbm, w_m_hbm, w_out_hbm,
-    cov_grad, send, keep,
-    pred, target, cov, obs, w_in, w_f, w_m, w_out,
-    tanh_act, gate_act, dpred, cov_t, gated_t, last_t, taps_t, sems,
+def score_kernel(
+    from_pair, from_far, sums, cov_hbm, obs_hbm, w_in_hbm, w_f_hbm, w_m_hbm, w_out_hbm,
+    grad_out, send, keep, tanh_act, gate_act, cov_t, gated_t, taps_t, w_in, w_f, w_m,
+    pred, target, cov, obs, w_out, dpred, last_t, sems,
 ):
     cov_copy = pltpu.make_async_copy(cov_hbm, cov, sems.at[0])
     w_in_copy = pltpu.make_async_copy(w_in_hbm, w_in, sems.at[1])
@@ -112,7 +111,7 @@
     w_out_copy = pltpu.make_async_copy(w_out_hbm, w_out, sems.at[5])
     for copy in (cov_copy, w_in_copy, w_f_copy, w_m_copy, obs_copy, w_out_copy):
         copy.start()
-    core = place[0]
+    core = lax.axis_index("core")
     perm4 = permutation(core, 4)
     perm8 = permutation(core, 8)
 
@@ -158,10 +157,10 @@
             first_core, from_pair[b, :, NODES:], from_far[b, :, NODES:]
         )
 
-    at_end = place[1]
-    steps = ROWS * place[2]
+    at_end = lax.axis_index(TM) == lax.axis_size(TM) - 1
+    steps = ROWS * lax.axis_size(TM)
     total = jnp.sum(sums[...], axis=0)
-    inv = lax.rsqrt(total / (steps * NODES).astype(F32) + epsilon)
+    inv = lax.rsqrt(total / (steps * NODES) + epsilon)
     inv = inv * (NODES**0.5 / (SCENARIOS * (SCENARIOS - 1) * NODES))
 
     def step(i, carry):
@@ -169,7 +168,7 @@
         for part in range(2):
             chunk = i * 2 + part
             first = (chunk < ROWS // 8) | (chunk == OWN // 8)
-            beyond = (chunk >= OWN // 8) & (at_end == 1)
+            beyond = (chunk >= OWN // 8) & at_end
             scale = jnp.where(beyond, 0.0, jnp.where(first, inv[0:1], inv[1:2]))
             at = pl.ds(pl.multiple_of(chunk * 8, 8), 8)
             y = [
@@ -192,7 +191,7 @@
         for ref, half in places:
             for y in range(4):
                 top = half * 128 + y * 32
-                ref[x, y, :, :1024] = out_grad[top : top + 32].astype(BF16)
+                ref[x, y] = out_grad[top : top + 32].astype(BF16)
     head_grad = mm_nt(dpred[...], w_out[...])
     pieces = []
     for b in range(SEQ):
@@ -201,13 +200,21 @@
             head_grad[b * ROWS : (b + 1) * ROWS],
             head_grad[OWN + b * HALO : OWN + (b + 1) * HALO],
         ]
-    grad = jnp.concatenate(pieces, axis=0).astype(BF16)
+    grad_out[...] = jnp.concatenate(pieces, axis=0).astype(BF16)
+
+
+def layers_kernel(
+    grad_in, tanh_act, gate_act, cov_t, gated_t, taps_t, w_in, w_f, w_m,
+    cov_grad, send, keep,
+):
+    grad = grad_in[...]
+    places = ((send, 0), (keep, 1))
 
     def store_small(x, value):
         for ref, half in places:
             for y in range(4):
                 top = half * 128 + y * 32
-                ref[x, y, :, 1024:1280] = value[top : top + 32].astype(BF16)
+                ref[x, y, :, :256] = value[top : top + 32].astype(BF16)
 
     for layer in reversed(range(LAYERS)):
         grad_wide = grad.astype(F32)
@@ -232,7 +239,7 @@
                     for x in range(4):
                         columns = slice(x * 128, (x + 1) * 128)
                         for low in range(2):
-                            base = 1280 + low * 384 + layer * 128
+                            base = 256 + low * 384 + layer * 128
                             ref[x, tap * 2 + y_low, :, base : base + 128] = tap_grad[
                                 top + low * 32 : top + low * 32 + 32, columns
                             ].astype(BF16)
@@ -252,6 +259,11 @@
     out[...] = keep[...] + got[...]
 
 
+def join_kernel(score, keep, got, out):
+    out[:, :, :, :1024] = score[...]
+    out[:, :, :, 1024:] = keep[...] + got[...]
+
+
 def plane_kernel(pieces, out):
     total = pieces[0].astype(F32)
     for i in range(1, pieces.shape[0]):
@@ -292,11 +304,10 @@
 
 HBM = pl.BlockSpec(memory_space=pltpu.HBM)
 ANY = pl.BlockSpec(memory_space=pl.ANY)
-SCALARS = pl.BlockSpec(memory_space=pltpu.SMEM)
 WHOLE = pl.BlockSpec(memory_space=VMEM)
 
 
-def call(kernel, out_shape, in_specs, scratch=(), limit=16, name=None):
+def call(kernel, out_shape, in_specs, scratch=(), limit=16, name=None, cost=None):
     return pl.pallas_call(
         kernel,
         out_shape=out_shape,
@@ -305,19 +316,12 @@
         scratch_shapes=scratch,
         compiler_params=pltpu.CompilerParams(vmem_limit_bytes=limit * 1024 * 1024),
         name=name,
+        cost_estimate=cost,
     )
 
 
 def per_device(cov, obs, w_in, w_f, w_m, w_out):
     count = lax.axis_size(TM)
-    me = lax.axis_index(TM)
-    place = jnp.stack(
-        [
-            lax.axis_index("core"),
-            jnp.where(me == count - 1, 1, 0),
-            jnp.int32(count),
-        ]
-    ).astype(jnp.int32)
     cov, obs, w_in, w_f, w_m, w_out = (
         pltpu.with_memory_space_constraint(a, pltpu.HBM) for a in (cov, obs, w_in, w_f, w_m, w_out)
     )
@@ -325,7 +329,7 @@
     to_pair, to_far, squares = call(
         start_kernel,
         (edge, edge, shape((count, SEQ, 128), F32)),
-        [SCALARS, HBM, HBM],
+        [HBM, HBM],
         scratch=[
             VMEM((SEQ, 16, NODES), BF16),
             VMEM((SEQ, 16, NODES), BF16),
@@ -334,40 +338,59 @@
         ],
         limit=4,
         name="start",
-    )(place, cov, obs)
+    )(cov, obs)
     sums = lax.all_to_all(squares, TM, 0, 0, tiled=True)
     from_pair = lax.ppermute(to_pair, "core", [(0, 1), (1, 0)])
     seams = [(i, i + 1) for i in range(1, count - 1, 2)]
     from_far = lax.ppermute(to_far, TM, seams + [(j, i) for i, j in seams])
 
-    piece = shape((4, 4, 32, 2048), BF16)
-    cov_grad, send, keep = call(
-        step_kernel,
-        (shape((SEQ, ROWS, NODES), BF16), piece, piece),
-        [SCALARS, WHOLE, WHOLE, WHOLE] + [HBM] * 6,
+    part = shape((4, 4, 32, 1024), BF16)
+    act = shape((LAYERS, ALL_ROWS, NODES), F32)
+    grad, send_score, keep_score, *saved = call(
+        score_kernel,
+        (
+            shape((ALL_ROWS, NODES), BF16),
+            part,
+            part,
+            act,
+            act,
+            shape((NODES, OWN), BF16),
+            shape((LAYERS, NODES, OWN), BF16),
+            shape((LAYERS, 2, NODES, OWN), BF16),
+            shape(w_in.shape, BF16),
+            shape(w_f.shape, BF16),
+            shape(w_m.shape, BF16),
+        ),
+        [WHOLE, WHOLE, WHOLE] + [HBM] * 6,
         scratch=[
             VMEM((ALL_HEAD, SCENARIOS * NODES), F32),
             VMEM((ALL_HEAD, NODES), F32),
             VMEM(cov.shape, BF16),
             VMEM(obs.shape, F32),
-            VMEM(w_in.shape, BF16),
-            VMEM(w_f.shape, BF16),
-            VMEM(w_m.shape, BF16),
             VMEM(w_out.shape, BF16),
-            VMEM((LAYERS, ALL_ROWS, NODES), F32),
-            VMEM((LAYERS, ALL_ROWS, NODES), F32),
             VMEM((ALL_HEAD, SCENARIOS * NODES), BF16),
             VMEM((NODES, OWN), BF16),
-            VMEM((LAYERS, NODES, OWN), BF16),
-            VMEM((NODES, OWN), BF16),
-            VMEM((LAYERS, 2, NODES, OWN), BF16),
             pltpu.SemaphoreType.DMA((6,)),
         ],
-        limit=44,
-        name="step",
-    )(place, from_pair, from_far, sums, cov, obs, w_in, w_f, w_m, w_out)
-    got = lax.ppermute(send, "core", [(0, 1), (1, 0)])
-    chip = call(add_kernel, piece, [WHOLE] * 2, limit=4, name="pair")(keep, got)
+        limit=36,
+        name="score",
+        cost=pl.CostEstimate(flops=10**10, transcendentals=0, bytes_accessed=10**7),
+    )(from_pair, from_far, sums, cov, obs, w_in, w_f, w_m, w_out)
+    swap = [(0, 1), (1, 0)]
+    got_score = lax.ppermute(send_score, "core", swap)
+    cov_grad, send_rest, keep_rest = call(
+        layers_kernel,
+        (shape((SEQ, ROWS, NODES), BF16), part, part),
+        [WHOLE] * 9,
+        limit=16,
+        name="layers",
+        cost=pl.CostEstimate(flops=4 * 10**9, transcendentals=0, bytes_accessed=10**7),
+    )(grad, *saved)
+    got_rest = lax.ppermute(send_rest, "core", swap)
+    score = call(add_kernel, part, [WHOLE] * 2, limit=4, name="pair")(keep_score, got_score)
+    chip = call(join_kernel, shape((4, 4, 32, 2048), BF16), [WHOLE] * 3, limit=4, name="join")(
+        score, keep_rest, got_rest
+    )
     plane = lax.all_to_all(chip.reshape(16, 32, 2048), ("x", "y"), 0, 0, tiled=True)
     by_z = call(plane_kernel, shape((8, 8, 1024), BF16), [WHOLE], limit=4, name="plane")(plane)
     line = lax.all_to_all(by_z, "z", 0, 0, tiled=True)

time: 104 us -> 102 us (0.981)
  waiting for transfers between devices: 8.08 us -> 6.21 us
    ppermute x1 -> x2, waiting for transfers between devices: 4.05 us -> 2.18 us  [the longest x1 2.17 us: per_device(): got_rest = lax.ppermute(send_rest, 'core', swap)]
    pallas_call x3 -> x5, Pallas kernels: 21 us -> 20.2 us  [the longest x1 15.3 us: per_device(): call(score_kernel, (shape((ALL_ROWS, NODES), BF16), part, part, act, act,...]
  transfers between devices with their start and end apart: 4 -> 5, of which waited for: 3 -> 3; matrix products, arithmetic and copies ran while one was open for 0% -> 0% of each run, Pallas kernels for 0% -> 3%
where the time goes in v8:
time: 102 us
  blocking collectives  56.1 us (55%)
  Pallas kernels  21.1 us (21%)
  starting transfers between devices  17.5 us (17%)
  waiting for transfers between devices  6.21 us (6%)
    all_to_all x1, blocking collectives, per_device(): lax.all_to_all(chip.reshape(16, 32, 2048), ('x', 'y'), 0, 0, tiled=True)  33.9 us
    pallas_call x1, Pallas kernels, per_device(): call(score_kernel, (shape((ALL_ROWS, NODES), BF16), part, part, act, act,...  15.3 us
    all_to_all x1, blocking collectives, per_device(): line = lax.all_to_all(by_z, 'z', 0, 0, tiled=True)  14.3 us
    all_to_all x1, starting transfers between devices, per_device(): sums = lax.all_to_all(squares, TM, 0, 0, tiled=True)  12.1 us
    all_to_all x1, blocking collectives, per_device(): whole = lax.all_to_all(mine, 'x', 0, 0, tiled=True)  7.99 us
    ppermute x1, starting transfers between devices, per_device(): from_far = lax.ppermute(to_far, TM, seams + [(j, i) for i, j in seams])  4.53 us
    pallas_call x1, Pallas kernels, per_device(): call(layers_kernel, (shape((SEQ, ROWS, NODES), BF16), part, part), [WHOLE...  2.83 us
    ppermute x1, waiting for transfers between devices, per_device(): from_far = lax.ppermute(to_far, TM, seams + [(j, i) for i, j in seams])  2.81 us
  transfers between devices with their start and end apart: 5, of which 3 were waited for; matrix products, arithmetic and copies ran while one was open for 0% of the time, Pallas kernels for 3%

profile of v8, /device:TPU:8, one launch (start us, length us, event | category | flops | bytes accessed | tf_op | source)
XLA Modules:
  0.0 101.6 jit_solution(7573366700619900789)
XLA Ops:
  0.6 1.7 %start.1 = (f32[2,8,512]{2,1,0:T(8,128)S(1)}, f32[2,8,512]{2,1,0:T(8,128)S(1)}, f32[64,2,128]{2,1,0:T(2,128)}) custom-call(bf16[2,128,256]{2,1,0:T(8,128)(2,1)} %cov_hbm.3, f32[2,128,256]{2,1,0:T(8,128)} %obs_hbm.3), custom_call_target="tpu_custom_call" | custom-call | tf_op jit(solution)/shard_map/start/pallas_call | solution.py:329
  2.4 12.1 %all-to-all-start = ((f32[64,2,128]{2,1,0:T(2,128)}), f32[64,2,128]{2,1,0:T(2,128)S(1)}, u32[]{:S(2)}, u32[]{:S(2)}) async-start(f32[64,2,128]{2,1,0:T(2,128)} %get-tuple-element.28), calls=%async_computation | async-start | bytes 131072 | tf_op jit(solution)/shard_map/all_to_all | solution.py:342
  14.5 0.2 collective-permute-start
  14.7 4.5 %collective-permute-start.1 = (f32[2,8,512]{2,1,0:T(8,128)S(1)}, f32[2,8,512]{2,1,0:T(8,128)S(1)}, u32[]{:S(2)}, u32[]{:S(2)}) collective-permute-start(f32[2,8,512]{2,1,0:T(8,128)S(1)} %get-tuple-element.27), channel_id=1, source_target_pairs={{4,8},{12,16},{20,24},{28,32},{36,40},{44,48},{52,56},{60,64},{68,... | collective-permute-start | bytes 98312 | tf_op jit(solution)/shard_map/ppermute | solution.py:345
  19.3 0.0 collective-permute-done.from_pair
  19.3 2.8 %collective-permute-done.1.from_far = f32[2,8,512]{2,1,0:T(8,128)S(1)} collective-permute-done((f32[2,8,512]{2,1,0:T(8,128)S(1)}, f32[2,8,512]{2,1,0:T(8,128)S(1)}, u32[]{:S(2)}, u32[]{:S(2)}) %collective-permute-start.1) | collective-permute-done | bytes 32800 | tf_op jit(solution)/shard_map/ppermute | solution.py:345
  22.1 1.2 %all-to-all-done.sums = f32[64,2,128]{2,1,0:T(2,128)S(1)} async-done(((f32[64,2,128]{2,1,0:T(2,128)}), f32[64,2,128]{2,1,0:T(2,128)S(1)}, u32[]{:S(2)}, u32[]{:S(2)}) %all-to-all-start) | async-done | bytes 65568 | tf_op jit(solution)/shard_map/all_to_all | solution.py:342
  23.3 15.3 %score.1 = (bf16[288,256]{1,0:T(8,128)(2,1)S(1)}, bf16[4,4,32,1024]{3,2,1,0:T(8,128)(2,1)S(1)}, bf16[4,4,32,1024]{3,2,1,0:T(8,128)(2,1)S(1)}, f32[3,288,256]{2,1...) custom-call(f32[2,8,512]{2,1,0:T(8,128)S(1)} %collective-permute-don, ...), custom_call_target="tpu_custom_call" | custom-call | flops 10000000000 | bytes 10000000 | tf_op jit(solution)/shard_map/score/pallas_call | solution.py:349
  38.7 0.2 collective-permute-start.2
  38.9 2.8 %layers.1 = (bf16[2,128,256]{2,1,0:T(8,128)(2,1)}, bf16[4,4,32,1024]{3,2,1,0:T(8,128)(2,1)S(1)}, bf16[4,4,32,1024]{3,2,1,0:T(8,128)(2,1)S(1)}) custom-call(bf16[288,256]{1,0:T(8,128)(2,1)S(1)} %get-tuple-element.29.grad_in, f32[3,288,256]{2,1,0:T(8,128)S(1)} %get-tuple-element.30.tanh_act, f32[3,288,256]{2,1,0:T(8,128)S(1)} %get-tuple-element.31.gate_act, ...), custom_call_target="tpu_custom_call" | custom-call | flops 4000000000 | bytes 10000000 | tf_op jit(solution)/shard_map/layers/pallas_call | solution.py:381
  41.7 0.4 collective-permute-start.3
  42.1 0.0 collective-permute-done.2.got
  42.1 0.1 pair.1.score
  42.2 2.2 %collective-permute-done.3.got = bf16[4,4,32,1024]{3,2,1,0:T(8,128)(2,1)S(1)} collective-permute-done((bf16[4,4,32,1024]{3,2,1,0:T(8,128)(2,1)S(1)}, bf16[4,4,32,1024]{3,2,1,0:T(8,128)(2,1)S(1)}, u32[]{:S(2)}, u32[]{:S(2)}) %collective-permute-start.3) | collective-permute-done | bytes 1048608 | tf_op jit(solution)/shard_map/ppermute | solution.py:389
  44.4 0.2 join.1
  44.6 33.9 %all_to_all.20.pieces = bf16[16,32,2048]{2,1,0:T(8,128)(2,1)S(1)} all-to-all(bf16[16,32,2048]{2,1,0:T(8,128)(2,1)S(1)} %bitcast.1), channel_id=1, replica_groups=mesh['y'=4,'z'=8,'core'=2,'x'=4] {'x','y'}, dimensions={0} | all-to-all | bytes 4194304 | tf_op jit(solution)/shard_map/all_to_all | solution.py:394
  78.4 0.3 plane.1
  78.7 14.3 %all_to_all.21.pieces = bf16[8,8,1024]{2,1,0:T(8,128)(2,1)S(1)} all-to-all(bf16[8,8,1024]{2,1,0:T(8,128)(2,1)S(1)} %plane.1), channel_id=1, replica_groups=mesh['y'=4,'z'=8,'core'=2,'x'=4] {'z'}, dimensions={0} | all-to-all | bytes 262144 | tf_op jit(solution)/shard_map/all_to_all | solution.py:396
  93.0 8.0 %all_to_all.22.g = bf16[4,8,1024]{2,1,0:T(8,128)(2,1)S(1)} all-to-all(bf16[4,8,1024]{2,1,0:T(8,128)(2,1)S(1)} %line.1), channel_id=1, replica_groups=mesh['y'=4,'z'=8,'core'=2,'x'=4] {'x'}, dimensions={0} | all-to-all | bytes 131072 | tf_op jit(solution)/shard_map/all_to_all | solution.py:398
  101.0 0.6 finish.1
  (1 shorter events, 0.0 us)
Async XLA Ops:
  2.4 20.9 %all-to-all-start = ((f32[64,2,128]{2,1,0:T(2,128)}), f32[64,2,128]{2,1,0:T(2,128)S(1)}, u32[]{:S(2)}, u32[]{:S(2)}) async-start(f32[64,2,128]{2,1,0:T(2,128)} %get-tuple-element.28), calls=%async_computation | async-start | bytes 131072 | tf_op jit(solution)/shard_map/all_to_all | solution.py:342
  14.5 4.8 %collective-permute-start = (f32[2,8,512]{2,1,0:T(8,128)S(1)}, f32[2,8,512]{2,1,0:T(8,128)S(1)}, u32[]{:S(2)}, u32[]{:S(2)}) collective-permute-start(f32[2,8,512]{2,1,0:T(8,128)S(1)} %get-tuple-element.26), channel_id=1, source_target_pairs={{0,4},{4,0},{1,5},{5,1},{2,6},{6,2},{3,7},{7,3},{8,12},{12,8},{9,1... | collective-permute-start | bytes 98312 | tf_op jit(solution)/shard_map/ppermute | solution.py:343
  14.7 7.4 %collective-permute-start.1 = (f32[2,8,512]{2,1,0:T(8,128)S(1)}, f32[2,8,512]{2,1,0:T(8,128)S(1)}, u32[]{:S(2)}, u32[]{:S(2)}) collective-permute-start(f32[2,8,512]{2,1,0:T(8,128)S(1)} %get-tuple-element.27), channel_id=1, source_target_pairs={{4,8},{12,16},{20,24},{28,32},{36,40},{44,48},{52,56},{60,64},{68,... | collective-permute-start | bytes 98312 | tf_op jit(solution)/shard_map/ppermute | solution.py:345
  38.7 3.4 %collective-permute-start.2 = (bf16[4,4,32,1024]{3,2,1,0:T(8,128)(2,1)S(1)}, bf16[4,4,32,1024]{3,2,1,0:T(8,128)(2,1)S(1)}, u32[]{:S(2)}, u32[]{:S(2)}) collective-permute-start(bf16[4,4,32,1024]{3,2,1,0:T(8,128)(2,1)S(1)} %get-tuple-element.40), channel_id=1, source_target_pairs={{0,4},{4,0},{1,5},{5,1},{2,6},{6,2},{3,7},{7,3},{8,12},{12,8},{9,1... | collective-permute-start | bytes 3145736 | tf_op jit(solution)/shard_map/ppermute | solution.py:380
  41.7 2.7 %collective-permute-start.3 = (bf16[4,4,32,1024]{3,2,1,0:T(8,128)(2,1)S(1)}, bf16[4,4,32,1024]{3,2,1,0:T(8,128)(2,1)S(1)}, u32[]{:S(2)}, u32[]{:S(2)}) collective-permute-start(bf16[4,4,32,1024]{3,2,1,0:T(8,128)(2,1)S(1)} %get-tuple-element.42), channel_id=1, source_target_pairs={{0,4},{4,0},{1,5},{5,1},{2,6},{6,2},{3,7},{7,3},{8,12},{12,8},{9,1... | collective-permute-start | bytes 3145736 | tf_op jit(solution)/shard_map/ppermute | solution.py:389

commit v9 on v8

--- a/solution.py
+++ b/solution.py
@@ -183,7 +183,8 @@
             dpred[at, s * NODES : (s + 1) * NODES] = both.astype(BF16)
         return carry
 
-    lax.fori_loop(0, ALL_HEAD // 16, step, 0)
+    lax.fori_loop(0, OWN // 16, step, 0, unroll=4)
+    step(OWN // 16, 0)
 
     places = ((send, 0), (keep, 1))
     for x in range(4):

time: 102 us -> 101 us (level)
  no operation moved by 1% of the time
where the time goes in v9:
time: 101 us
  blocking collectives  56.1 us (56%)
  Pallas kernels  20.4 us (20%)
  starting transfers between devices  17.5 us (17%)
  waiting for transfers between devices  6.21 us (6%)
    all_to_all x1, blocking collectives, per_device(): lax.all_to_all(chip.reshape(16, 32, 2048), ('x', 'y'), 0, 0, tiled=True)  33.8 us
    pallas_call x1, Pallas kernels, per_device(): call(score_kernel, (shape((ALL_ROWS, NODES), BF16), part, part, act, act,...  14.6 us
    all_to_all x1, blocking collectives, per_device(): line = lax.all_to_all(by_z, 'z', 0, 0, tiled=True)  14.3 us
    all_to_all x1, starting transfers between devices, per_device(): sums = lax.all_to_all(squares, TM, 0, 0, tiled=True)  12.1 us
    all_to_all x1, blocking collectives, per_device(): whole = lax.all_to_all(mine, 'x', 0, 0, tiled=True)  7.99 us
    ppermute x1, starting transfers between devices, per_device(): from_far = lax.ppermute(to_far, TM, seams + [(j, i) for i, j in seams])  4.53 us
    pallas_call x1, Pallas kernels, per_device(): call(layers_kernel, (shape((SEQ, ROWS, NODES), BF16), part, part), [WHOLE...  2.83 us
    ppermute x1, waiting for transfers between devices, per_device(): from_far = lax.ppermute(to_far, TM, seams + [(j, i) for i, j in seams])  2.81 us
  transfers between devices with their start and end apart: 5, of which 3 were waited for; matrix products, arithmetic and copies ran while one was open for 0% of the time, Pallas kernels for 3%

profile of v9, /device:TPU:8, one launch (start us, length us, event | category | flops | bytes accessed | tf_op | source)
XLA Modules:
  0.0 100.9 jit_solution(14867514375664608382)
XLA Ops:
  0.6 1.7 %start.1 = (f32[2,8,512]{2,1,0:T(8,128)S(1)}, f32[2,8,512]{2,1,0:T(8,128)S(1)}, f32[64,2,128]{2,1,0:T(2,128)}) custom-call(bf16[2,128,256]{2,1,0:T(8,128)(2,1)} %cov_hbm.3, f32[2,128,256]{2,1,0:T(8,128)} %obs_hbm.3), custom_call_target="tpu_custom_call" | custom-call | tf_op jit(solution)/shard_map/start/pallas_call | solution.py:330
  2.4 12.1 %all-to-all-start = ((f32[64,2,128]{2,1,0:T(2,128)}), f32[64,2,128]{2,1,0:T(2,128)S(1)}, u32[]{:S(2)}, u32[]{:S(2)}) async-start(f32[64,2,128]{2,1,0:T(2,128)} %get-tuple-element.28), calls=%async_computation | async-start | bytes 131072 | tf_op jit(solution)/shard_map/all_to_all | solution.py:343
  14.5 0.2 collective-permute-start
  14.7 4.5 %collective-permute-start.1 = (f32[2,8,512]{2,1,0:T(8,128)S(1)}, f32[2,8,512]{2,1,0:T(8,128)S(1)}, u32[]{:S(2)}, u32[]{:S(2)}) collective-permute-start(f32[2,8,512]{2,1,0:T(8,128)S(1)} %get-tuple-element.27), channel_id=1, source_target_pairs={{4,8},{12,16},{20,24},{28,32},{36,40},{44,48},{52,56},{60,64},{68,... | collective-permute-start | bytes 98312 | tf_op jit(solution)/shard_map/ppermute | solution.py:346
  19.3 0.0 collective-permute-done.from_pair
  19.3 2.8 %collective-permute-done.1.from_far = f32[2,8,512]{2,1,0:T(8,128)S(1)} collective-permute-done((f32[2,8,512]{2,1,0:T(8,128)S(1)}, f32[2,8,512]{2,1,0:T(8,128)S(1)}, u32[]{:S(2)}, u32[]{:S(2)}) %collective-permute-start.1) | collective-permute-done | bytes 32800 | tf_op jit(solution)/shard_map/ppermute | solution.py:346
  22.1 1.2 %all-to-all-done.sums = f32[64,2,128]{2,1,0:T(2,128)S(1)} async-done(((f32[64,2,128]{2,1,0:T(2,128)}), f32[64,2,128]{2,1,0:T(2,128)S(1)}, u32[]{:S(2)}, u32[]{:S(2)}) %all-to-all-start) | async-done | bytes 65568 | tf_op jit(solution)/shard_map/all_to_all | solution.py:343
  23.3 14.6 %score.1 = (bf16[288,256]{1,0:T(8,128)(2,1)S(1)}, bf16[4,4,32,1024]{3,2,1,0:T(8,128)(2,1)S(1)}, bf16[4,4,32,1024]{3,2,1,0:T(8,128)(2,1)S(1)}, f32[3,288,256]{2,1...) custom-call(f32[2,8,512]{2,1,0:T(8,128)S(1)} %collective-permute-don, ...), custom_call_target="tpu_custom_call" | custom-call | flops 10000000000 | bytes 10000000 | tf_op jit(solution)/shard_map/score/pallas_call | solution.py:350
  38.0 0.2 collective-permute-start.2
  38.2 2.8 %layers.1 = (bf16[2,128,256]{2,1,0:T(8,128)(2,1)}, bf16[4,4,32,1024]{3,2,1,0:T(8,128)(2,1)S(1)}, bf16[4,4,32,1024]{3,2,1,0:T(8,128)(2,1)S(1)}) custom-call(bf16[288,256]{1,0:T(8,128)(2,1)S(1)} %get-tuple-element.29.grad_in, f32[3,288,256]{2,1,0:T(8,128)S(1)} %get-tuple-element.30.tanh_act, f32[3,288,256]{2,1,0:T(8,128)S(1)} %get-tuple-element.31.gate_act, ...), custom_call_target="tpu_custom_call" | custom-call | flops 4000000000 | bytes 10000000 | tf_op jit(solution)/shard_map/layers/pallas_call | solution.py:382
  41.0 0.4 collective-permute-start.3
  41.4 0.0 collective-permute-done.2.got
  41.4 0.1 pair.1.score
  41.5 2.2 %collective-permute-done.3.got = bf16[4,4,32,1024]{3,2,1,0:T(8,128)(2,1)S(1)} collective-permute-done((bf16[4,4,32,1024]{3,2,1,0:T(8,128)(2,1)S(1)}, bf16[4,4,32,1024]{3,2,1,0:T(8,128)(2,1)S(1)}, u32[]{:S(2)}, u32[]{:S(2)}) %collective-permute-start.3) | collective-permute-done | bytes 1048608 | tf_op jit(solution)/shard_map/ppermute | solution.py:390
  43.7 0.2 join.1
  43.9 33.8 %all_to_all.20.pieces = bf16[16,32,2048]{2,1,0:T(8,128)(2,1)S(1)} all-to-all(bf16[16,32,2048]{2,1,0:T(8,128)(2,1)S(1)} %bitcast.1), channel_id=1, replica_groups=mesh['y'=4,'z'=8,'core'=2,'x'=4] {'x','y'}, dimensions={0} | all-to-all | bytes 4194304 | tf_op jit(solution)/shard_map/all_to_all | solution.py:395
  77.7 0.3 plane.1
  78.0 14.3 %all_to_all.21.pieces = bf16[8,8,1024]{2,1,0:T(8,128)(2,1)S(1)} all-to-all(bf16[8,8,1024]{2,1,0:T(8,128)(2,1)S(1)} %plane.1), channel_id=1, replica_groups=mesh['y'=4,'z'=8,'core'=2,'x'=4] {'z'}, dimensions={0} | all-to-all | bytes 262144 | tf_op jit(solution)/shard_map/all_to_all | solution.py:397
  92.3 8.0 %all_to_all.22.g = bf16[4,8,1024]{2,1,0:T(8,128)(2,1)S(1)} all-to-all(bf16[4,8,1024]{2,1,0:T(8,128)(2,1)S(1)} %line.1), channel_id=1, replica_groups=mesh['y'=4,'z'=8,'core'=2,'x'=4] {'x'}, dimensions={0} | all-to-all | bytes 131072 | tf_op jit(solution)/shard_map/all_to_all | solution.py:399
  100.3 0.6 finish.1
  (1 shorter events, 0.0 us)
Async XLA Ops:
  2.4 20.9 %all-to-all-start = ((f32[64,2,128]{2,1,0:T(2,128)}), f32[64,2,128]{2,1,0:T(2,128)S(1)}, u32[]{:S(2)}, u32[]{:S(2)}) async-start(f32[64,2,128]{2,1,0:T(2,128)} %get-tuple-element.28), calls=%async_computation | async-start | bytes 131072 | tf_op jit(solution)/shard_map/all_to_all | solution.py:343
  14.5 4.8 %collective-permute-start = (f32[2,8,512]{2,1,0:T(8,128)S(1)}, f32[2,8,512]{2,1,0:T(8,128)S(1)}, u32[]{:S(2)}, u32[]{:S(2)}) collective-permute-start(f32[2,8,512]{2,1,0:T(8,128)S(1)} %get-tuple-element.26), channel_id=1, source_target_pairs={{0,4},{4,0},{1,5},{5,1},{2,6},{6,2},{3,7},{7,3},{8,12},{12,8},{9,1... | collective-permute-start | bytes 98312 | tf_op jit(solution)/shard_map/ppermute | solution.py:344
  14.7 7.4 %collective-permute-start.1 = (f32[2,8,512]{2,1,0:T(8,128)S(1)}, f32[2,8,512]{2,1,0:T(8,128)S(1)}, u32[]{:S(2)}, u32[]{:S(2)}) collective-permute-start(f32[2,8,512]{2,1,0:T(8,128)S(1)} %get-tuple-element.27), channel_id=1, source_target_pairs={{4,8},{12,16},{20,24},{28,32},{36,40},{44,48},{52,56},{60,64},{68,... | collective-permute-start | bytes 98312 | tf_op jit(solution)/shard_map/ppermute | solution.py:346
  38.0 3.4 %collective-permute-start.2 = (bf16[4,4,32,1024]{3,2,1,0:T(8,128)(2,1)S(1)}, bf16[4,4,32,1024]{3,2,1,0:T(8,128)(2,1)S(1)}, u32[]{:S(2)}, u32[]{:S(2)}) collective-permute-start(bf16[4,4,32,1024]{3,2,1,0:T(8,128)(2,1)S(1)} %get-tuple-element.40), channel_id=1, source_target_pairs={{0,4},{4,0},{1,5},{5,1},{2,6},{6,2},{3,7},{7,3},{8,12},{12,8},{9,1... | collective-permute-start | bytes 3145736 | tf_op jit(solution)/shard_map/ppermute | solution.py:381
  41.0 2.7 %collective-permute-start.3 = (bf16[4,4,32,1024]{3,2,1,0:T(8,128)(2,1)S(1)}, bf16[4,4,32,1024]{3,2,1,0:T(8,128)(2,1)S(1)}, u32[]{:S(2)}, u32[]{:S(2)}) collective-permute-start(bf16[4,4,32,1024]{3,2,1,0:T(8,128)(2,1)S(1)} %get-tuple-element.42), channel_id=1, source_target_pairs={{0,4},{4,0},{1,5},{5,1},{2,6},{6,2},{3,7},{7,3},{8,12},{12,8},{9,1... | collective-permute-start | bytes 3145736 | tf_op jit(solution)/shard_map/ppermute | solution.py:390

commit v10 on v9

--- a/solution.py
+++ b/solution.py
@@ -192,7 +192,7 @@
         for ref, half in places:
             for y in range(4):
                 top = half * 128 + y * 32
-                ref[x, y] = out_grad[top : top + 32].astype(BF16)
+                ref[y, x] = out_grad[top : top + 32].astype(BF16)
     head_grad = mm_nt(dpred[...], w_out[...])
     pieces = []
     for b in range(SEQ):
@@ -215,7 +215,7 @@
         for ref, half in places:
             for y in range(4):
                 top = half * 128 + y * 32
-                ref[x, y, :, :256] = value[top : top + 32].astype(BF16)
+                ref[y, x, :, :256] = value[top : top + 32].astype(BF16)
 
     for layer in reversed(range(LAYERS)):
         grad_wide = grad.astype(F32)
@@ -241,7 +241,7 @@
                         columns = slice(x * 128, (x + 1) * 128)
                         for low in range(2):
                             base = 256 + low * 384 + layer * 128
-                            ref[x, tap * 2 + y_low, :, base : base + 128] = tap_grad[
+                            ref[tap * 2 + y_low, x, :, base : base + 128] = tap_grad[
                                 top + low * 32 : top + low * 32 + 32, columns
                             ].astype(BF16)
         grad_joined = mm_nt(grad_preact, w_f[layer]).astype(BF16)
@@ -392,7 +392,7 @@
     chip = call(join_kernel, shape((4, 4, 32, 2048), BF16), [WHOLE] * 3, limit=4, name="join")(
         score, keep_rest, got_rest
     )
-    plane = lax.all_to_all(chip.reshape(16, 32, 2048), ("x", "y"), 0, 0, tiled=True)
+    plane = lax.all_to_all(chip.reshape(16, 32, 2048), ("y", "x"), 0, 0, tiled=True)
     by_z = call(plane_kernel, shape((8, 8, 1024), BF16), [WHOLE], limit=4, name="plane")(plane)
     line = lax.all_to_all(by_z, "z", 0, 0, tiled=True)
     mine = call(line_kernel, shape((4, 8, 1024), BF16), [WHOLE], limit=4, name="line")(line)

time: 101 us -> 101 us (level)
    all_to_all x1, blocking collectives: 33.8 us -> 32.8 us  [per_device(): lax.all_to_all(chip.reshape(16, 32, 2048), ('y', 'x'), 0, 0, tiled=True)]
where the time goes in v10:
time: 101 us; the launch traced here: 100 us
  blocking collectives  55.6 us (55%)
  Pallas kernels  20.4 us (20%)
  starting transfers between devices  17.5 us (17%)
  waiting for transfers between devices  6.21 us (6%)
    all_to_all x1, blocking collectives, per_device(): lax.all_to_all(chip.reshape(16, 32, 2048), ('y', 'x'), 0, 0, tiled=True)  32.8 us
    pallas_call x1, Pallas kernels, per_device(): call(score_kernel, (shape((ALL_ROWS, NODES), BF16), part, part, act, act,...  14.6 us
    all_to_all x1, blocking collectives, per_device(): line = lax.all_to_all(by_z, 'z', 0, 0, tiled=True)  14.3 us
    all_to_all x1, starting transfers between devices, per_device(): sums = lax.all_to_all(squares, TM, 0, 0, tiled=True)  12.1 us
    all_to_all x1, blocking collectives, per_device(): whole = lax.all_to_all(mine, 'x', 0, 0, tiled=True)  8.58 us
    ppermute x1, starting transfers between devices, per_device(): from_far = lax.ppermute(to_far, TM, seams + [(j, i) for i, j in seams])  4.53 us
    pallas_call x1, Pallas kernels, per_device(): call(layers_kernel, (shape((SEQ, ROWS, NODES), BF16), part, part), [WHOLE...  2.83 us
    ppermute x1, waiting for transfers between devices, per_device(): from_far = lax.ppermute(to_far, TM, seams + [(j, i) for i, j in seams])  2.81 us
  transfers between devices with their start and end apart: 5, of which 3 were waited for; matrix products, arithmetic and copies ran while one was open for 0% of the time, Pallas kernels for 3%

profile of v10, /device:TPU:8, one launch (start us, length us, event | category | flops | bytes accessed | tf_op | source)
XLA Modules:
  0.0 100.5 jit_solution(3928264353326099192)
XLA Ops:
  0.6 1.7 %start.1 = (f32[2,8,512]{2,1,0:T(8,128)S(1)}, f32[2,8,512]{2,1,0:T(8,128)S(1)}, f32[64,2,128]{2,1,0:T(2,128)}) custom-call(bf16[2,128,256]{2,1,0:T(8,128)(2,1)} %cov_hbm.3, f32[2,128,256]{2,1,0:T(8,128)} %obs_hbm.3), custom_call_target="tpu_custom_call" | custom-call | tf_op jit(solution)/shard_map/start/pallas_call | solution.py:330
  2.4 12.1 %all-to-all-start = ((f32[64,2,128]{2,1,0:T(2,128)}), f32[64,2,128]{2,1,0:T(2,128)S(1)}, u32[]{:S(2)}, u32[]{:S(2)}) async-start(f32[64,2,128]{2,1,0:T(2,128)} %get-tuple-element.28), calls=%async_computation | async-start | bytes 131072 | tf_op jit(solution)/shard_map/all_to_all | solution.py:343
  14.5 0.2 collective-permute-start
  14.7 4.5 %collective-permute-start.1 = (f32[2,8,512]{2,1,0:T(8,128)S(1)}, f32[2,8,512]{2,1,0:T(8,128)S(1)}, u32[]{:S(2)}, u32[]{:S(2)}) collective-permute-start(f32[2,8,512]{2,1,0:T(8,128)S(1)} %get-tuple-element.27), channel_id=1, source_target_pairs={{4,8},{12,16},{20,24},{28,32},{36,40},{44,48},{52,56},{60,64},{68,... | collective-permute-start | bytes 98312 | tf_op jit(solution)/shard_map/ppermute | solution.py:346
  19.3 0.0 collective-permute-done.from_pair
  19.3 2.8 %collective-permute-done.1.from_far = f32[2,8,512]{2,1,0:T(8,128)S(1)} collective-permute-done((f32[2,8,512]{2,1,0:T(8,128)S(1)}, f32[2,8,512]{2,1,0:T(8,128)S(1)}, u32[]{:S(2)}, u32[]{:S(2)}) %collective-permute-start.1) | collective-permute-done | bytes 32800 | tf_op jit(solution)/shard_map/ppermute | solution.py:346
  22.1 1.2 %all-to-all-done.sums = f32[64,2,128]{2,1,0:T(2,128)S(1)} async-done(((f32[64,2,128]{2,1,0:T(2,128)}), f32[64,2,128]{2,1,0:T(2,128)S(1)}, u32[]{:S(2)}, u32[]{:S(2)}) %all-to-all-start) | async-done | bytes 65568 | tf_op jit(solution)/shard_map/all_to_all | solution.py:343
  23.3 14.6 %score.1 = (bf16[288,256]{1,0:T(8,128)(2,1)S(1)}, bf16[4,4,32,1024]{3,2,1,0:T(8,128)(2,1)S(1)}, bf16[4,4,32,1024]{3,2,1,0:T(8,128)(2,1)S(1)}, f32[3,288,256]{2,1...) custom-call(f32[2,8,512]{2,1,0:T(8,128)S(1)} %collective-permute-don, ...), custom_call_target="tpu_custom_call" | custom-call | flops 10000000000 | bytes 10000000 | tf_op jit(solution)/shard_map/score/pallas_call | solution.py:350
  38.0 0.2 collective-permute-start.2
  38.2 2.8 %layers.1 = (bf16[2,128,256]{2,1,0:T(8,128)(2,1)}, bf16[4,4,32,1024]{3,2,1,0:T(8,128)(2,1)S(1)}, bf16[4,4,32,1024]{3,2,1,0:T(8,128)(2,1)S(1)}) custom-call(bf16[288,256]{1,0:T(8,128)(2,1)S(1)} %get-tuple-element.29.grad_in, f32[3,288,256]{2,1,0:T(8,128)S(1)} %get-tuple-element.30.tanh_act, f32[3,288,256]{2,1,0:T(8,128)S(1)} %get-tuple-element.31.gate_act, ...), custom_call_target="tpu_custom_call" | custom-call | flops 4000000000 | bytes 10000000 | tf_op jit(solution)/shard_map/layers/pallas_call | solution.py:382
  41.0 0.4 collective-permute-start.3
  41.4 0.0 collective-permute-done.2.got
  41.4 0.1 pair.1.score
  41.5 2.2 %collective-permute-done.3.got = bf16[4,4,32,1024]{3,2,1,0:T(8,128)(2,1)S(1)} collective-permute-done((bf16[4,4,32,1024]{3,2,1,0:T(8,128)(2,1)S(1)}, bf16[4,4,32,1024]{3,2,1,0:T(8,128)(2,1)S(1)}, u32[]{:S(2)}, u32[]{:S(2)}) %collective-permute-start.3) | collective-permute-done | bytes 1048608 | tf_op jit(solution)/shard_map/ppermute | solution.py:390
  43.7 0.2 join.1
  43.9 32.8 %all_to_all.20.pieces = bf16[16,32,2048]{2,1,0:T(8,128)(2,1)S(1)} all-to-all(bf16[16,32,2048]{2,1,0:T(8,128)(2,1)S(1)} %bitcast.1), channel_id=1, replica_groups=mesh['y'=4,'z'=8,'core'=2,'x'=4] {'y','x'}, dimensions={0} | all-to-all | bytes 4194304 | tf_op jit(solution)/shard_map/all_to_all | solution.py:395
  76.7 0.3 plane.1
  77.0 14.3 %all_to_all.21.pieces = bf16[8,8,1024]{2,1,0:T(8,128)(2,1)S(1)} all-to-all(bf16[8,8,1024]{2,1,0:T(8,128)(2,1)S(1)} %plane.1), channel_id=1, replica_groups=mesh['y'=4,'z'=8,'core'=2,'x'=4] {'z'}, dimensions={0} | all-to-all | bytes 262144 | tf_op jit(solution)/shard_map/all_to_all | solution.py:397
  91.3 8.6 %all_to_all.22.g = bf16[4,8,1024]{2,1,0:T(8,128)(2,1)S(1)} all-to-all(bf16[4,8,1024]{2,1,0:T(8,128)(2,1)S(1)} %line.1), channel_id=1, replica_groups=mesh['y'=4,'z'=8,'core'=2,'x'=4] {'x'}, dimensions={0} | all-to-all | bytes 131072 | tf_op jit(solution)/shard_map/all_to_all | solution.py:399
  99.8 0.6 finish.1
  (1 shorter events, 0.0 us)
Async XLA Ops:
  2.4 20.9 %all-to-all-start = ((f32[64,2,128]{2,1,0:T(2,128)}), f32[64,2,128]{2,1,0:T(2,128)S(1)}, u32[]{:S(2)}, u32[]{:S(2)}) async-start(f32[64,2,128]{2,1,0:T(2,128)} %get-tuple-element.28), calls=%async_computation | async-start | bytes 131072 | tf_op jit(solution)/shard_map/all_to_all | solution.py:343
  14.5 4.8 %collective-permute-start = (f32[2,8,512]{2,1,0:T(8,128)S(1)}, f32[2,8,512]{2,1,0:T(8,128)S(1)}, u32[]{:S(2)}, u32[]{:S(2)}) collective-permute-start(f32[2,8,512]{2,1,0:T(8,128)S(1)} %get-tuple-element.26), channel_id=1, source_target_pairs={{0,4},{4,0},{1,5},{5,1},{2,6},{6,2},{3,7},{7,3},{8,12},{12,8},{9,1... | collective-permute-start | bytes 98312 | tf_op jit(solution)/shard_map/ppermute | solution.py:344
  14.7 7.4 %collective-permute-start.1 = (f32[2,8,512]{2,1,0:T(8,128)S(1)}, f32[2,8,512]{2,1,0:T(8,128)S(1)}, u32[]{:S(2)}, u32[]{:S(2)}) collective-permute-start(f32[2,8,512]{2,1,0:T(8,128)S(1)} %get-tuple-element.27), channel_id=1, source_target_pairs={{4,8},{12,16},{20,24},{28,32},{36,40},{44,48},{52,56},{60,64},{68,... | collective-permute-start | bytes 98312 | tf_op jit(solution)/shard_map/ppermute | solution.py:346
  38.0 3.4 %collective-permute-start.2 = (bf16[4,4,32,1024]{3,2,1,0:T(8,128)(2,1)S(1)}, bf16[4,4,32,1024]{3,2,1,0:T(8,128)(2,1)S(1)}, u32[]{:S(2)}, u32[]{:S(2)}) collective-permute-start(bf16[4,4,32,1024]{3,2,1,0:T(8,128)(2,1)S(1)} %get-tuple-element.40), channel_id=1, source_target_pairs={{0,4},{4,0},{1,5},{5,1},{2,6},{6,2},{3,7},{7,3},{8,12},{12,8},{9,1... | collective-permute-start | bytes 3145736 | tf_op jit(solution)/shard_map/ppermute | solution.py:381
  41.0 2.7 %collective-permute-start.3 = (bf16[4,4,32,1024]{3,2,1,0:T(8,128)(2,1)S(1)}, bf16[4,4,32,1024]{3,2,1,0:T(8,128)(2,1)S(1)}, u32[]{:S(2)}, u32[]{:S(2)}) collective-permute-start(bf16[4,4,32,1024]{3,2,1,0:T(8,128)(2,1)S(1)} %get-tuple-element.42), channel_id=1, source_target_pairs={{0,4},{4,0},{1,5},{5,1},{2,6},{6,2},{3,7},{7,3},{8,12},{12,8},{9,1... | collective-permute-start | bytes 3145736 | tf_op jit(solution)/shard_map/ppermute | solution.py:390
